TPU v7x, 128 devices: a whole 4x4x4 slice. The times are simulated.
128 devices in a mesh: ctx: 16 (over x, z), batch: 8 (over y, core).
Axes of the slice: x: 4, y: 4, z: 4, core: 2. Of those that a mesh axis runs over, the one named last changes fastest.
Arguments:
- mixer_input: bfloat16 [8, 2048, 10240], P('batch', 'ctx'), may hold values from -6 to 6
- z_gate: bfloat16 [8, 2048, 8192], P('batch', 'ctx'), may hold values from -6 to 6
- time_step: bfloat16 [8, 2048, 128], P('batch', 'ctx'), may hold values from -4.5 to 0.5
- conv_weight: float32 [4, 10240], replicated, may hold values from -3 to 3
- conv_bias: float32 [10240], replicated, may hold values from -3 to 3
- decay_rate: float32 [128], replicated, may hold values from 0.000146484375 to 0.25
- skip_gain: float32 [128], replicated, may hold values from 0.3 to 1.5
- norm_gain: float32 [8192], replicated, may hold values from 0.5 to 1.5
- doc_lengths: int32 [8, 6], replicated, may hold values from 1 to 1536, 2048 in all within a row
- queries: bfloat16 [8, 2048, 4096], P('batch', 'ctx'), may hold values from -101.6466 to 101.6466
- attn_keys: bfloat16 [8, 2048, 1024], P('batch', 'ctx'), may hold values from -5 to 5
- attn_values: bfloat16 [8, 2048, 1024], P('batch', 'ctx'), may hold values from -6 to 6
Outputs:
- mixer_out: bfloat16 [8, 2048, 8192], P('batch', 'ctx')
- attn_out: bfloat16 [8, 2048, 4096], P('batch', 'ctx')
Inputs may be any that keep to these rules, and one draw needn't show every extreme that they name: `doc_lengths`: each sequence's 6 lengths sum to 2048, and the longest is exactly 1536.
All inputs are finite; a program needn't handle non-finite values.
Results may differ from a plain program's by a relative error of at most 0.011.
Values may be sent and summed in bfloat16 or wider, within the bound.
No kernel may reach another device: no remote copies, remote signals or barrier semaphores. Data moves between devices by JAX's collectives and lax.ppermute only.
A program may use at most 256 MiB of HBM per device.

v0:
```python
import jax
import jax.numpy as jnp
from jax import lax
from jax.sharding import PartitionSpec as P

HEADS = 128
HEAD_DIM = 64
STATE = 128
GROUPS = 8
QHEADS = 32
KVHEADS = 8
QDIM = 128
STRETCH = 128
WINDOW = 2048


EPSILON = 1e-05
NEGATIVE = -1e30


def segment_ids(doc_lengths, positions):
    endings = jnp.cumsum(doc_lengths, axis=-1, dtype=jnp.int32)
    starting = endings - doc_lengths
    return (
        jnp.sum(
            (starting[:, None, :] <= positions[None, :, None]).astype(jnp.int32),
            axis=-1,
            dtype=jnp.int32,
        )
        - 1
    )


def causal_conv(inputs, conv_weight, conv_bias, segments, rim_rows, rim_segments):
    padded = jnp.concatenate([rim_rows, inputs], axis=1).astype(jnp.float32)
    padded_seg = jnp.concatenate([rim_segments, segments], axis=1)
    length = inputs.shape[1]
    kernel_taps = conv_weight.shape[0]
    summed = jnp.zeros(inputs.shape, jnp.float32) + conv_bias
    for offset in range(kernel_taps):
        window_rows = padded[:, offset : offset + length]
        matches = (padded_seg[:, offset : offset + length] == segments)[..., None]
        summed = summed + jnp.where(matches, window_rows * conv_weight[offset], 0.0)
    return jax.nn.silu(summed).astype(jnp.bfloat16)


def ssd_block(carried_in, pieces, decay_rates, skip_gains):
    state_now, prev_seg = carried_in
    head_inputs, step_sizes, input_proj, output_proj, segments = pieces
    log_decay = jnp.cumsum(-step_sizes * decay_rates, axis=1)
    block_len = segments.shape[1]
    position = jnp.arange(block_len, dtype=jnp.int32)
    related = (segments[:, :, None] == segments[:, None, :]) & (
        position[:, None] >= position[None, :]
    )
    spread = log_decay[:, :, None] - log_decay[:, None, :]
    decays = jnp.where(related[..., None, None], jnp.exp(jnp.minimum(spread, 0.0)), 0.0)
    scores = jnp.einsum(
        "sqgn,skgn->sqkg", output_proj, input_proj, preferred_element_type=jnp.float32
    )
    weights = (scores[..., None] * decays * step_sizes[:, None]).astype(jnp.bfloat16)
    inner_part = jnp.einsum(
        "sqkgr,skgrp->sqgrp", weights, head_inputs, preferred_element_type=jnp.float32
    )
    carried = jnp.einsum(
        "sqgn,sgrnp->sqgrp",
        output_proj.astype(jnp.float32),
        state_now,
        precision=lax.Precision.HIGHEST,
    )
    keep_rows = (segments == prev_seg[:, None])[:, :, None, None]
    between = jnp.where(keep_rows, jnp.exp(log_decay), 0.0)[..., None] * carried
    outputs = inner_part + between + skip_gains[..., None] * head_inputs.astype(jnp.float32)
    last_seg = segments[:, -1]
    trailing = jnp.where(
        (segments == last_seg[:, None])[:, :, None, None],
        jnp.exp(log_decay[:, -1:] - log_decay) * step_sizes,
        0.0,
    )
    fresh_state = jnp.einsum(
        "sqgn,sqgrp->sgrnp",
        input_proj.astype(jnp.float32),
        trailing[..., None] * head_inputs.astype(jnp.float32),
        precision=lax.Precision.HIGHEST,
    )
    through = jnp.where((last_seg == prev_seg)[:, None, None], jnp.exp(log_decay[:, -1]), 0.0)
    return ((through[..., None, None] * state_now + fresh_state, last_seg), outputs)


def run_blocks(
    head_inputs, step_sizes, input_proj, output_proj, segments, decay_rates, skip_gains, block_len
):
    num_seqs, length = segments.shape
    state_zero = jnp.zeros(
        (num_seqs,) + head_inputs.shape[2:4] + (input_proj.shape[-1], head_inputs.shape[-1]),
        jnp.float32,
    )
    prev_zero = jnp.full((num_seqs,), -1, jnp.int32)

    def run_advance(carried_in, block_index):
        block_start = block_index * block_len
        pieces = tuple(
            (
                lax.dynamic_slice_in_dim(array_in, block_start, block_len, 1)
                for array_in in (head_inputs, step_sizes, input_proj, output_proj, segments)
            )
        )
        return ssd_block(carried_in, pieces, decay_rates, skip_gains)

    final_carry, outputs = lax.scan(
        run_advance, (state_zero, prev_zero), jnp.arange(length // block_len, dtype=jnp.int32)
    )
    return (final_carry[0], jnp.moveaxis(outputs, 0, 1).reshape(head_inputs.shape))


def gated_norm(mixed, z_gate, norm_gain):
    gated = mixed.astype(jnp.float32) * jax.nn.silu(z_gate.astype(jnp.float32))
    grouped = gated.reshape(gated.shape[:-1] + (GROUPS, gated.shape[-1] // GROUPS))
    scaling = lax.rsqrt(jnp.mean(grouped * grouped, axis=-1, keepdims=True) + EPSILON)
    return ((grouped * scaling).reshape(gated.shape) * norm_gain).astype(jnp.bfloat16)


def on_device(
    mixer_input,
    z_gate,
    time_step,
    conv_weight,
    conv_bias,
    decay_rate,
    skip_gain,
    norm_gain,
    doc_lengths,
    queries,
    attn_keys,
    attn_values,
):
    local_rows = mixer_input.shape[1]
    ctx_count = lax.axis_size("ctx")
    batch_count = lax.axis_size("batch")
    ctx_rank = lax.axis_index("ctx")
    batch_rank = lax.axis_index("batch")
    inner_width = HEADS * HEAD_DIM
    proj_width = GROUPS * STATE
    kernel_taps = conv_weight.shape[0]
    first_row = ctx_rank * local_rows
    local_pos = first_row + jnp.arange(local_rows, dtype=jnp.int32)
    own_lengths = lax.dynamic_slice_in_dim(doc_lengths, batch_rank, 1, 0)
    local_seg = segment_ids(own_lengths, local_pos)
    seq_len = local_rows * ctx_count
    per_device = HEADS // (ctx_count * batch_count)
    first_head = batch_rank * (HEADS // batch_count) + ctx_rank * per_device
    group_global = first_head // (HEADS // GROUPS)
    head_raw, step_raw = (
        lax.all_to_all(
            lax.all_to_all(
                mixer_input[:, :, :inner_width], "batch", split_axis=2, concat_axis=0, tiled=True
            ),
            "ctx",
            split_axis=2,
            concat_axis=1,
            tiled=True,
        ),
        lax.all_to_all(
            lax.all_to_all(time_step, "batch", split_axis=2, concat_axis=0, tiled=True),
            "ctx",
            split_axis=2,
            concat_axis=1,
            tiled=True,
        ),
    )
    proj_raw = mixer_input[:, :, inner_width:].reshape(1, local_rows, 2, GROUPS, STATE)
    group_rows = lax.all_to_all(proj_raw, "batch", split_axis=3, concat_axis=0, tiled=True)
    whole_proj = lax.all_gather(group_rows, "ctx", axis=1, tiled=True)
    own_proj = whole_proj.reshape(batch_count, seq_len, 2 * STATE)
    input_cols = inner_width + group_global * STATE
    output_cols = inner_width + proj_width + group_global * STATE
    proj_weight = jnp.concatenate(
        [
            lax.dynamic_slice_in_dim(conv_weight, input_cols, STATE, 1),
            lax.dynamic_slice_in_dim(conv_weight, output_cols, STATE, 1),
        ],
        axis=1,
    )
    proj_bias = jnp.concatenate(
        [
            lax.dynamic_slice_in_dim(conv_bias, input_cols, STATE, 0),
            lax.dynamic_slice_in_dim(conv_bias, output_cols, STATE, 0),
        ],
        axis=0,
    )
    all_seg = segment_ids(doc_lengths, jnp.arange(seq_len, dtype=jnp.int32))
    rim_segments = jnp.full((batch_count, kernel_taps - 1), -1, jnp.int32)
    proj_act = causal_conv(
        own_proj,
        proj_weight,
        proj_bias,
        all_seg,
        jnp.zeros((batch_count, kernel_taps - 1, 2 * STATE), jnp.bfloat16),
        rim_segments,
    )
    head_weight = lax.dynamic_slice_in_dim(
        conv_weight, first_head * HEAD_DIM, per_device * HEAD_DIM, 1
    )
    head_bias = lax.dynamic_slice_in_dim(conv_bias, first_head * HEAD_DIM, per_device * HEAD_DIM, 0)
    head_act = causal_conv(
        head_raw,
        head_weight,
        head_bias,
        all_seg,
        jnp.zeros((batch_count, kernel_taps - 1, per_device * HEAD_DIM), jnp.bfloat16),
        rim_segments,
    )
    step_sizes = jax.nn.softplus(step_raw.astype(jnp.float32)).reshape(
        batch_count, seq_len, 1, per_device
    )
    head_rates = lax.dynamic_slice_in_dim(decay_rate, first_head, per_device, 0).reshape(
        1, per_device
    )
    head_skips = lax.dynamic_slice_in_dim(skip_gain, first_head, per_device, 0).reshape(
        1, per_device
    )
    final_state, mixed_heads = run_blocks(
        head_act.reshape(batch_count, seq_len, 1, per_device, HEAD_DIM),
        step_sizes,
        proj_act[:, :, :STATE].reshape(batch_count, seq_len, 1, STATE),
        proj_act[:, :, STATE:].reshape(batch_count, seq_len, 1, STATE),
        all_seg,
        head_rates,
        head_skips,
        STRETCH,
    )
    mixed_send = mixed_heads.astype(jnp.bfloat16).reshape(
        batch_count, seq_len, per_device * HEAD_DIM
    )
    mixed = lax.all_to_all(
        lax.all_to_all(mixed_send, "ctx", split_axis=1, concat_axis=2, tiled=True),
        "batch",
        split_axis=0,
        concat_axis=2,
        tiled=True,
    )
    mixer_out = gated_norm(mixed, z_gate, norm_gain)
    group_size = QHEADS // KVHEADS
    scaling = QDIM ** (-0.5)
    query_rows = queries[0].reshape(local_rows, KVHEADS, group_size, QDIM)
    row_seg = local_seg[0]

    def attend_rows(carry_in, key_rows, value_rows, key_start):
        high_now, total_now, accum_now = carry_in
        key_count = key_rows.shape[0]
        key_pos = key_start + jnp.arange(key_count, dtype=jnp.int32)
        key_seg = segment_ids(own_lengths, key_pos)
        visible = (
            (key_seg == row_seg[:, None])
            & (key_pos[None, :] <= local_pos[:, None])
            & (local_pos[:, None] - key_pos[None, :] < WINDOW)
        )
        scores = (
            jnp.einsum(
                "qkgd,rkd->kgqr",
                query_rows,
                key_rows.reshape(key_count, KVHEADS, QDIM),
                preferred_element_type=jnp.float32,
            )
            * scaling
        )
        masked = jnp.where(visible, scores, NEGATIVE)
        high_next = jnp.maximum(high_now, jnp.max(masked, axis=-1))
        numerators = jnp.where(visible, jnp.exp(masked - high_next[..., None]), 0.0)
        fading = jnp.exp(high_now - high_next)
        total_next = total_now * fading + jnp.sum(numerators, axis=-1)
        accum_next = accum_now * jnp.moveaxis(fading, -1, 0)[..., None] + jnp.einsum(
            "kgqr,rkd->qkgd",
            numerators.astype(jnp.bfloat16),
            value_rows.reshape(key_count, KVHEADS, QDIM),
            preferred_element_type=jnp.float32,
        )
        return (high_next, total_next, accum_next)

    initial = (
        jnp.full((KVHEADS, group_size, local_rows), NEGATIVE, jnp.float32),
        jnp.zeros((KVHEADS, group_size, local_rows), jnp.float32),
        jnp.zeros((local_rows, KVHEADS, group_size, QDIM), jnp.float32),
    )
    key_piece = lax.all_gather(attn_keys[0], "ctx", axis=0, tiled=True)
    value_piece = lax.all_gather(attn_values[0], "ctx", axis=0, tiled=True)
    piece_rows = key_piece.shape[0]
    step_rows = 512

    def sweep_advance(carry_inner, block_index):
        offset = block_index * step_rows
        updated = attend_rows(
            carry_inner,
            lax.dynamic_slice_in_dim(key_piece, offset, step_rows, 0),
            lax.dynamic_slice_in_dim(value_piece, offset, step_rows, 0),
            offset,
        )
        return (updated, None)

    high_final, total_final, accum_final = lax.scan(
        sweep_advance, initial, jnp.arange(piece_rows // step_rows, dtype=jnp.int32)
    )[0]
    attn_out = (
        (accum_final / jnp.moveaxis(total_final, -1, 0)[..., None])
        .reshape(1, local_rows, QHEADS * QDIM)
        .astype(jnp.bfloat16)
    )
    return (mixer_out, attn_out)


def solution(mesh):
    placed = (
        P("batch", "ctx", None),
        P("batch", "ctx", None),
        P("batch", "ctx", None),
        P(),
        P(),
        P(),
        P(),
        P(),
        P(),
        P("batch", "ctx", None),
        P("batch", "ctx", None),
        P("batch", "ctx", None),
    )
    return jax.shard_map(
        on_device,
        mesh=mesh,
        in_specs=placed,
        out_specs=(P("batch", "ctx", None), P("batch", "ctx", None)),
        check_vma=False,
    )
```

profile of v0, /device:TPU:0, one launch (start us, length us, event | category | flops | bytes accessed | tf_op | source)
XLA Modules:
  0.0 583.9 jit_solution(4237152893659472588)
XLA Ops:
  9.1 15.0 %all_to_all.108 = bf16[1,128,2,8,128]{4,2,1,0,3:T(2,128)(2,1)} all-to-all(bf16[1,128,2,8,128]{4,2,1,0,3:T(2,128)(2,1)S(1)} %copy.237), channel_id=1, replica_groups=mesh['ctx'=16,'batch'=8] {'batch'}, dimensions={3} | all-to-all | bytes 1048576 | tf_op jit(solution)/shard_map/all_to_all | solution.py:172
  27.1 3.3 all-to-all-start
  30.5 6.9 %copy.266 = bf16[1,128,8192]{1,0,2:T(2,128)(2,1)} copy(bf16[1,128,8192]{2,1,0:T(8,128)(2,1)S(1)} %slice-done) | data formatting | bytes 4194304
  37.4 45.2 %reduce.12 = bf16[8192,128]{1,0:T(8,128)(2,1)S(1)} reduce(bf16[8192,1,128]{2,1,0:T(2,128)(2,1)} %bitcast.270, bf16[]{:T(256)} %broadcast.338), dimensions={1}, to_apply=%bitcast.192.reduce_sub_computation | reduce | bytes 4194306
  82.6 3.2 reshape.497
  85.8 4.7 all-to-all-start.2
  93.6 24.1 %all-to-all-done.2 = bf16[8,2,65536]{2,1,0:T(2,128)(2,1)S(1)} async-done(((bf16[8,2,65536]{2,1,0:T(2,128)(2,1)}), bf16[8,2,65536]{2,1,0:T(2,128)(2,1)S(1)}, u32[]{:S(2)}, u32[]{:S(2)}) %all-to-all-start.2) | async-done | bytes 2097184 | tf_op jit(solution)/shard_map/all_to_all | solution.py:155
  117.7 7.9 %all-to-all-start.1 = ((bf16[8,128,16]{1,0,2:T(8,128)(2,1)}), bf16[8,128,16]{1,0,2:T(8,128)(2,1)S(1)}, u32[]{:S(2)}, u32[]{:S(2)}) async-start(bf16[8,128,16]{1,0,2:T(8,128)(2,1)} %copy.230), calls=%async_computation.1 | async-start | bytes 65536 | tf_op jit(solution)/shard_map/all_to_all | solution.py:163
  126.3 4.4 reshape.498
  135.9 16.9 %all-to-all-start.3 = ((bf16[8,128,1024]{1,0,2:T(8,128)(2,1)}), bf16[8,128,1024]{1,0,2:T(8,128)(2,1)}, u32[]{:S(2)}, u32[]{:S(2)}) async-start(bf16[8,128,1024]{1,0,2:T(8,128)(2,1)} %copy.233), calls=%async_computation.3 | async-start | bytes 4194304 | tf_op jit(solution)/shard_map/all_to_all | solution.py:154
  155.6 26.4 %all-to-all-done.3 = bf16[8,128,1024]{1,0,2:T(8,128)(2,1)} async-done(((bf16[8,128,1024]{1,0,2:T(8,128)(2,1)}), bf16[8,128,1024]{1,0,2:T(8,128)(2,1)}, u32[]{:S(2)}, u32[]{:S(2)}) %all-to-all-start.3) | async-done | bytes 2097184 | tf_op jit(solution)/shard_map/all_to_all | solution.py:154
  182.0 4.3 copy.235
  186.2 4.2 all_to_all.91
  193.0 4.9 fusion.92
  197.9 14.1 %reshape.473 = bf16[8,2048,256]{2,1,0:T(8,128)(2,1)} reshape(bf16[8,1,2048,2,1,128]{5,3,2,0,4,1:T(2,128)(2,1)} %all-gather.7.cloned.1.call-done) | data formatting | bytes 16777216 | tf_op jit(solution)/shard_map/reshape | solution.py:174
  212.1 10.8 %pad_convert_fusion = f32[8,2051,256]{2,1,0:T(8,128)} fusion(bf16[8,2048,256]{2,1,0:T(8,128)(2,1)} %reshape.473), kind=kLoop, calls=%fused_computation.104 | loop fusion | flops 4200448 | bytes 25190400 | tf_op jit(solution)/shard_map/convert_element_type | solution.py:35
  222.8 26.2 %multiply_convert_fusion = bf16[8,2048,256]{2,1,0:T(8,128)(2,1)S(1)} fusion(f32[8,2051,256]{2,1,0:T(8,128)} %pad_convert_fusion, f32[256]{0:T(256)S(1)} %bitcast.297, f32[256]{0:T(256)S(1)} %bitcast.298, f32[256]{0:T(256)S(1)} %bitcast.296, f32[256]{0:T(256)S(1)} %bitcast.295, f32[256]{0:T(256)S(1)} %pad_maximum_fusion.1, ...), kind=kLoop, calls=%fused_computation.103 | loop fusion | flops 67108864 | bytes 75551744 | tf_op jit(solution)/shard_map/convert_element_type | solution.py:44
  249.1 4.0 slice_bitcast_fusion
  253.0 153.0 %while.32 = (s32[]{:T(128)}, f32[8,1,1,128,64]{3,4,0,2,1:T(8,128)S(1)}, s32[8]{0:T(128)S(1)}, bf16[16,8,128,1,1,64]{2,5,1,4,3,0:T(8,128)(2,1)}, s32[16]{0:T(128)...) while((s32[]{:T(128)}, ...), condition=%wide.region_4.5_spmd.clone, body=%wide.region_2.4_spmd.clone.sunk | while | flops 253582368 | bytes 3160228 | solution.py:110
  258.4 2.8 fusion.136
  267.9 2.8 fusion.136
  277.5 2.8 fusion.136
  287.1 2.8 fusion.136
  296.6 2.8 fusion.136
  315.8 2.8 fusion.136
  363.6 2.8 fusion.136
  406.1 5.0 copy.256
  411.1 7.6 %reshape.499 = bf16[16,2,32768]{2,1,0:T(2,128)(2,1)} reshape(bf16[2048,8,64]{2,1,0:T(8,128)(2,1)} %bitcast.272) | data formatting | bytes 4194304
  418.7 4.7 all-to-all-start.5
  426.9 25.4 %all-to-all-done.5 = bf16[16,2,32768]{2,1,0:T(2,128)(2,1)S(1)} async-done(((bf16[16,2,32768]{2,1,0:T(2,128)(2,1)}), bf16[16,2,32768]{2,1,0:T(2,128)(2,1)S(1)}, u32[]{:S(2)}, u32[]{:S(2)}) %all-to-all-start.5) | async-done | bytes 2097184 | tf_op jit(solution)/shard_map/all_to_all | solution.py:236
  452.3 5.0 reshape.500
  457.3 5.5 copy.242
  462.8 5.8 all-to-all-start.6
  468.6 70.9 %while.33 = (s32[]{:T(128)}, f32[8,4,128]{2,1,0:T(4,128)S(1)}, f32[8,4,128]{2,1,0:T(4,128)S(1)}, f32[128,8,4,128]{0,3,2,1:T(8,128)}, s32[1,1,6]{2,1,0:T(1,128)S(...) while((s32[]{:T(128)}, f32[8,4,128]{2,1,0:T(4,128)S(1)}, ...), condition=%wide.region_13.14_spmd.clone, body=%wide.region_9.13_spmd.clone.sunk | while | flops 1103005312 | bytes 70795024 | solution.py:300
  471.9 4.7 fusion.143
  476.6 7.1 %bitcast_add_fusion.2 = f32[128,8,4,128]{0,3,2,1:T(8,128)} fusion(f32[128,8,4,128]{0,3,2,1:T(8,128)} %get-tuple-element.715, bf16[512,8,128,1]{0,2,3,1:T(8,128)(2,1)S(1)} %bitcast.269, f32[8,512,128,4]{2,1,3,0:T(8,128)} %get-tuple-element.646, f32[8,4,128]{2,1,0:T(4,128)S(1)} %get-tuple-element.728, pred[128,512]{0,1:T(8,128)(4,1)S(1)} %fusion.142, ...), kind=kOutput, calls=%fused_computation.8.clone.1 | convolution fusion | flops 548929536 | bytes 13729793 | tf_op jit(solution)/shard_map/while/body/eval_jaxpr/kgqr,rkd->qkgd/dot_general | solution.py:272
  489.2 4.7 fusion.143
  493.9 7.7 %bitcast_add_fusion.2 = f32[128,8,4,128]{0,3,2,1:T(8,128)} fusion(f32[128,8,4,128]{0,3,2,1:T(8,128)} %get-tuple-element.715, bf16[512,8,128,1]{0,2,3,1:T(8,128)(2,1)S(1)} %bitcast.269, f32[8,512,128,4]{2,1,3,0:T(8,128)} %get-tuple-element.646, f32[8,4,128]{2,1,0:T(4,128)S(1)} %get-tuple-element.728, pred[128,512]{0,1:T(8,128)(4,1)S(1)} %fusion.142, ...), kind=kOutput, calls=%fused_computation.8.clone.1 | convolution fusion | flops 548929536 | bytes 13729793 | tf_op jit(solution)/shard_map/while/body/eval_jaxpr/kgqr,rkd->qkgd/dot_general | solution.py:272
  507.1 4.7 fusion.143
  511.8 7.7 %bitcast_add_fusion.2 = f32[128,8,4,128]{0,3,2,1:T(8,128)} fusion(f32[128,8,4,128]{0,3,2,1:T(8,128)} %get-tuple-element.715, bf16[512,8,128,1]{0,2,3,1:T(8,128)(2,1)S(1)} %bitcast.269, f32[8,512,128,4]{2,1,3,0:T(8,128)} %get-tuple-element.646, f32[8,4,128]{2,1,0:T(4,128)S(1)} %get-tuple-element.728, pred[128,512]{0,1:T(8,128)(4,1)S(1)} %fusion.142, ...), kind=kOutput, calls=%fused_computation.8.clone.1 | convolution fusion | flops 548929536 | bytes 13729793 | tf_op jit(solution)/shard_map/while/body/eval_jaxpr/kgqr,rkd->qkgd/dot_general | solution.py:272
  525.0 4.7 fusion.143
  529.7 7.7 %bitcast_add_fusion.2 = f32[128,8,4,128]{0,3,2,1:T(8,128)} fusion(f32[128,8,4,128]{0,3,2,1:T(8,128)} %get-tuple-element.715, bf16[512,8,128,1]{0,2,3,1:T(8,128)(2,1)S(1)} %bitcast.269, f32[8,512,128,4]{2,1,3,0:T(8,128)} %get-tuple-element.646, f32[8,4,128]{2,1,0:T(4,128)S(1)} %get-tuple-element.728, pred[128,512]{0,1:T(8,128)(4,1)S(1)} %fusion.142, ...), kind=kOutput, calls=%fused_computation.8.clone.1 | convolution fusion | flops 548929536 | bytes 13729793 | tf_op jit(solution)/shard_map/while/body/eval_jaxpr/kgqr,rkd->qkgd/dot_general | solution.py:272
  542.7 3.8 bitcast_convert_fusion
  546.6 5.8 copy.243
  552.4 3.3 fusion.97
  555.7 5.2 copy.269
  565.8 5.0 mul.297
  570.8 6.2 %multiply_convert_fusion.1 = bf16[1,128,8192]{2,1,0:T(8,128)(2,1)} fusion(f32[1,128,8192]{2,1,0:T(8,128)} %mul.297, f32[8192]{0:T(1024)S(1)} %copy-done.5, f32[1,128,8192]{2,1,0:T(8,128)} %copy.243, bf16[1,128,8192]{2,1,0:T(8,128)(2,1)S(1)} %copy-done.1), kind=kLoop, calls=%fused_computation.124 | loop fusion | flops 9437184 | bytes 12615680 | tf_op jit(solution)/shard_map/convert_element_type | solution.py:120
  (423 shorter events, 172.8 us)
Async XLA Ops:
  7.2 17.0 %copy-start.3 = (bf16[1,128,1024]{2,1,0:T(8,128)(2,1)S(1)}, bf16[1,128,1024]{2,1,0:T(8,128)(2,1)}, u32[]{:S(2)}) copy-start(bf16[1,128,1024]{2,1,0:T(8,128)(2,1)} %param.26) | copy-start | bytes 786436
  7.2 17.8 %copy-start.6 = (bf16[1,128,128]{2,1,0:T(8,128)(2,1)S(1)}, bf16[1,128,128]{2,1,0:T(8,128)(2,1)}, u32[]{:S(2)}) copy-start(bf16[1,128,128]{2,1,0:T(8,128)(2,1)} %param.18) | copy-start | bytes 98308
  7.2 190.7 %all-gather.7.cloned.1.call-start = ((), (), s32[]{:S(2)}) async-start(), calls=%async_computation.7 | async-start | bytes 8912896 | tf_op jit(solution)/shard_map/all_gather | solution.py:173
  8.6 21.8 %slice-start = ((bf16[1,128,10240]{2,1,0:T(8,128)(2,1)}), bf16[1,128,8192]{2,1,0:T(8,128)(2,1)S(1)}, s32[]{:S(2)}) async-start(bf16[1,128,10240]{2,1,0:T(8,128)(2,1)} %param.16), calls=%async_computation.10 | async-start | bytes 4194304 | tf_op jit(solution)/shard_map/slice | solution.py:156
  24.1 444.5 %all-gather.9.cloned.1.call-start = ((), (), s32[]{:S(2)}) async-start(), calls=%async_computation.8 | async-start | bytes 4456448 | tf_op jit(solution)/shard_map/all_gather | solution.py:285
  27.1 58.7 %all-to-all-start = ((bf16[8,2,1024]{2,1,0:T(2,128)(2,1)}), bf16[8,2,1024]{2,1,0:T(2,128)(2,1)S(1)}, u32[]{:S(2)}, u32[]{:S(2)}) async-start(bf16[8,2,1024]{2,1,0:T(2,128)(2,1)} %reshape.495), calls=%async_computation | async-start | bytes 65536 | tf_op jit(solution)/shard_map/all_to_all | solution.py:164
  82.6 7.9 %copy-start.4 = (bf16[1,128,1024]{2,1,0:T(8,128)(2,1)S(1)}, bf16[1,128,1024]{2,1,0:T(8,128)(2,1)}, u32[]{:S(2)}) copy-start(bf16[1,128,1024]{2,1,0:T(8,128)(2,1)} %param.27) | copy-start | bytes 786436
  85.8 31.9 %all-to-all-start.2 = ((bf16[8,2,65536]{2,1,0:T(2,128)(2,1)}), bf16[8,2,65536]{2,1,0:T(2,128)(2,1)S(1)}, u32[]{:S(2)}, u32[]{:S(2)}) async-start(bf16[8,2,65536]{2,1,0:T(2,128)(2,1)} %reshape.497), calls=%async_computation.2 | async-start | bytes 4194304 | tf_op jit(solution)/shard_map/all_to_all | solution.py:155
  90.4 378.2 %all-gather.11.cloned.1.call-start = ((), (), s32[]{:S(2)}) async-start(), calls=%async_computation.9 | async-start | bytes 4456448 | tf_op jit(solution)/shard_map/all_gather | solution.py:286
  117.7 18.3 %all-to-all-start.1 = ((bf16[8,128,16]{1,0,2:T(8,128)(2,1)}), bf16[8,128,16]{1,0,2:T(8,128)(2,1)S(1)}, u32[]{:S(2)}, u32[]{:S(2)}) async-start(bf16[8,128,16]{1,0,2:T(8,128)(2,1)} %copy.230), calls=%async_computation.1 | async-start | bytes 65536 | tf_op jit(solution)/shard_map/all_to_all | solution.py:163
  133.2 20.4 %copy-start.7 = (s32[8,6]{1,0:T(8,128)S(1)}, s32[8,6]{1,0:T(8,128)}, u32[]{:S(2)}) copy-start(s32[8,6]{1,0:T(8,128)} %param.24) | copy-start | bytes 580
  133.2 20.6 %copy-start.8 = (f32[128]{0:T(128)S(1)}, f32[128]{0:T(128)}, u32[]{:S(2)}) copy-start(f32[128]{0:T(128)} %param.21) | copy-start | bytes 1540
  133.2 21.2 %copy-start.9 = (f32[128]{0:T(128)S(1)}, f32[128]{0:T(128)}, u32[]{:S(2)}) copy-start(f32[128]{0:T(128)} %param.22) | copy-start | bytes 1540
  135.9 46.1 %all-to-all-start.3 = ((bf16[8,128,1024]{1,0,2:T(8,128)(2,1)}), bf16[8,128,1024]{1,0,2:T(8,128)(2,1)}, u32[]{:S(2)}, u32[]{:S(2)}) async-start(bf16[8,128,1024]{1,0,2:T(8,128)(2,1)} %copy.233), calls=%async_computation.3 | async-start | bytes 4194304 | tf_op jit(solution)/shard_map/all_to_all | solution.py:154
  411.1 12.8 %copy-start.2 = (bf16[1,128,4096]{2,1,0:T(8,128)(2,1)S(1)}, bf16[1,128,4096]{2,1,0:T(8,128)(2,1)}, u32[]{:S(2)}) copy-start(bf16[1,128,4096]{2,1,0:T(8,128)(2,1)} %param.25) | copy-start | bytes 3145732
  418.7 33.6 %all-to-all-start.5 = ((bf16[16,2,32768]{2,1,0:T(2,128)(2,1)}), bf16[16,2,32768]{2,1,0:T(2,128)(2,1)S(1)}, u32[]{:S(2)}, u32[]{:S(2)}) async-start(bf16[16,2,32768]{2,1,0:T(2,128)(2,1)} %reshape.499), calls=%async_computation.5 | async-start | bytes 4194304 | tf_op jit(solution)/shard_map/all_to_all | solution.py:236
  462.8 79.9 %all-to-all-start.6 = ((bf16[8,128,1024]{1,2,0:T(8,128)(2,1)}), bf16[8,128,1024]{1,2,0:T(8,128)(2,1)}, u32[]{:S(2)}, u32[]{:S(2)}) async-start(bf16[8,128,1024]{1,2,0:T(8,128)(2,1)} %bitcast.31), calls=%async_computation.6 | async-start | bytes 4194304 | tf_op jit(solution)/shard_map/all_to_all | solution.py:235
  476.6 7.1 %copy-start = (f32[8,512,128,4]{2,1,3,0:T(8,128)S(1)}, f32[8,512,128,4]{2,1,3,0:T(8,128)}, u32[]{:S(2)}) copy-start(f32[8,512,128,4]{2,1,3,0:T(8,128)} %get-tuple-element.646) | copy-start | bytes 25165828 | tf_op jit(solution)/shard_map/while
  493.9 7.7 %copy-start = (f32[8,512,128,4]{2,1,3,0:T(8,128)S(1)}, f32[8,512,128,4]{2,1,3,0:T(8,128)}, u32[]{:S(2)}) copy-start(f32[8,512,128,4]{2,1,3,0:T(8,128)} %get-tuple-element.646) | copy-start | bytes 25165828 | tf_op jit(solution)/shard_map/while
  511.8 7.7 %copy-start = (f32[8,512,128,4]{2,1,3,0:T(8,128)S(1)}, f32[8,512,128,4]{2,1,3,0:T(8,128)}, u32[]{:S(2)}) copy-start(f32[8,512,128,4]{2,1,3,0:T(8,128)} %get-tuple-element.646) | copy-start | bytes 25165828 | tf_op jit(solution)/shard_map/while
  529.7 7.7 %copy-start = (f32[8,512,128,4]{2,1,3,0:T(8,128)S(1)}, f32[8,512,128,4]{2,1,3,0:T(8,128)}, u32[]{:S(2)}) copy-start(f32[8,512,128,4]{2,1,3,0:T(8,128)} %get-tuple-element.646) | copy-start | bytes 25165828 | tf_op jit(solution)/shard_map/while
  546.6 5.8 copy-start.1
  565.8 5.0 copy-start.5
Sparse Core Ops, SparseCore 0:
  24.2 71.2 all-gather.6
  97.6 61.5 all-gather.8
  161.3 61.9 all-gather.10
where the time goes:
time: 596 us; the launch traced here: 584 us
  matrix products  144 us (24%)
  local copies, waits for them, and re-layouts  140 us (23%)
  other arithmetic  137 us (23%)
  waiting for transfers between devices  76 us (13%)
  starting transfers between devices  43.4 us (7%)
  blocking collectives  15 us (3%)
  between operations  14.5 us (2%)
  loops' own time  13.2 us (2%)
    unnamed x6, other arithmetic  46 us
    dot_general x16, matrix products, ssd_block(): jnp.einsum('sqgn,sgrnp->sqgrp', output_proj.astype(jnp.float32), state_no...  45.2 us
    unnamed x35, local copies, waits for them, and re-layouts  41 us
    dot_general x4, matrix products, attend_rows(): jnp.einsum('kgqr,rkd->qkgd', numerators.astype(jnp.bfloat16), value_rows....  30.2 us
    dot_general x16, matrix products, ssd_block(): jnp.einsum('sqkgr,skgrp->sqgrp', weights, head_inputs, preferred_element_...  28.1 us
    all_to_all x1, waiting for transfers between devices, on_device(): lax.all_to_all(lax.all_to_all(mixer_input[:, :, :inner_width], 'batch', s...  26.4 us
    convert_element_type x1, other arithmetic, causal_conv(): return jax.nn.silu(summed).astype(jnp.bfloat16)  26.2 us
    all_to_all x1, waiting for transfers between devices, on_device(): lax.all_to_all(mixed_send, 'ctx', split_axis=1, concat_axis=2, tiled=True)  25.4 us
  transfers between devices with their start and end apart: 9, of which 3 were waited for; matrix products, arithmetic and copies ran while one was open for 65% of the time, Pallas kernels for 0%

commit v1 on v0

v1 whole, which is shorter than its diff:
```python
import functools

import jax
import jax.numpy as jnp
from jax import lax
from jax.experimental import pallas as pl
from jax.experimental.pallas import tpu as pltpu
from jax.sharding import PartitionSpec as P

HEADS = 128
HEAD_DIM = 64
STATE = 128
GROUPS = 8
QHEADS = 32
KVHEADS = 8
QDIM = 128
CONV = 4
WINDOW = 2048

PER_GROUP = HEADS // GROUPS
WIDTH = PER_GROUP * HEAD_DIM
INNER = HEADS * HEAD_DIM
DOCS = 6
EPSILON = 1e-05
NEGATIVE = -1e30
LOG2E = 1.4426950408889634
EXTRA = 8
KEYS = 512

F32 = jnp.float32
BF16 = jnp.bfloat16
HIGH = lax.Precision.HIGHEST


def dot(a, b, dims=(((1,), (0,)), ((), ())), precision=None):
    return lax.dot_general(a, b, dims, precision=precision, preferred_element_type=F32)


def doc_starts(place_ref, lengths_ref):
    seq = place_ref[1]
    starts = [jnp.int32(0)]
    for d in range(DOCS - 1):
        starts.append(starts[-1] + lengths_ref[seq, d])
    return starts


def row_starts(starts, pos):
    first = jnp.zeros_like(pos)
    for s in starts[1:]:
        first = jnp.where(pos >= s, s, first)
    return first


def scalar_start(starts, pos):
    first = jnp.int32(0)
    for s in starts[1:]:
        first = jnp.where(pos >= s, s, first)
    return first


def expand_heads():
    row = lax.broadcasted_iota(jnp.int32, (PER_GROUP, WIDTH), 0)
    lane = lax.broadcasted_iota(jnp.int32, (PER_GROUP, WIDTH), 1)
    return (lane // HEAD_DIM == row).astype(F32)


def prep_kernel(place_ref, lengths_ref, step_ref, rate_ref, col_ref, row_ref, trail_ref, keep_ref, thr_ref):
    rows = step_ref.shape[0]
    base = place_ref[0] * rows
    starts = doc_starts(place_ref, lengths_ref)
    pos = base + lax.broadcasted_iota(jnp.int32, (rows, HEADS), 0)
    first = row_starts(starts, pos)
    last_first = scalar_start(starts, base + rows - 1)
    t = step_ref[...].astype(F32)
    dt = jnp.maximum(t, 0.0) + jnp.log1p(jnp.exp(-jnp.abs(t)))
    a = dt * rate_ref[...] * (-LOG2E)
    i = lax.broadcasted_iota(jnp.int32, (rows, rows), 0)
    j = lax.broadcasted_iota(jnp.int32, (rows, rows), 1)
    tri = (i >= j).astype(F32)
    cum = dot(tri, a, precision=HIGH)
    total = cum[rows - 1 : rows, :]
    trail = jnp.where(first == last_first, jnp.exp2(total - cum) * dt, 0.0)
    keep = jnp.where(first < base, jnp.exp2(cum), 0.0)
    thr = jnp.where(last_first < base, jnp.exp2(total), 0.0)
    row_ref[...] = jnp.transpose(cum - jnp.log2(dt))
    for g in range(GROUPS):
        part = slice(g * PER_GROUP, (g + 1) * PER_GROUP)
        col_ref[g] = cum[:, part]
        trail_ref[g] = trail[:, part]
        keep_ref[g] = keep[:, part]
        thr_ref[g] = jnp.broadcast_to(thr[:, part], (8, PER_GROUP))


def front_kernel(
    place_ref, lengths_ref, x_ref, b_ref, c_ref, hx_ref, hb_ref, hc_ref,
    wx_ref, wb_ref, wc_ref, ox_ref, ob_ref, oc_ref, trail_ref, thr_ref,
    xa_ref, ba_ref, ca_ref, f_ref, pad_ref,
):
    rows = x_ref.shape[0]
    base = place_ref[0] * rows
    starts = doc_starts(place_ref, lengths_ref)
    pos = base + lax.broadcasted_iota(jnp.int32, (rows, 128), 0)
    rel = pos - row_starts(starts, pos)
    masks = [None] + [rel >= d for d in range(1, CONV)]

    def conv(src, rim, weight, bias, dst, lo):
        at = slice(lo, lo + 128)
        pad_ref[0:8, :] = rim[:, at].astype(F32)
        pad_ref[8 : 8 + rows, :] = src[:, at].astype(F32)
        acc = pad_ref[8 : 8 + rows, :] * weight[3:4, at] + bias[:, at]
        for d in range(1, CONV):
            tap = pad_ref[8 - d : 8 - d + rows, :] * weight[3 - d : 4 - d, at]
            acc = acc + jnp.where(masks[d], tap, 0.0)
        dst[:, at] = (acc / (1.0 + jnp.exp(-acc))).astype(BF16)

    for lo in range(0, WIDTH, 128):
        conv(x_ref, hx_ref, wx_ref, ox_ref, xa_ref, lo)
    conv(b_ref, hb_ref, wb_ref, ob_ref, ba_ref, 0)
    conv(c_ref, hc_ref, wc_ref, oc_ref, ca_ref, 0)

    spread = expand_heads()
    scale = dot(trail_ref[0], spread, precision=HIGH)
    weighted = (xa_ref[...].astype(F32) * scale).astype(BF16)
    fresh = dot(ba_ref[...], weighted, (((0,), (0,)), ((), ()))).astype(BF16)
    thr = dot(thr_ref[0], spread, precision=HIGH)
    upper = thr.astype(BF16)
    lower = (thr - upper.astype(F32)).astype(BF16)
    rowid = lax.broadcasted_iota(jnp.int32, (8, WIDTH), 0)
    extra = jnp.where(rowid == 0, upper.astype(F32), jnp.where(rowid == 1, lower.astype(F32), 0.0)).astype(BF16)
    half = WIDTH // 2
    for k in range(2):
        f_ref[k, 0:STATE, :] = fresh[:, k * half : (k + 1) * half]
        f_ref[k, STATE : STATE + EXTRA, :] = extra[:, k * half : (k + 1) * half]


def inner_kernel(place_ref, lengths_ref, xa_ref, ba_ref, ca_ref, col_ref, row_ref, skip_ref, y_ref):
    rows = xa_ref.shape[0]
    base = place_ref[0] * rows
    starts = doc_starts(place_ref, lengths_ref)
    i = base + lax.broadcasted_iota(jnp.int32, (rows, rows), 0)
    j = base + lax.broadcasted_iota(jnp.int32, (rows, rows), 1)
    first = row_starts(starts, i)
    blocked = jnp.where((j <= i) & (j >= first), 0.0, NEGATIVE)
    scores = dot(ca_ref[...], ba_ref[...], (((1,), (1,)), ((), ())))
    lane = lax.broadcasted_iota(jnp.int32, (rows, 128), 1)
    col = col_ref[0]
    for p in range(PER_GROUP // 2):
        weights = []
        for h in (2 * p, 2 * p + 1):
            spread = (col[:, h : h + 1] + blocked) - row_ref[h : h + 1, :]
            weights.append((scores * jnp.exp2(spread)).astype(BF16))
        at = slice(p * 128, (p + 1) * 128)
        x = xa_ref[:, at]
        zero = jnp.zeros_like(x)
        both = jnp.concatenate(
            [jnp.where(lane < HEAD_DIM, x, zero), jnp.where(lane < HEAD_DIM, zero, x)], axis=0
        )
        y = dot(jnp.concatenate(weights, axis=1), both)
        y_ref[:, at] = y + x.astype(F32) * skip_ref[:, at]


def scan_kernel(f_ref, s_ref):
    blocks = f_ref.shape[0]
    piece = 32

    def body(q, carry):
        at = pl.ds(pl.multiple_of(q * piece, piece), piece)
        state = jnp.zeros((piece, f_ref.shape[2]), F32)
        for r in range(blocks):
            s_ref[r, at, :] = state.astype(BF16)
            if r + 1 < blocks:
                tail = f_ref[r, STATE : STATE + EXTRA, :].astype(F32)
                thr = tail[0:1, :] + tail[1:2, :]
                state = state * thr + f_ref[r, at, :].astype(F32)
        return carry

    lax.fori_loop(0, STATE // piece, body, 0)


def final_kernel(y_ref, s_ref, ca_ref, keep_ref, z_ref, gain_ref, o_ref):
    spread = expand_heads()
    scale = dot(keep_ref[0], spread, precision=HIGH)
    states = jnp.concatenate([s_ref[0], s_ref[1]], axis=1)
    carried = dot(ca_ref[...], states)
    mixed = (y_ref[...] + scale * carried).astype(BF16).astype(F32)
    z = z_ref[...].astype(F32)
    gated = mixed * (z / (1.0 + jnp.exp(-z)))
    mean = jnp.mean(gated * gated, axis=1, keepdims=True)
    o_ref[...] = (gated * lax.rsqrt(mean + EPSILON) * gain_ref[...]).astype(BF16)


def attend_kernel(place_ref, lengths_ref, q_ref, k_ref, v_ref, o_ref, m_ref, l_ref, acc_ref):
    rows = q_ref.shape[0]
    share = q_ref.shape[1] // QDIM
    base = place_ref[0] * rows
    starts = doc_starts(place_ref, lengths_ref)
    pos = base + lax.broadcasted_iota(jnp.int32, (rows, KEYS), 0)
    first = jnp.maximum(row_starts(starts, pos), pos - (WINDOW - 1))
    lane = lax.broadcasted_iota(jnp.int32, (rows, KEYS), 1)
    scaling = QDIM ** (-0.5) * LOG2E
    m_ref[...] = jnp.full_like(m_ref, NEGATIVE)
    l_ref[...] = jnp.zeros_like(l_ref)
    acc_ref[...] = jnp.zeros_like(acc_ref)
    lowest = jnp.maximum(scalar_start(starts, base), base - (WINDOW - 1))

    def step(j, carry):
        at = pl.ds(pl.multiple_of(j * KEYS, KEYS), KEYS)
        k = k_ref[at, :]
        v = v_ref[at, :]
        key = j * KEYS + lane
        visible = (key <= pos) & (key >= first)
        for h in range(share):
            s = dot(q_ref[:, h * QDIM : (h + 1) * QDIM], k, (((1,), (1,)), ((), ()))) * scaling
            s = jnp.where(visible, s, NEGATIVE)
            m_old = m_ref[h]
            m_new = jnp.maximum(m_old, jnp.max(s, axis=1, keepdims=True))
            fade = jnp.exp2(m_old - m_new)
            p = jnp.exp2(s - m_new)
            l_ref[h] = l_ref[h] * fade + jnp.sum(p, axis=1, keepdims=True)
            acc_ref[h] = acc_ref[h] * fade + dot(p.astype(BF16), v)
            m_ref[h] = m_new
        return carry

    lax.fori_loop(lowest // KEYS, (base + rows - 1) // KEYS + 1, step, 0)
    for h in range(share):
        o_ref[:, h * QDIM : (h + 1) * QDIM] = (acc_ref[h] / l_ref[h]).astype(BF16)


def smem():
    return pl.BlockSpec(memory_space=pltpu.SMEM)


def on_device(
    mixer_input, z_gate, time_step, conv_weight, conv_bias, decay_rate, skip_gain,
    norm_gain, doc_lengths, queries, attn_keys, attn_values,
):
    rows = mixer_input.shape[1]
    blocks = lax.axis_size("ctx")
    place = jnp.stack([lax.axis_index("ctx"), lax.axis_index("batch")]).astype(jnp.int32)
    raw = mixer_input[0]
    call = functools.partial(
        pl.pallas_call, compiler_params=pltpu.CompilerParams(vmem_limit_bytes=56 << 20)
    )

    keys_values = jnp.concatenate([attn_keys[0], attn_values[0]], axis=1)
    rim = lax.ppermute(raw[rows - 8 :], "ctx", [(r, r + 1) for r in range(blocks - 1)])
    whole_kv = lax.all_gather(keys_values, "ctx", axis=0, tiled=True)

    col, row, trail, keep, thr = call(
        prep_kernel,
        in_specs=[smem(), smem(), pl.BlockSpec(), pl.BlockSpec()],
        out_shape=[
            jax.ShapeDtypeStruct((GROUPS, rows, PER_GROUP), F32),
            jax.ShapeDtypeStruct((HEADS, rows), F32),
            jax.ShapeDtypeStruct((GROUPS, rows, PER_GROUP), F32),
            jax.ShapeDtypeStruct((GROUPS, rows, PER_GROUP), F32),
            jax.ShapeDtypeStruct((GROUPS, 8, PER_GROUP), F32),
        ],
        name="prep",
    )(place, doc_lengths, time_step[0], decay_rate[None])

    wide = lambda n: pl.BlockSpec((n, WIDTH), lambda g: (0, g))
    b_cols = lambda n: pl.BlockSpec((n, STATE), lambda g: (0, INNER // STATE + g))
    c_cols = lambda n: pl.BlockSpec((n, STATE), lambda g: (0, INNER // STATE + GROUPS + g))
    group_cols = lambda n: pl.BlockSpec((n, STATE), lambda g: (0, g))
    per_group = pl.BlockSpec((1, rows, PER_GROUP), lambda g: (g, 0, 0))
    bias = conv_bias[None]
    half = WIDTH // 2
    x_act, b_act, c_act, fresh = call(
        front_kernel,
        grid=(GROUPS,),
        in_specs=[
            smem(), smem(),
            wide(rows), b_cols(rows), c_cols(rows),
            wide(8), b_cols(8), c_cols(8),
            wide(CONV), b_cols(CONV), c_cols(CONV),
            wide(1), b_cols(1), c_cols(1),
            per_group, pl.BlockSpec((1, 8, PER_GROUP), lambda g: (g, 0, 0)),
        ],
        out_specs=[
            wide(rows), group_cols(rows), group_cols(rows),
            pl.BlockSpec((2, STATE + EXTRA, half), lambda g: (g, 0, 0)),
        ],
        out_shape=[
            jax.ShapeDtypeStruct((rows, INNER), BF16),
            jax.ShapeDtypeStruct((rows, GROUPS * STATE), BF16),
            jax.ShapeDtypeStruct((rows, GROUPS * STATE), BF16),
            jax.ShapeDtypeStruct((2 * GROUPS, STATE + EXTRA, half), BF16),
        ],
        scratch_shapes=[pltpu.VMEM((8 + rows, 128), F32)],
        name="front",
    )(
        place, doc_lengths, raw, raw, raw, rim, rim, rim,
        conv_weight, conv_weight, conv_weight, bias, bias, bias, trail, thr,
    )

    own_fresh = lax.all_to_all(fresh, "ctx", split_axis=0, concat_axis=0, tiled=True)

    local = call(
        inner_kernel,
        grid=(GROUPS,),
        in_specs=[
            smem(), smem(), wide(rows), group_cols(rows), group_cols(rows), per_group,
            pl.BlockSpec((PER_GROUP, rows), lambda g: (g, 0)), wide(1),
        ],
        out_specs=wide(rows),
        out_shape=jax.ShapeDtypeStruct((rows, INNER), F32),
        name="inner",
    )(place, doc_lengths, x_act, b_act, c_act, col, row, jnp.repeat(skip_gain, HEAD_DIM)[None])

    own_states = call(
        scan_kernel,
        out_shape=jax.ShapeDtypeStruct((blocks, STATE, half), BF16),
        name="scan",
    )(own_fresh)
    states = lax.all_to_all(own_states, "ctx", split_axis=0, concat_axis=0, tiled=True)

    share = QHEADS // KVHEADS
    keys = whole_kv.shape[0]
    attn_out = call(
        attend_kernel,
        grid=(KVHEADS,),
        in_specs=[
            smem(), smem(),
            pl.BlockSpec((rows, share * QDIM), lambda h: (0, h)),
            pl.BlockSpec((keys, QDIM), lambda h: (0, h)),
            pl.BlockSpec((keys, QDIM), lambda h: (0, KVHEADS + h)),
        ],
        out_specs=pl.BlockSpec((rows, share * QDIM), lambda h: (0, h)),
        out_shape=jax.ShapeDtypeStruct((rows, QHEADS * QDIM), BF16),
        scratch_shapes=[
            pltpu.VMEM((share, rows, 1), F32),
            pltpu.VMEM((share, rows, 1), F32),
            pltpu.VMEM((share, rows, QDIM), F32),
        ],
        name="attend",
    )(place, doc_lengths, queries[0], whole_kv, whole_kv)

    mixer_out = call(
        final_kernel,
        grid=(GROUPS,),
        in_specs=[
            wide(rows), pl.BlockSpec((2, STATE, half), lambda g: (g, 0, 0)), group_cols(rows),
            per_group, wide(rows), wide(1),
        ],
        out_specs=wide(rows),
        out_shape=jax.ShapeDtypeStruct((rows, INNER), BF16),
        name="final",
    )(local, states, c_act, keep, z_gate[0], norm_gain[None])
    return (mixer_out[None], attn_out[None])


def solution(mesh):
    placed = P("batch", "ctx", None)
    whole = P()
    return jax.shard_map(
        on_device,
        mesh=mesh,
        in_specs=(placed, placed, placed) + (whole,) * 6 + (placed,) * 3,
        out_specs=(placed, placed),
        check_vma=False,
    )
```

time: 596 us -> 195 us (0.33)
  the two profiles are of different devices: /device:TPU:0 before, /device:TPU:22 now
where the time goes in v1:
time: 195 us
  Pallas kernels  90.3 us (46%)
  blocking collectives  50.5 us (26%)
  waiting for transfers between devices  23.9 us (12%)
  between operations  14.1 us (7%)
  starting transfers between devices  9.59 us (5%)
  local copies, waits for them, and re-layouts  3.71 us (2%)
  other arithmetic  2.45 us (1%)
    pallas_call x1, Pallas kernels, on_device(): call(attend_kernel, grid=(KVHEADS,), in_specs=[smem(), smem(), pl.BlockSp...  53.4 us
    all_to_all x1, blocking collectives, on_device(): lax.all_to_all(fresh, 'ctx', split_axis=0, concat_axis=0, tiled=True)  50.5 us
    all_to_all x1, waiting for transfers between devices, on_device(): lax.all_to_all(own_states, 'ctx', split_axis=0, concat_axis=0, tiled=True)  20.5 us
    pallas_call x1, Pallas kernels, on_device(): call(front_kernel, grid=(GROUPS,), in_specs=[smem(), smem(), wide(rows),...  11.9 us
    pallas_call x1, Pallas kernels, on_device(): call(final_kernel, grid=(GROUPS,), in_specs=[wide(rows), pl.BlockSpec((2,...  10.4 us
    pallas_call x1, Pallas kernels, on_device(): call(inner_kernel, grid=(GROUPS,), in_specs=[smem(), smem(), wide(rows),...  8.5 us
    all_to_all x1, starting transfers between devices, on_device(): lax.all_to_all(own_states, 'ctx', split_axis=0, concat_axis=0, tiled=True)  5.72 us
  transfers between devices with their start and end apart: 3, of which 2 were waited for; matrix products, arithmetic and copies ran while one was open for 1% of the time, Pallas kernels for 19%

profile of v1, /device:TPU:22, one launch (start us, length us, event | category | flops | bytes accessed | tf_op | source)
XLA Modules:
  0.0 194.6 jit_solution(314196266198468818)
XLA Ops:
  7.2 0.0 all-gather.2.cloned.1.call-start
  7.2 1.9 pad_maximum_fusion
  9.1 0.0 all-gather.2.cloned.1.call-update
  9.1 0.9 slice_bitcast_fusion
  10.0 3.8 %collective-permute-start = (bf16[8,10240]{1,0:T(8,128)(2,1)S(1)}, bf16[8,10240]{1,0:T(8,128)(2,1)S(1)}, u32[]{:S(2)}, u32[]{:S(2)}) collective-permute-start(bf16[8,10240]{1,0:T(8,128)(2,1)S(1)} %slice_bitcast_fusion), channel_id=1, source_target_pairs={{0,8},{8,16},{16,24},{24,32},{32,40},{40,48},{48,56},{56,64},{64,7... | collective-permute-start | bytes 491528 | tf_op jit(solution)/shard_map/ppermute | solution.py:246
  13.9 0.6 pad_add_fusion.place_ref
  14.5 2.6 %prep.1 = (f32[8,128,16]{2,1,0:T(8,128)}, f32[128,128]{1,0:T(8,128)}, f32[8,128,16]{2,1,0:T(8,128)}, f32[8,128,16]{2,1,0:T(8,128)}, f32[8,8,16]{2,1,0:T(8,128)}) custom-call(s32[2]{0:T(128)} %pad_add_fusion.place_ref, s32[8,6]{1,0:T(8,128)} %lengths_ref.7, bf16[128,128]{1,0:T(8,128)(2,1)} %bitcast.28, f32[1,128]{1,0:T(1,128)} %bitcast.29), custom_call_target="tpu_custom_call" | custom-call | tf_op jit(solution)/shard_map/prep/pallas_call | solution.py:249
  17.0 3.4 %collective-permute-done.hx_ref.hb_ref.hc_ref = bf16[8,10240]{1,0:T(8,128)(2,1)S(1)} collective-permute-done((bf16[8,10240]{1,0:T(8,128)(2,1)S(1)}, bf16[8,10240]{1,0:T(8,128)(2,1)S(1)}, u32[]{:S(2)}, u32[]{:S(2)}) %collective-permute-start) | collective-permute-done | bytes 163872 | tf_op jit(solution)/shard_map/ppermute | solution.py:246
  20.4 0.0 copy-start.1
  20.4 0.7 copy-done.1
  21.1 11.9 %front.1 = (bf16[128,8192]{1,0:T(8,128)(2,1)}, bf16[128,1024]{1,0:T(8,128)(2,1)}, bf16[128,1024]{1,0:T(8,128)(2,1)}, bf16[16,136,512]{2,1,0:T(8,128)(2,1)}) custom-call(s32[2]{0:T(128)} %pad_add_fusion.place_ref, s32[8,6]{1,0:T(8,128)} %lengths_ref.7, bf16[128,10240]{1,0:T(8,128)(2,1)} %bitcast.15, bf16[128,10240]{1,0:T(8,128)(2,1)} %bitcast.16, ...), custom_call_target="tpu_custom_call" | custom-call | tf_op jit(solution)/shard_map/front/pallas_call | solution.py:269
  33.1 50.5 %all_to_all.10.f_ref = bf16[16,136,512]{2,1,0:T(8,128)(2,1)} all-to-all(bf16[16,136,512]{2,1,0:T(8,128)(2,1)} %get-tuple-element.18), channel_id=1, replica_groups=mesh['ctx'=16,'batch'=8] {'ctx'}, dimensions={0} | all-to-all | bytes 4456448 | tf_op jit(solution)/shard_map/all_to_all | solution.py:297
  83.6 3.5 %scan.1 = bf16[16,128,512]{2,1,0:T(8,128)(2,1)} custom-call(bf16[16,136,512]{2,1,0:T(8,128)(2,1)} %all_to_all.10.f_ref), custom_call_target="tpu_custom_call" | custom-call | tf_op jit(solution)/shard_map/scan/pallas_call | solution.py:311
  87.1 0.0 copy-start.2
  87.1 5.7 %all-to-all-start.1 = ((bf16[16,128,512]{2,1,0:T(8,128)(2,1)}), bf16[16,128,512]{2,1,0:T(8,128)(2,1)S(1)}, u32[]{:S(2)}, u32[]{:S(2)}) async-start(bf16[16,128,512]{2,1,0:T(8,128)(2,1)} %scan.1), calls=%async_computation.1 | async-start | bytes 4194304 | tf_op jit(solution)/shard_map/all_to_all | solution.py:316
  92.8 0.0 copy-done.2
  92.8 0.1 broadcast_in_dim.20
  92.9 0.7 broadcast_in_dim_reshape.3.skip_ref
  93.6 8.5 %inner.1.y_ref = f32[128,8192]{1,0:T(8,128)} custom-call(s32[2]{0:T(128)} %pad_add_fusion.place_ref, s32[8,6]{1,0:T(8,128)} %lengths_ref.7, bf16[128,8192]{1,0:T(8,128)(2,1)} %get-tuple-element.13.xa_ref, bf16[128,1024]{1,0:T(8,128)(2,1)} %get-tuple-element.14.ba_ref, bf16[128,1024]{1,0:T(8,128)(2,1)} %get-tuple-element.15.ca_ref, ...), custom_call_target="tpu_custom_call" | custom-call | tf_op jit(solution)/shard_map/inner/pallas_call | solution.py:299
  102.1 20.5 %all-to-all-done.1.s_ref = bf16[16,128,512]{2,1,0:T(8,128)(2,1)S(1)} async-done(((bf16[16,128,512]{2,1,0:T(8,128)(2,1)}), bf16[16,128,512]{2,1,0:T(8,128)(2,1)S(1)}, u32[]{:S(2)}, u32[]{:S(2)}) %all-to-all-start.1) | async-done | bytes 2097184 | tf_op jit(solution)/shard_map/all_to_all | solution.py:316
  122.6 0.0 copy-start
  122.6 1.3 copy-done
  123.9 10.4 %final.1 = bf16[128,8192]{1,0:T(8,128)(2,1)} custom-call(f32[128,8192]{1,0:T(8,128)} %inner.1.y_ref, bf16[16,128,512]{2,1,0:T(8,128)(2,1)} %copy-done, bf16[128,1024]{1,0:T(8,128)(2,1)} %get-tuple-element.15.ca_ref, f32[8,128,16]{2,1,0:T(8,128)} %get-tuple-element.19.keep_ref, bf16[128,8192]{1,0:T(8,128)(2,1)} %bitcast.18, f32[1,8192]{1,0:T(1,128)} %bitcast.27), custom_call_target="tpu_custom_call" | custom-call | tf_op jit(solution)/shard_map/final/pallas_call | solution.py:339
  134.3 0.0 all-gather.2.cloned.1.call-done.k_ref.v_ref
  134.3 53.4 %attend.1 = bf16[128,4096]{1,0:T(8,128)(2,1)} custom-call(s32[2]{0:T(128)} %pad_add_fusion.place_ref, s32[8,6]{1,0:T(8,128)} %lengths_ref.7, bf16[128,4096]{1,0:T(8,128)(2,1)} %bitcast.20, bf16[2048,2048]{1,0:T(8,128)(2,1)} %all-gather.2.cloned.1.call-done.k_ref.v_ref, bf16[2048,2048]{1,0:T(8,128)(2,1)} %all-gather.2.cloned.1.call-done.k_ref.v_ref), custom_call_target="tpu_custom_call" | custom-call | tf_op jit(solution)/shard_map/attend/pallas_call | solution.py:320
Async XLA Ops:
  7.2 127.1 %all-gather.2.cloned.1.call-start = ((), (), s32[]{:S(2)}) async-start(), calls=%async_computation.2 | async-start | bytes 8912896 | tf_op jit(solution)/shard_map/all_gather | solution.py:247
  10.0 10.4 %collective-permute-start = (bf16[8,10240]{1,0:T(8,128)(2,1)S(1)}, bf16[8,10240]{1,0:T(8,128)(2,1)S(1)}, u32[]{:S(2)}, u32[]{:S(2)}) collective-permute-start(bf16[8,10240]{1,0:T(8,128)(2,1)S(1)} %slice_bitcast_fusion), channel_id=1, source_target_pairs={{0,8},{8,16},{16,24},{24,32},{32,40},{40,48},{48,56},{56,64},{64,7... | collective-permute-start | bytes 491528 | tf_op jit(solution)/shard_map/ppermute | solution.py:246
  20.4 0.7 copy-start.1
  87.1 5.7 %copy-start.2 = (f32[128]{0:T(128)S(1)}, f32[128]{0:T(128)}, u32[]{:S(2)}) copy-start(f32[128]{0:T(128)} %param.18) | copy-start | bytes 1540
  87.1 35.5 %all-to-all-start.1 = ((bf16[16,128,512]{2,1,0:T(8,128)(2,1)}), bf16[16,128,512]{2,1,0:T(8,128)(2,1)S(1)}, u32[]{:S(2)}, u32[]{:S(2)}) async-start(bf16[16,128,512]{2,1,0:T(8,128)(2,1)} %scan.1), calls=%async_computation.1 | async-start | bytes 4194304 | tf_op jit(solution)/shard_map/all_to_all | solution.py:316
  122.6 1.3 copy-start
Sparse Core Ops, SparseCore 0:
  10.1 110.0 all-gather.1

commit v2 on v1

v2 whole, which is shorter than its diff:
```python
import functools

import jax
import jax.numpy as jnp
from jax import lax
from jax.experimental import pallas as pl
from jax.experimental.pallas import tpu as pltpu
from jax.sharding import PartitionSpec as P

HEADS = 128
HEAD_DIM = 64
STATE = 128
GROUPS = 8
QHEADS = 32
KVHEADS = 8
QDIM = 128
CONV = 4
WINDOW = 2048

PER_GROUP = HEADS // GROUPS
WIDTH = PER_GROUP * HEAD_DIM
INNER = HEADS * HEAD_DIM
DOCS = 6
EPSILON = 1e-05
NEGATIVE = -1e30
LOG2E = 1.4426950408889634
EXTRA = 8
KEYS = 256

F32 = jnp.float32
BF16 = jnp.bfloat16
HIGH = lax.Precision.HIGHEST


def dot(a, b, dims=(((1,), (0,)), ((), ())), precision=None):
    return lax.dot_general(a, b, dims, precision=precision, preferred_element_type=F32)


def doc_starts(place_ref, lengths_ref):
    seq = place_ref[1]
    starts = [jnp.int32(0)]
    for d in range(DOCS - 1):
        starts.append(starts[-1] + lengths_ref[seq, d])
    return starts


def row_starts(starts, pos):
    first = jnp.zeros_like(pos)
    for s in starts[1:]:
        first = jnp.where(pos >= s, s, first)
    return first


def scalar_start(starts, pos):
    first = jnp.int32(0)
    for s in starts[1:]:
        first = jnp.where(pos >= s, s, first)
    return first


def expand_heads(copies):
    shape = (copies * PER_GROUP, WIDTH)
    row = lax.broadcasted_iota(jnp.int32, shape, 0) % PER_GROUP
    lane = lax.broadcasted_iota(jnp.int32, shape, 1)
    return jnp.where(lane // HEAD_DIM == row, 1.0, 0.0).astype(BF16)


def halves(x):
    upper = x.astype(BF16)
    return upper, (x - upper.astype(F32)).astype(BF16)


def silu(x):
    return (0.5 * x) * (1.0 + jnp.tanh(0.5 * x))


def prep_kernel(place_ref, lengths_ref, step_ref, rate_ref, col_ref, row_ref, trail_ref, keep_ref, thr_ref):
    rows = step_ref.shape[0]
    base = place_ref[0] * rows
    starts = doc_starts(place_ref, lengths_ref)
    pos = base + lax.broadcasted_iota(jnp.int32, (rows, HEADS), 0)
    first = row_starts(starts, pos)
    last_first = scalar_start(starts, base + rows - 1)
    t = step_ref[...].astype(F32)
    dt = jnp.maximum(t, 0.0) + jnp.log1p(jnp.exp(-jnp.abs(t)))
    a = dt * rate_ref[...] * (-LOG2E)
    i = lax.broadcasted_iota(jnp.int32, (rows, rows), 0)
    j = lax.broadcasted_iota(jnp.int32, (rows, rows), 1)
    tri = (i >= j).astype(F32)
    cum = dot(tri, a, precision=HIGH)
    total = cum[rows - 1 : rows, :]
    trail = halves(jnp.where(first == last_first, jnp.exp2(total - cum) * dt, 0.0))
    keep = halves(jnp.where(first < base, jnp.exp2(cum), 0.0))
    thr = halves(jnp.where(last_first < base, jnp.exp2(total), 0.0))
    row8 = lax.broadcasted_iota(jnp.int32, (8, HEADS), 0)
    thr_rows = jnp.where(
        row8 == 0, thr[0].astype(F32), jnp.where(row8 == 1, thr[1].astype(F32), 0.0)
    ).astype(BF16)
    row_ref[...] = jnp.transpose(cum - jnp.log2(dt))
    for g in range(GROUPS):
        part = slice(g * PER_GROUP, (g + 1) * PER_GROUP)
        col_ref[g] = cum[:, part]
        trail_ref[g] = jnp.concatenate([trail[0][:, part], trail[1][:, part]], axis=1)
        keep_ref[g] = jnp.concatenate([keep[0][:, part], keep[1][:, part]], axis=1)
        thr_ref[g] = thr_rows[:, part]


def front_kernel(
    place_ref, lengths_ref, x_ref, b_ref, c_ref, hx_ref, hb_ref, hc_ref,
    wx_ref, wb_ref, wc_ref, ox_ref, ob_ref, oc_ref, trail_ref, thr_ref,
    xa_ref, ba_ref, ca_ref, f_ref, pad_ref,
):
    rows = x_ref.shape[0]
    base = place_ref[0] * rows
    starts = doc_starts(place_ref, lengths_ref)
    pos = base + lax.broadcasted_iota(jnp.int32, (rows, 128), 0)
    rel = pos - row_starts(starts, pos)
    masks = [None] + [rel >= d for d in range(1, CONV)]

    def conv(src, rim, weight, bias, dst, lo):
        at = slice(lo, lo + 128)
        pad_ref[0:8, :] = rim[:, at].astype(F32)
        pad_ref[8 : 8 + rows, :] = src[:, at].astype(F32)
        acc = pad_ref[8 : 8 + rows, :] * weight[3:4, at] + bias[:, at]
        for d in range(1, CONV):
            tap = pad_ref[8 - d : 8 - d + rows, :] * weight[3 - d : 4 - d, at]
            acc = acc + jnp.where(masks[d], tap, 0.0)
        dst[:, at] = silu(acc).astype(BF16)

    for lo in range(0, WIDTH, 128):
        conv(x_ref, hx_ref, wx_ref, ox_ref, xa_ref, lo)
    conv(b_ref, hb_ref, wb_ref, ob_ref, ba_ref, 0)
    conv(c_ref, hc_ref, wc_ref, oc_ref, ca_ref, 0)

    scale = dot(trail_ref[0], expand_heads(2))
    weighted = (xa_ref[...].astype(F32) * scale).astype(BF16)
    fresh = dot(ba_ref[...], weighted, (((0,), (0,)), ((), ()))).astype(BF16)
    extra = dot(thr_ref[0], expand_heads(1)).astype(BF16)
    half = WIDTH // 2
    for k in range(2):
        f_ref[k, 0:STATE, :] = fresh[:, k * half : (k + 1) * half]
        f_ref[k, STATE : STATE + EXTRA, :] = extra[:, k * half : (k + 1) * half]


def inner_kernel(place_ref, lengths_ref, xa_ref, ba_ref, ca_ref, col_ref, row_ref, skip_ref, y_ref):
    rows = xa_ref.shape[0]
    base = place_ref[0] * rows
    starts = doc_starts(place_ref, lengths_ref)
    i = base + lax.broadcasted_iota(jnp.int32, (rows, rows), 0)
    j = base + lax.broadcasted_iota(jnp.int32, (rows, rows), 1)
    first = row_starts(starts, i)
    blocked = jnp.where((j <= i) & (j >= first), 0.0, NEGATIVE)
    scores = dot(ca_ref[...], ba_ref[...], (((1,), (1,)), ((), ())))
    lane = lax.broadcasted_iota(jnp.int32, (rows, 128), 1)
    col = col_ref[0]
    for p in range(PER_GROUP // 2):
        weights = []
        for h in (2 * p, 2 * p + 1):
            spread = (col[:, h : h + 1] + blocked) - row_ref[h : h + 1, :]
            weights.append((scores * jnp.exp2(spread)).astype(BF16))
        at = slice(p * 128, (p + 1) * 128)
        x = xa_ref[:, at]
        zero = jnp.zeros_like(x)
        both = jnp.concatenate(
            [jnp.where(lane < HEAD_DIM, x, zero), jnp.where(lane < HEAD_DIM, zero, x)], axis=0
        )
        y = dot(jnp.concatenate(weights, axis=1), both)
        y_ref[:, at] = y + x.astype(F32) * skip_ref[:, at]


def scan_kernel(f_ref, o_ref, out_ref):
    blocks, _, width = f_ref.shape
    piece = 32
    for r in range(blocks):
        out_ref[r, :, width:] = o_ref[r]

    def body(q, carry):
        at = pl.ds(pl.multiple_of(q * piece, piece), piece)
        state = jnp.zeros((piece, width), F32)
        for r in range(blocks):
            out_ref[r, at, :width] = state.astype(BF16)
            if r + 1 < blocks:
                tail = f_ref[r, STATE : STATE + EXTRA, :].astype(F32)
                thr = tail[0:1, :] + tail[1:2, :]
                state = state * thr + f_ref[r, at, :].astype(F32)
        return carry

    lax.fori_loop(0, STATE // piece, body, 0)


def final_kernel(y_ref, s_ref, ca_ref, keep_ref, z_ref, gain_ref, o_ref, attn_ref):
    scale = dot(keep_ref[0], expand_heads(2))
    half = WIDTH // 2
    parts = []
    for k in range(2):
        parts.append(dot(ca_ref[...], s_ref[k, :, :half]))
        own = s_ref.shape[2] - half
        attn_ref[:, k * own : (k + 1) * own] = s_ref[k, :, half:]
    carried = jnp.concatenate(parts, axis=1)
    mixed = (y_ref[...] + scale * carried).astype(BF16).astype(F32)
    gated = mixed * silu(z_ref[...].astype(F32))
    mean = jnp.mean(gated * gated, axis=1, keepdims=True)
    o_ref[...] = (gated * lax.rsqrt(mean + EPSILON) * gain_ref[...]).astype(BF16)


def pack_kernel(q_ref, k_ref, v_ref, out_ref):
    parts = out_ref.shape[0]
    width = q_ref.shape[1] // parts
    for d in range(parts):
        at = d * KVHEADS // parts * QDIM
        out_ref[d, :, :width] = q_ref[:, d * width : (d + 1) * width]
        out_ref[d, :, width : width + QDIM] = k_ref[:, at : at + QDIM]
        out_ref[d, :, width + QDIM :] = v_ref[:, at : at + QDIM]


def attend_kernel(place_ref, lengths_ref, qkv_ref, o_ref, s_ref, m_ref, l_ref, acc_ref):
    length = qkv_ref.shape[0]
    q_width = qkv_ref.shape[1] - 2 * QDIM
    heads = q_width // QDIM
    k_cols, v_cols = slice(q_width, q_width + QDIM), slice(q_width + QDIM, q_width + 2 * QDIM)
    starts = doc_starts(place_ref, lengths_ref)
    lane = lax.broadcasted_iota(jnp.int32, (KEYS, KEYS), 1)
    scaling = QDIM ** (-0.5) * LOG2E

    def one_tile(t, outer):
        base = t * KEYS
        here = pl.ds(pl.multiple_of(base, KEYS), KEYS)
        pos = base + lax.broadcasted_iota(jnp.int32, (KEYS, KEYS), 0)
        first = jnp.maximum(row_starts(starts, pos), pos - (WINDOW - 1))
        last = base + KEYS - 1
        lowest = jnp.maximum(scalar_start(starts, base), base - (WINDOW - 1))
        highest = jnp.maximum(scalar_start(starts, last), last - (WINDOW - 1))
        begin = lowest // KEYS
        clear = jnp.minimum((highest + KEYS - 1) // KEYS, t)
        queries = jnp.concatenate([qkv_ref[here, h * QDIM : (h + 1) * QDIM] for h in range(heads)], axis=0)
        m_ref[...] = jnp.full_like(m_ref, NEGATIVE)

        def score(masked, j, carry):
            k = qkv_ref[pl.ds(pl.multiple_of(j * KEYS, KEYS), KEYS), k_cols]
            s = dot(queries, k, (((1,), (1,)), ((), ())))
            if masked:
                key = j * KEYS + lane
                visible = (key <= pos) & (key >= first)
            for h in range(heads):
                at = slice(h * KEYS, (h + 1) * KEYS)
                part = s[at]
                if masked:
                    part = jnp.where(visible, part, NEGATIVE)
                s_ref[j, at, :] = part
                top = m_ref[at, :]
                for c in range(0, KEYS, 128):
                    top = jnp.maximum(top, part[:, c : c + 128])
                m_ref[at, :] = top
            return carry

        lax.fori_loop(begin, clear, functools.partial(score, True), 0)
        lax.fori_loop(clear, t, functools.partial(score, False), 0)
        score(True, t, 0)
        m_ref[...] = jnp.broadcast_to(jnp.max(m_ref[...], axis=1, keepdims=True), m_ref.shape)
        l_ref[...] = jnp.zeros_like(l_ref)
        acc_ref[...] = jnp.zeros_like(acc_ref)

        def gather(j, carry):
            v = qkv_ref[pl.ds(pl.multiple_of(j * KEYS, KEYS), KEYS), v_cols]
            numerators = []
            for h in range(heads):
                at = slice(h * KEYS, (h + 1) * KEYS)
                top = m_ref[at, :]
                total = l_ref[at, :]
                parts = []
                for c in range(0, KEYS, 128):
                    p = jnp.exp2((s_ref[j, at, c : c + 128] - top) * scaling)
                    total = total + p
                    parts.append(p.astype(BF16))
                l_ref[at, :] = total
                numerators.append(jnp.concatenate(parts, axis=1))
            acc_ref[...] += dot(jnp.concatenate(numerators, axis=0), v)
            return carry

        lax.fori_loop(begin, t + 1, gather, 0)
        for h in range(heads):
            at = slice(h * KEYS, (h + 1) * KEYS)
            total = jnp.sum(l_ref[at, :], axis=1, keepdims=True)
            o_ref[here, h * QDIM : (h + 1) * QDIM] = (acc_ref[at, :] / total).astype(BF16)
        return outer

    lax.fori_loop(0, length // KEYS, one_tile, 0)


def work(microseconds):
    return pl.CostEstimate(flops=0, transcendentals=0, bytes_accessed=int(microseconds * 3.5e6))


def smem():
    return pl.BlockSpec(memory_space=pltpu.SMEM)


def on_device(
    mixer_input, z_gate, time_step, conv_weight, conv_bias, decay_rate, skip_gain,
    norm_gain, doc_lengths, queries, attn_keys, attn_values,
):
    rows = mixer_input.shape[1]
    blocks = lax.axis_size("ctx")
    place = jnp.stack([lax.axis_index("ctx"), lax.axis_index("batch")]).astype(jnp.int32)
    raw = mixer_input[0]
    call = functools.partial(
        pl.pallas_call, compiler_params=pltpu.CompilerParams(vmem_limit_bytes=56 << 20)
    )

    o_width = QHEADS * QDIM // blocks
    qkv = call(
        pack_kernel,
        out_shape=jax.ShapeDtypeStruct((blocks, rows, o_width + 2 * QDIM), BF16),
        name="pack",
        cost_estimate=work(3),
    )(queries[0], attn_keys[0], attn_values[0])
    raw, qkv = lax.optimization_barrier((raw, qkv))
    qkv = lax.all_to_all(qkv, "ctx", split_axis=0, concat_axis=0, tiled=True)
    rim = lax.ppermute(raw[rows - 8 :], "ctx", [(r, r + 1) for r in range(blocks - 1)])

    col, row, trail, keep, thr = call(
        prep_kernel,
        in_specs=[smem(), smem(), pl.BlockSpec(), pl.BlockSpec()],
        out_shape=[
            jax.ShapeDtypeStruct((GROUPS, rows, PER_GROUP), F32),
            jax.ShapeDtypeStruct((HEADS, rows), F32),
            jax.ShapeDtypeStruct((GROUPS, rows, 2 * PER_GROUP), BF16),
            jax.ShapeDtypeStruct((GROUPS, rows, 2 * PER_GROUP), BF16),
            jax.ShapeDtypeStruct((GROUPS, 8, PER_GROUP), BF16),
        ],
        name="prep",
        cost_estimate=work(3),
    )(place, doc_lengths, time_step[0], decay_rate[None])

    wide = lambda n: pl.BlockSpec((n, WIDTH), lambda g: (0, g))
    b_cols = lambda n: pl.BlockSpec((n, STATE), lambda g: (0, INNER // STATE + g))
    c_cols = lambda n: pl.BlockSpec((n, STATE), lambda g: (0, INNER // STATE + GROUPS + g))
    group_cols = lambda n: pl.BlockSpec((n, STATE), lambda g: (0, g))
    per_group = pl.BlockSpec((1, rows, PER_GROUP), lambda g: (g, 0, 0))
    per_group_two = pl.BlockSpec((1, rows, 2 * PER_GROUP), lambda g: (g, 0, 0))
    bias = conv_bias[None]
    half = WIDTH // 2
    x_act, b_act, c_act, fresh = call(
        front_kernel,
        grid=(GROUPS,),
        in_specs=[
            smem(), smem(),
            wide(rows), b_cols(rows), c_cols(rows),
            wide(8), b_cols(8), c_cols(8),
            wide(CONV), b_cols(CONV), c_cols(CONV),
            wide(1), b_cols(1), c_cols(1),
            per_group_two, pl.BlockSpec((1, 8, PER_GROUP), lambda g: (g, 0, 0)),
        ],
        out_specs=[
            wide(rows), group_cols(rows), group_cols(rows),
            pl.BlockSpec((2, STATE + EXTRA, half), lambda g: (g, 0, 0)),
        ],
        out_shape=[
            jax.ShapeDtypeStruct((rows, INNER), BF16),
            jax.ShapeDtypeStruct((rows, GROUPS * STATE), BF16),
            jax.ShapeDtypeStruct((rows, GROUPS * STATE), BF16),
            jax.ShapeDtypeStruct((2 * GROUPS, STATE + EXTRA, half), BF16),
        ],
        scratch_shapes=[pltpu.VMEM((8 + rows, 128), F32)],
        name="front",
        cost_estimate=work(40),
    )(
        place, doc_lengths, raw, raw, raw, rim, rim, rim,
        conv_weight, conv_weight, conv_weight, bias, bias, bias, trail, thr,
    )

    local = call(
        inner_kernel,
        grid=(GROUPS,),
        in_specs=[
            smem(), smem(), wide(rows), group_cols(rows), group_cols(rows), per_group,
            pl.BlockSpec((PER_GROUP, rows), lambda g: (g, 0)), wide(1),
        ],
        out_specs=wide(rows),
        out_shape=jax.ShapeDtypeStruct((rows, INNER), F32),
        name="inner",
        cost_estimate=work(9),
    )(place, doc_lengths, x_act, b_act, c_act, col, row, jnp.repeat(skip_gain, HEAD_DIM)[None])

    fresh, qkv, local = lax.optimization_barrier((fresh, qkv, local))
    own_fresh = lax.all_to_all(fresh, "ctx", split_axis=0, concat_axis=0, tiled=True)

    tall = o_width // QDIM * KEYS
    attended = call(
        attend_kernel,
        in_specs=[smem(), smem(), pl.BlockSpec()],
        out_shape=jax.ShapeDtypeStruct((blocks * rows, o_width), BF16),
        scratch_shapes=[
            pltpu.VMEM((blocks * rows // KEYS, tall, KEYS), F32),
            pltpu.VMEM((tall, 128), F32),
            pltpu.VMEM((tall, 128), F32),
            pltpu.VMEM((tall, QDIM), F32),
        ],
        name="attend",
        cost_estimate=work(30),
    )(place, doc_lengths, qkv.reshape(blocks * rows, o_width + 2 * QDIM))
    own_states = call(
        scan_kernel,
        out_shape=jax.ShapeDtypeStruct((blocks, STATE, half + o_width), BF16),
        name="scan",
        cost_estimate=work(4),
    )(own_fresh, attended.reshape(blocks, rows, o_width))
    states = lax.all_to_all(own_states, "ctx", split_axis=0, concat_axis=0, tiled=True)

    mixer_out, attn_out = call(
        final_kernel,
        grid=(GROUPS,),
        in_specs=[
            wide(rows), pl.BlockSpec((2, STATE, half + o_width), lambda g: (g, 0, 0)), group_cols(rows),
            per_group_two, wide(rows), wide(1),
        ],
        out_specs=[wide(rows), pl.BlockSpec((rows, 2 * o_width), lambda g: (0, g))],
        out_shape=[
            jax.ShapeDtypeStruct((rows, INNER), BF16),
            jax.ShapeDtypeStruct((rows, QHEADS * QDIM), BF16),
        ],
        name="final",
        cost_estimate=work(7),
    )(local, states, c_act, keep, z_gate[0], norm_gain[None])
    return (mixer_out[None], attn_out[None])


def solution(mesh):
    placed = P("batch", "ctx", None)
    whole = P()
    return jax.shard_map(
        on_device,
        mesh=mesh,
        in_specs=(placed, placed, placed) + (whole,) * 6 + (placed,) * 3,
        out_specs=(placed, placed),
        check_vma=False,
    )
```

time: 195 us -> 154 us (0.79)
  the two profiles are of different devices: /device:TPU:22 before, /device:TPU:0 now
where the time goes in v2:
time: 154 us; the launch traced here: 153 us
  Pallas kernels  53.3 us (35%)
  blocking collectives  41.1 us (27%)
  waiting for transfers between devices  32.3 us (21%)
  starting transfers between devices  20.3 us (13%)
  local copies, waits for them, and re-layouts  5.11 us (3%)
    all_to_all x1, blocking collectives, on_device(): lax.all_to_all(own_states, 'ctx', split_axis=0, concat_axis=0, tiled=True)  41.1 us
    ppermute x1, waiting for transfers between devices, on_device(): lax.ppermute(raw[rows - 8:], 'ctx', [(r, r + 1) for r in range(blocks - 1)])  17.5 us
    pallas_call x1, Pallas kernels, on_device(): call(attend_kernel, in_specs=[smem(), smem(), pl.BlockSpec()], out_shape=...  16.4 us
    all_to_all x1, waiting for transfers between devices, on_device(): lax.all_to_all(fresh, 'ctx', split_axis=0, concat_axis=0, tiled=True)  14.8 us
    pallas_call x1, Pallas kernels, on_device(): call(front_kernel, grid=(GROUPS,), in_specs=[smem(), smem(), wide(rows),...  10 us
    pallas_call x1, Pallas kernels, on_device(): call(final_kernel, grid=(GROUPS,), in_specs=[wide(rows), pl.BlockSpec((2,...  8.82 us
    pallas_call x1, Pallas kernels, on_device(): call(inner_kernel, grid=(GROUPS,), in_specs=[smem(), smem(), wide(rows),...  8.47 us
    all_to_all x1, starting transfers between devices, on_device(): lax.all_to_all(fresh, 'ctx', split_axis=0, concat_axis=0, tiled=True)  8.37 us
  transfers between devices with their start and end apart: 3, of which 2 were waited for; matrix products, arithmetic and copies ran while one was open for 2% of the time, Pallas kernels for 24%

profile of v2, /device:TPU:0, one launch (start us, length us, event | category | flops | bytes accessed | tf_op | source)
XLA Modules:
  0.0 153.3 jit_solution(9895240044214566787)
XLA Ops:
  0.6 2.9 %pack.1 = bf16[16,128,512]{2,1,0:T(8,128)(2,1)} custom-call(bf16[128,4096]{1,0:T(8,128)(2,1)} %bitcast.22, bf16[128,1024]{1,0:T(8,128)(2,1)} %bitcast.26, bf16[128,1024]{1,0:T(8,128)(2,1)} %bitcast.27), custom_call_target="tpu_custom_call" | custom-call | bytes 10500000 | tf_op jit(solution)/shard_map/pack/pallas_call | solution.py:311
  3.6 0.0 copy-start.3
  3.6 8.1 %all-to-all-start = ((bf16[16,128,512]{2,1,0:T(8,128)(2,1)}), bf16[16,128,512]{2,1,0:T(8,128)(2,1)S(1)}, u32[]{:S(2)}, u32[]{:S(2)}) async-start(bf16[16,128,512]{2,1,0:T(8,128)(2,1)} %pack.1), calls=%async_computation | async-start | bytes 4194304 | tf_op jit(solution)/shard_map/all_to_all | solution.py:318
  11.7 0.9 slice.3
  12.6 3.8 %collective-permute-start = (bf16[8,10240]{1,0:T(8,128)(2,1)S(1)}, bf16[8,10240]{1,0:T(8,128)(2,1)S(1)}, u32[]{:S(2)}, u32[]{:S(2)}) collective-permute-start(bf16[8,10240]{1,0:T(8,128)(2,1)S(1)} %slice.3), channel_id=1, source_target_pairs={{0,8},{8,16},{16,24},{24,32},{32,40},{40,48},{48,56},{56,64},{64,7... | collective-permute-start | bytes 491528 | tf_op jit(solution)/shard_map/ppermute | solution.py:319
  16.4 0.0 copy-done.3
  16.5 0.1 broadcast_in_dim.20
  16.5 0.7 broadcast_in_dim_reshape.3.skip_ref
  17.2 0.6 pad_add_fusion.place_ref
  17.8 2.4 %prep.1 = (f32[8,128,16]{2,1,0:T(8,128)}, f32[128,128]{1,0:T(8,128)}, bf16[8,128,32]{2,1,0:T(8,128)(2,1)}, bf16[8,128,32]{2,1,0:T(8,128)(2,1)}, bf16[8,8,16]{2,1,0:T(8,128)(2,1)}) custom-call(s32[2]{0:T(128)} %pad_add_fusion.place_ref, s32[8,6]{1,0:T(8,128)} %lengths_ref.7, bf16[128,128]{1,0:T(8,128)(2,1)} %bitcast.29, f32[1,128]{1,0:T(1,128)} %bitcast.30), custom_call_target="tpu_custom_call" | custom-call | bytes 10500000 | tf_op jit(solution)/shard_map/prep/pallas_call | solution.py:321
  20.3 17.5 %collective-permute-done.hx_ref.hb_ref.hc_ref = bf16[8,10240]{1,0:T(8,128)(2,1)S(1)} collective-permute-done((bf16[8,10240]{1,0:T(8,128)(2,1)S(1)}, bf16[8,10240]{1,0:T(8,128)(2,1)S(1)}, u32[]{:S(2)}, u32[]{:S(2)}) %collective-permute-start) | collective-permute-done | bytes 163872 | tf_op jit(solution)/shard_map/ppermute | solution.py:319
  37.7 0.0 copy-start.2
  37.7 0.7 copy-done.2
  38.4 10.0 %front.1 = (bf16[128,8192]{1,0:T(8,128)(2,1)}, bf16[128,1024]{1,0:T(8,128)(2,1)}, bf16[128,1024]{1,0:T(8,128)(2,1)}, bf16[16,136,512]{2,1,0:T(8,128)(2,1)}) custom-call(s32[2]{0:T(128)} %pad_add_fusion.place_ref, s32[8,6]{1,0:T(8,128)} %lengths_ref.7, bf16[128,10240]{1,0:T(8,128)(2,1)} %bitcast.16, bf16[128,10240]{1,0:T(8,128)(2,1)} %bitcast.17, ...), custom_call_target="tpu_custom_call" | custom-call | bytes 140000000 | tf_op jit(solution)/shard_map/front/pallas_call | solution.py:343
  48.4 8.5 %inner.1.y_ref = f32[128,8192]{1,0:T(8,128)} custom-call(s32[2]{0:T(128)} %pad_add_fusion.place_ref, s32[8,6]{1,0:T(8,128)} %lengths_ref.7, bf16[128,8192]{1,0:T(8,128)(2,1)} %get-tuple-element.23.xa_ref, bf16[128,1024]{1,0:T(8,128)(2,1)} %get-tuple-element.24.ba_ref, bf16[128,1024]{1,0:T(8,128)(2,1)} %get-tuple-element.25.ca_ref, ...), custom_call_target="tpu_custom_call" | custom-call | bytes 31500000 | tf_op jit(solution)/shard_map/inner/pallas_call | solution.py:372
  56.9 0.0 all-to-all-done
  56.9 0.0 copy-start.1
  56.9 1.3 copy-done.1
  58.2 8.4 %all-to-all-start.1 = ((bf16[16,136,512]{2,1,0:T(8,128)(2,1)}), bf16[16,136,512]{2,1,0:T(8,128)(2,1)S(1)}, u32[]{:S(2)}, u32[]{:S(2)}) async-start(bf16[16,136,512]{2,1,0:T(8,128)(2,1)} %get-tuple-element.29), calls=%async_computation.1 | async-start | bytes 4456448 | tf_op jit(solution)/shard_map/all_to_all | solution.py:386
  66.6 16.4 %attend.1 = bf16[2048,256]{1,0:T(8,128)(2,1)} custom-call(s32[2]{0:T(128)} %pad_add_fusion.place_ref, s32[8,6]{1,0:T(8,128)} %lengths_ref.7, bf16[2048,512]{1,0:T(8,128)(2,1)} %bitcast.19), custom_call_target="tpu_custom_call" | custom-call | bytes 105000000 | tf_op jit(solution)/shard_map/attend/pallas_call | solution.py:389
  83.0 14.8 %all-to-all-done.1.f_ref = bf16[16,136,512]{2,1,0:T(8,128)(2,1)S(1)} async-done(((bf16[16,136,512]{2,1,0:T(8,128)(2,1)}), bf16[16,136,512]{2,1,0:T(8,128)(2,1)S(1)}, u32[]{:S(2)}, u32[]{:S(2)}) %all-to-all-start.1) | async-done | bytes 2228256 | tf_op jit(solution)/shard_map/all_to_all | solution.py:386
  97.8 0.0 copy-start
  97.8 1.4 copy-done
  99.2 4.3 %scan.1 = bf16[16,128,768]{2,1,0:T(8,128)(2,1)} custom-call(bf16[16,136,512]{2,1,0:T(8,128)(2,1)} %copy-done, bf16[16,128,256]{2,1,0:T(8,128)(2,1)} %bitcast.20), custom_call_target="tpu_custom_call" | custom-call | bytes 14000000 | tf_op jit(solution)/shard_map/scan/pallas_call | solution.py:402
  103.4 41.1 %all_to_all.15.s_ref = bf16[16,128,768]{2,1,0:T(8,128)(2,1)} all-to-all(bf16[16,128,768]{2,1,0:T(8,128)(2,1)} %scan.1), channel_id=1, replica_groups=mesh['ctx'=16,'batch'=8] {'ctx'}, dimensions={0} | all-to-all | bytes 6291456 | tf_op jit(solution)/shard_map/all_to_all | solution.py:408
  144.5 8.8 %final.1 = (bf16[128,8192]{1,0:T(8,128)(2,1)}, bf16[128,4096]{1,0:T(8,128)(2,1)}) custom-call(f32[128,8192]{1,0:T(8,128)} %inner.1.y_ref, bf16[16,128,768]{2,1,0:T(8,128)(2,1)} %all_to_all.15.s_ref, bf16[128,1024]{1,0:T(8,128)(2,1)} %get-tuple-element.25.ca_ref, bf16[8,128,32]{2,1,0:T(8,128)(2,1)} %get-tuple-element.31.keep_ref, bf16[128,8192]{1,0:T(8,128)(2,1)} %bitcast.21, ...), custom_call_target="tpu_custom_call" | custom-call | bytes 24500000 | tf_op jit(solution)/shard_map/final/pallas_call | solution.py:410
Async XLA Ops:
  3.6 12.9 %copy-start.3 = (f32[128]{0:T(128)S(1)}, f32[128]{0:T(128)}, u32[]{:S(2)}) copy-start(f32[128]{0:T(128)} %param.18) | copy-start | bytes 1540
  3.6 53.3 %all-to-all-start = ((bf16[16,128,512]{2,1,0:T(8,128)(2,1)}), bf16[16,128,512]{2,1,0:T(8,128)(2,1)S(1)}, u32[]{:S(2)}, u32[]{:S(2)}) async-start(bf16[16,128,512]{2,1,0:T(8,128)(2,1)} %pack.1), calls=%async_computation | async-start | bytes 4194304 | tf_op jit(solution)/shard_map/all_to_all | solution.py:318
  12.6 25.1 %collective-permute-start = (bf16[8,10240]{1,0:T(8,128)(2,1)S(1)}, bf16[8,10240]{1,0:T(8,128)(2,1)S(1)}, u32[]{:S(2)}, u32[]{:S(2)}) collective-permute-start(bf16[8,10240]{1,0:T(8,128)(2,1)S(1)} %slice.3), channel_id=1, source_target_pairs={{0,8},{8,16},{16,24},{24,32},{32,40},{40,48},{48,56},{56,64},{64,7... | collective-permute-start | bytes 491528 | tf_op jit(solution)/shard_map/ppermute | solution.py:319
  37.7 0.7 copy-start.2
  56.9 1.3 copy-start.1
  58.2 39.6 %all-to-all-start.1 = ((bf16[16,136,512]{2,1,0:T(8,128)(2,1)}), bf16[16,136,512]{2,1,0:T(8,128)(2,1)S(1)}, u32[]{:S(2)}, u32[]{:S(2)}) async-start(bf16[16,136,512]{2,1,0:T(8,128)(2,1)} %get-tuple-element.29), calls=%async_computation.1 | async-start | bytes 4456448 | tf_op jit(solution)/shard_map/all_to_all | solution.py:386
  97.8 1.4 copy-start

commit v3 on v2

--- a/solution.py
+++ b/solution.py
@@ -26,6 +26,7 @@
 LOG2E = 1.4426950408889634
 EXTRA = 8
 KEYS = 256
+PIECE = 32
 
 F32 = jnp.float32
 BF16 = jnp.bfloat16
@@ -168,24 +169,32 @@
         y_ref[:, at] = y + x.astype(F32) * skip_ref[:, at]
 
 
-def scan_kernel(f_ref, o_ref, out_ref):
+def scan_kernel(f_ref, o_ref, out_ref, tail_ref, held_ref, sems, tail_sem):
     blocks, _, width = f_ref.shape
-    piece = 32
+    pieces, _, piece, _ = held_ref.shape
+
+    def copy(q):
+        at = pl.ds(q * piece, piece)
+        return pltpu.make_async_copy(f_ref.at[:, at, :], held_ref.at[q], sems.at[q])
+
+    tail = pltpu.make_async_copy(f_ref.at[:, pl.ds(STATE, EXTRA), :], tail_ref, tail_sem)
+
+    @pl.when(pl.program_id(0) == 0)
+    def _():
+        tail.start()
+        for q in range(pieces):
+            copy(q).start()
+        tail.wait()
+
+    step = pl.program_id(0)
+    copy(step).wait()
+    out_ref[:, :, width:] = o_ref[...]
+    state = jnp.zeros((piece, width), F32)
     for r in range(blocks):
-        out_ref[r, :, width:] = o_ref[r]
-
-    def body(q, carry):
-        at = pl.ds(pl.multiple_of(q * piece, piece), piece)
-        state = jnp.zeros((piece, width), F32)
-        for r in range(blocks):
-            out_ref[r, at, :width] = state.astype(BF16)
-            if r + 1 < blocks:
-                tail = f_ref[r, STATE : STATE + EXTRA, :].astype(F32)
-                thr = tail[0:1, :] + tail[1:2, :]
-                state = state * thr + f_ref[r, at, :].astype(F32)
-        return carry
-
-    lax.fori_loop(0, STATE // piece, body, 0)
+        out_ref[r, :, :width] = state.astype(BF16)
+        if r + 1 < blocks:
+            ends = tail_ref[r].astype(F32)
+            state = state * (ends[0:1, :] + ends[1:2, :]) + held_ref[step, r].astype(F32)
 
 
 def final_kernel(y_ref, s_ref, ca_ref, keep_ref, z_ref, gain_ref, o_ref, attn_ref):
@@ -213,7 +222,10 @@
         out_ref[d, :, width + QDIM :] = v_ref[:, at : at + QDIM]
 
 
-def attend_kernel(place_ref, lengths_ref, qkv_ref, o_ref, s_ref, m_ref, l_ref, acc_ref):
+def attend_kernel(place_ref, lengths_ref, far_ref, o_ref, qkv_ref, sem, s_ref, m_ref, l_ref, acc_ref):
+    copy = pltpu.make_async_copy(far_ref, qkv_ref, sem)
+    copy.start()
+    copy.wait()
     length = qkv_ref.shape[0]
     q_width = qkv_ref.shape[1] - 2 * QDIM
     heads = q_width // QDIM
@@ -304,7 +316,7 @@
     place = jnp.stack([lax.axis_index("ctx"), lax.axis_index("batch")]).astype(jnp.int32)
     raw = mixer_input[0]
     call = functools.partial(
-        pl.pallas_call, compiler_params=pltpu.CompilerParams(vmem_limit_bytes=56 << 20)
+        pl.pallas_call, compiler_params=pltpu.CompilerParams(vmem_limit_bytes=63 << 20)
     )
 
     o_width = QHEADS * QDIM // blocks
@@ -314,9 +326,9 @@
         name="pack",
         cost_estimate=work(3),
     )(queries[0], attn_keys[0], attn_values[0])
-    raw, qkv = lax.optimization_barrier((raw, qkv))
+    rim = lax.ppermute(raw[rows - 8 :], "ctx", [(r, r + 1) for r in range(blocks - 1)])
+    rim, qkv = lax.optimization_barrier((rim, qkv))
     qkv = lax.all_to_all(qkv, "ctx", split_axis=0, concat_axis=0, tiled=True)
-    rim = lax.ppermute(raw[rows - 8 :], "ctx", [(r, r + 1) for r in range(blocks - 1)])
 
     col, row, trail, keep, thr = call(
         prep_kernel,
@@ -388,9 +400,11 @@
     tall = o_width // QDIM * KEYS
     attended = call(
         attend_kernel,
-        in_specs=[smem(), smem(), pl.BlockSpec()],
+        in_specs=[smem(), smem(), pl.BlockSpec(memory_space=pl.ANY)],
         out_shape=jax.ShapeDtypeStruct((blocks * rows, o_width), BF16),
         scratch_shapes=[
+            pltpu.VMEM((blocks * rows, o_width + 2 * QDIM), BF16),
+            pltpu.SemaphoreType.DMA,
             pltpu.VMEM((blocks * rows // KEYS, tall, KEYS), F32),
             pltpu.VMEM((tall, 128), F32),
             pltpu.VMEM((tall, 128), F32),
@@ -401,7 +415,19 @@
     )(place, doc_lengths, qkv.reshape(blocks * rows, o_width + 2 * QDIM))
     own_states = call(
         scan_kernel,
+        grid=(STATE // PIECE,),
+        in_specs=[
+            pl.BlockSpec(memory_space=pl.ANY),
+            pl.BlockSpec((blocks, PIECE, o_width), lambda q: (0, q, 0)),
+        ],
+        out_specs=pl.BlockSpec((blocks, PIECE, half + o_width), lambda q: (0, q, 0)),
         out_shape=jax.ShapeDtypeStruct((blocks, STATE, half + o_width), BF16),
+        scratch_shapes=[
+            pltpu.VMEM((blocks, EXTRA, half), BF16),
+            pltpu.VMEM((STATE // PIECE, blocks, PIECE, half), BF16),
+            pltpu.SemaphoreType.DMA((STATE // PIECE,)),
+            pltpu.SemaphoreType.DMA,
+        ],
         name="scan",
         cost_estimate=work(4),
     )(own_fresh, attended.reshape(blocks, rows, o_width))

time: 154 us -> 135 us (0.88)
  waiting for transfers between devices: 32.3 us -> 15.6 us
  Pallas kernels: 53.3 us -> 58.2 us
  starting transfers between devices: 20.3 us -> 16.9 us
  local copies, waits for them, and re-layouts: 5.11 us -> 1.72 us
    ppermute x1, waiting for transfers between devices: 17.5 us -> 0.47 us  [on_device(): lax.ppermute(raw[rows - 8:], 'ctx', [(r, r + 1) for r in range(blocks - 1)])]
    all_to_all x1, waiting for transfers between devices: 0.01 us -> 6.56 us  [on_device(): qkv = lax.all_to_all(qkv, 'ctx', split_axis=0, concat_axis=0, tiled=True)]
    all_to_all x1, waiting for transfers between devices: 14.8 us -> 8.6 us  [on_device(): lax.all_to_all(fresh, 'ctx', split_axis=0, concat_axis=0, tiled=True)]
    pallas_call x2, Pallas kernels: 20.7 us -> 25.5 us  [the longest x1 20 us: on_device(): call(attend_kernel, in_specs=[smem(), smem(), pl.BlockSpec(memory_space=p...]
    all_to_all x1, starting transfers between devices: 8.37 us -> 4.46 us  [on_device(): lax.all_to_all(fresh, 'ctx', split_axis=0, concat_axis=0, tiled=True)]
    unnamed x8 -> x4, local copies, waits for them, and re-layouts: 3.39 us -> 0.01 us
  transfers between devices with their start and end apart: 3 -> 3, of which waited for: 2 -> 3; matrix products, arithmetic and copies ran while one was open for 2% -> 1% of each run, Pallas kernels for 24% -> 33%
where the time goes in v3:
time: 135 us; the launch traced here: 134 us
  Pallas kernels  58.2 us (43%)
  blocking collectives  40.2 us (30%)
  starting transfers between devices  16.9 us (13%)
  waiting for transfers between devices  15.6 us (12%)
  local copies, waits for them, and re-layouts  1.72 us (1%)
    all_to_all x1, blocking collectives, on_device(): lax.all_to_all(own_states, 'ctx', split_axis=0, concat_axis=0, tiled=True)  40.2 us
    pallas_call x1, Pallas kernels, on_device(): call(attend_kernel, in_specs=[smem(), smem(), pl.BlockSpec(memory_space=p...  20 us
    pallas_call x1, Pallas kernels, on_device(): call(front_kernel, grid=(GROUPS,), in_specs=[smem(), smem(), wide(rows),...  10 us
    pallas_call x1, Pallas kernels, on_device(): call(final_kernel, grid=(GROUPS,), in_specs=[wide(rows), pl.BlockSpec((2,...  8.8 us
    all_to_all x1, waiting for transfers between devices, on_device(): lax.all_to_all(fresh, 'ctx', split_axis=0, concat_axis=0, tiled=True)  8.6 us
    all_to_all x1, starting transfers between devices, on_device(): qkv = lax.all_to_all(qkv, 'ctx', split_axis=0, concat_axis=0, tiled=True)  8.49 us
    pallas_call x1, Pallas kernels, on_device(): call(inner_kernel, grid=(GROUPS,), in_specs=[smem(), smem(), wide(rows),...  8.46 us
    all_to_all x1, waiting for transfers between devices, on_device(): qkv = lax.all_to_all(qkv, 'ctx', split_axis=0, concat_axis=0, tiled=True)  6.56 us
  transfers between devices with their start and end apart: 3, of which 3 were waited for; matrix products, arithmetic and copies ran while one was open for 1% of the time, Pallas kernels for 33%

profile of v3, /device:TPU:0, one launch (start us, length us, event | category | flops | bytes accessed | tf_op | source)
XLA Modules:
  0.0 134.0 jit_solution(8167736155796628213)
XLA Ops:
  0.6 0.9 slice_bitcast_fusion
  1.6 3.9 %collective-permute-start = (bf16[8,10240]{1,0:T(8,128)(2,1)S(1)}, bf16[8,10240]{1,0:T(8,128)(2,1)S(1)}, u32[]{:S(2)}, u32[]{:S(2)}) collective-permute-start(bf16[8,10240]{1,0:T(8,128)(2,1)S(1)} %slice_bitcast_fusion), channel_id=1, source_target_pairs={{0,8},{8,16},{16,24},{24,32},{32,40},{40,48},{48,56},{56,64},{64,7... | collective-permute-start | bytes 491528 | tf_op jit(solution)/shard_map/ppermute | solution.py:329
  5.5 3.0 %pack.1 = bf16[16,128,512]{2,1,0:T(8,128)(2,1)} custom-call(bf16[128,4096]{1,0:T(8,128)(2,1)} %bitcast.22, bf16[128,1024]{1,0:T(8,128)(2,1)} %bitcast.26, bf16[128,1024]{1,0:T(8,128)(2,1)} %bitcast.27), custom_call_target="tpu_custom_call" | custom-call | bytes 10500000 | tf_op jit(solution)/shard_map/pack/pallas_call | solution.py:323
  8.4 0.0 copy-start.1
  8.4 0.5 collective-permute-done.hx_ref.hb_ref.hc_ref
  8.9 0.0 copy-start
  8.9 8.5 %all-to-all-start = ((bf16[16,128,512]{2,1,0:T(8,128)(2,1)}), bf16[16,128,512]{2,1,0:T(8,128)(2,1)}, u32[]{:S(2)}, u32[]{:S(2)}) async-start(bf16[16,128,512]{2,1,0:T(8,128)(2,1)} %pack.1), calls=%async_computation | async-start | bytes 4194304 | tf_op jit(solution)/shard_map/all_to_all | solution.py:331
  17.4 0.0 copy-done.1
  17.4 0.1 broadcast_in_dim.20
  17.5 0.7 broadcast_in_dim_reshape.3.skip_ref
  18.2 0.6 pad_add_fusion.place_ref
  18.9 2.4 %prep.1 = (f32[8,128,16]{2,1,0:T(8,128)}, f32[128,128]{1,0:T(8,128)}, bf16[8,128,32]{2,1,0:T(8,128)(2,1)}, bf16[8,128,32]{2,1,0:T(8,128)(2,1)}, bf16[8,8,16]{2,1,0:T(8,128)(2,1)}) custom-call(s32[2]{0:T(128)} %pad_add_fusion.place_ref, s32[8,6]{1,0:T(8,128)} %lengths_ref.7, bf16[128,128]{1,0:T(8,128)(2,1)} %bitcast.29, f32[1,128]{1,0:T(1,128)} %bitcast.30), custom_call_target="tpu_custom_call" | custom-call | bytes 10500000 | tf_op jit(solution)/shard_map/prep/pallas_call | solution.py:333
  21.3 0.0 copy-done
  21.3 10.0 %front.1 = (bf16[128,8192]{1,0:T(8,128)(2,1)}, bf16[128,1024]{1,0:T(8,128)(2,1)}, bf16[128,1024]{1,0:T(8,128)(2,1)}, bf16[16,136,512]{2,1,0:T(8,128)(2,1)}) custom-call(s32[2]{0:T(128)} %pad_add_fusion.place_ref, s32[8,6]{1,0:T(8,128)} %lengths_ref.7, bf16[128,10240]{1,0:T(8,128)(2,1)} %bitcast.17, bf16[128,10240]{1,0:T(8,128)(2,1)} %bitcast.18, ...), custom_call_target="tpu_custom_call" | custom-call | bytes 140000000 | tf_op jit(solution)/shard_map/front/pallas_call | solution.py:355
  31.3 8.5 %inner.1.y_ref = f32[128,8192]{1,0:T(8,128)} custom-call(s32[2]{0:T(128)} %pad_add_fusion.place_ref, s32[8,6]{1,0:T(8,128)} %lengths_ref.7, bf16[128,8192]{1,0:T(8,128)(2,1)} %get-tuple-element.23.xa_ref, bf16[128,1024]{1,0:T(8,128)(2,1)} %get-tuple-element.24.ba_ref, bf16[128,1024]{1,0:T(8,128)(2,1)} %get-tuple-element.25.ca_ref, ...), custom_call_target="tpu_custom_call" | custom-call | bytes 31500000 | tf_op jit(solution)/shard_map/inner/pallas_call | solution.py:384
  39.8 6.6 %all-to-all-done = bf16[16,128,512]{2,1,0:T(8,128)(2,1)} async-done(((bf16[16,128,512]{2,1,0:T(8,128)(2,1)}), bf16[16,128,512]{2,1,0:T(8,128)(2,1)}, u32[]{:S(2)}, u32[]{:S(2)}) %all-to-all-start) | async-done | bytes 2097184 | tf_op jit(solution)/shard_map/all_to_all | solution.py:331
  46.3 4.5 %all-to-all-start.1 = ((bf16[16,136,512]{2,1,0:T(8,128)(2,1)}), bf16[16,136,512]{2,1,0:T(8,128)(2,1)}, u32[]{:S(2)}, u32[]{:S(2)}) async-start(bf16[16,136,512]{2,1,0:T(8,128)(2,1)} %get-tuple-element.29), calls=%async_computation.1 | async-start | bytes 4456448 | tf_op jit(solution)/shard_map/all_to_all | solution.py:398
  50.8 20.0 %attend.1 = bf16[2048,256]{1,0:T(8,128)(2,1)} custom-call(s32[2]{0:T(128)} %pad_add_fusion.place_ref, s32[8,6]{1,0:T(8,128)} %lengths_ref.7, bf16[2048,512]{1,0:T(8,128)(2,1)} %bitcast.10.far_ref), custom_call_target="tpu_custom_call" | custom-call | bytes 105000000 | tf_op jit(solution)/shard_map/attend/pallas_call | solution.py:401
  70.8 8.6 %all-to-all-done.1.f_ref = bf16[16,136,512]{2,1,0:T(8,128)(2,1)} async-done(((bf16[16,136,512]{2,1,0:T(8,128)(2,1)}), bf16[16,136,512]{2,1,0:T(8,128)(2,1)}, u32[]{:S(2)}, u32[]{:S(2)}) %all-to-all-start.1) | async-done | bytes 2228256 | tf_op jit(solution)/shard_map/all_to_all | solution.py:398
  79.4 5.5 %scan.1 = bf16[16,128,768]{2,1,0:T(8,128)(2,1)} custom-call(bf16[16,136,512]{2,1,0:T(8,128)(2,1)} %all-to-all-done.1.f_ref, bf16[16,128,256]{2,1,0:T(8,128)(2,1)} %bitcast.20), custom_call_target="tpu_custom_call" | custom-call | bytes 14000000 | tf_op jit(solution)/shard_map/scan/pallas_call | solution.py:416
  84.9 40.2 %all_to_all.15.s_ref = bf16[16,128,768]{2,1,0:T(8,128)(2,1)} all-to-all(bf16[16,128,768]{2,1,0:T(8,128)(2,1)} %scan.1), channel_id=1, replica_groups=mesh['ctx'=16,'batch'=8] {'ctx'}, dimensions={0} | all-to-all | bytes 6291456 | tf_op jit(solution)/shard_map/all_to_all | solution.py:434
  125.2 8.8 %final.1 = (bf16[128,8192]{1,0:T(8,128)(2,1)}, bf16[128,4096]{1,0:T(8,128)(2,1)}) custom-call(f32[128,8192]{1,0:T(8,128)} %inner.1.y_ref, bf16[16,128,768]{2,1,0:T(8,128)(2,1)} %all_to_all.15.s_ref, bf16[128,1024]{1,0:T(8,128)(2,1)} %get-tuple-element.25.ca_ref, bf16[8,128,32]{2,1,0:T(8,128)(2,1)} %get-tuple-element.31.keep_ref, bf16[128,8192]{1,0:T(8,128)(2,1)} %bitcast.21, ...), custom_call_target="tpu_custom_call" | custom-call | bytes 24500000 | tf_op jit(solution)/shard_map/final/pallas_call | solution.py:436
Async XLA Ops:
  1.6 7.4 %collective-permute-start = (bf16[8,10240]{1,0:T(8,128)(2,1)S(1)}, bf16[8,10240]{1,0:T(8,128)(2,1)S(1)}, u32[]{:S(2)}, u32[]{:S(2)}) collective-permute-start(bf16[8,10240]{1,0:T(8,128)(2,1)S(1)} %slice_bitcast_fusion), channel_id=1, source_target_pairs={{0,8},{8,16},{16,24},{24,32},{32,40},{40,48},{48,56},{56,64},{64,7... | collective-permute-start | bytes 491528 | tf_op jit(solution)/shard_map/ppermute | solution.py:329
  8.4 9.0 %copy-start.1 = (f32[128]{0:T(128)S(1)}, f32[128]{0:T(128)}, u32[]{:S(2)}) copy-start(f32[128]{0:T(128)} %param.18) | copy-start | bytes 1540
  8.9 12.4 %copy-start = (bf16[8,10240]{1,0:T(8,128)(2,1)}, bf16[8,10240]{1,0:T(8,128)(2,1)S(1)}, u32[]{:S(2)}) copy-start(bf16[8,10240]{1,0:T(8,128)(2,1)S(1)} %collective-permute-done.hx_ref.hb_ref.hc_ref) | copy-start | bytes 491524
  8.9 37.4 %all-to-all-start = ((bf16[16,128,512]{2,1,0:T(8,128)(2,1)}), bf16[16,128,512]{2,1,0:T(8,128)(2,1)}, u32[]{:S(2)}, u32[]{:S(2)}) async-start(bf16[16,128,512]{2,1,0:T(8,128)(2,1)} %pack.1), calls=%async_computation | async-start | bytes 4194304 | tf_op jit(solution)/shard_map/all_to_all | solution.py:331
  46.3 33.0 %all-to-all-start.1 = ((bf16[16,136,512]{2,1,0:T(8,128)(2,1)}), bf16[16,136,512]{2,1,0:T(8,128)(2,1)}, u32[]{:S(2)}, u32[]{:S(2)}) async-start(bf16[16,136,512]{2,1,0:T(8,128)(2,1)} %get-tuple-element.29), calls=%async_computation.1 | async-start | bytes 4456448 | tf_op jit(solution)/shard_map/all_to_all | solution.py:398

commit v4 on v3

--- a/solution.py
+++ b/solution.py
@@ -27,6 +27,7 @@
 EXTRA = 8
 KEYS = 256
 PIECE = 32
+CHUNK = 16
 
 F32 = jnp.float32
 BF16 = jnp.bfloat16
@@ -169,47 +170,51 @@
         y_ref[:, at] = y + x.astype(F32) * skip_ref[:, at]
 
 
-def scan_kernel(f_ref, o_ref, out_ref, tail_ref, held_ref, sems, tail_sem):
+def scan_kernel(f_ref, held_out_ref, out_ref, tail_ref, held_ref, state_ref, sems, out_sems, tail_sem):
     blocks, _, width = f_ref.shape
     pieces, _, piece, _ = held_ref.shape
-
-    def copy(q):
-        at = pl.ds(q * piece, piece)
-        return pltpu.make_async_copy(f_ref.at[:, at, :], held_ref.at[q], sems.at[q])
-
     tail = pltpu.make_async_copy(f_ref.at[:, pl.ds(STATE, EXTRA), :], tail_ref, tail_sem)
-
-    @pl.when(pl.program_id(0) == 0)
-    def _():
-        tail.start()
-        for q in range(pieces):
-            copy(q).start()
-        tail.wait()
-
-    step = pl.program_id(0)
-    copy(step).wait()
-    out_ref[:, :, width:] = o_ref[...]
-    state = jnp.zeros((piece, width), F32)
-    for r in range(blocks):
-        out_ref[r, :, :width] = state.astype(BF16)
-        if r + 1 < blocks:
-            ends = tail_ref[r].astype(F32)
-            state = state * (ends[0:1, :] + ends[1:2, :]) + held_ref[step, r].astype(F32)
-
-
-def final_kernel(y_ref, s_ref, ca_ref, keep_ref, z_ref, gain_ref, o_ref, attn_ref):
-    scale = dot(keep_ref[0], expand_heads(2))
+    loads = [
+        pltpu.make_async_copy(f_ref.at[:, pl.ds(q * piece, piece), :], held_ref.at[q], sems.at[q])
+        for q in range(pieces)
+    ]
+    stores = [
+        pltpu.make_async_copy(
+            state_ref.at[q], out_ref.at[:, pl.ds(q * piece, piece), pl.ds(0, width)], out_sems.at[q]
+        )
+        for q in range(pieces)
+    ]
+    tail.start()
+    for load in loads:
+        load.start()
+    tail.wait()
+    for q in range(pieces):
+        loads[q].wait()
+        state = jnp.zeros((piece, width), F32)
+        for r in range(blocks):
+            state_ref[q, r] = state.astype(BF16)
+            if r + 1 < blocks:
+                ends = tail_ref[r].astype(F32)
+                state = state * (ends[0:1, :] + ends[1:2, :]) + held_ref[q, r].astype(F32)
+        stores[q].start()
+    for store in stores:
+        store.wait()
+
+
+def final_kernel(y_ref, s_ref, ca_ref, keep_ref, z_ref, gain_ref, o_ref, attn_ref, scale_ref, carried_ref):
     half = WIDTH // 2
-    parts = []
+    scale_ref[...] = dot(keep_ref[0], expand_heads(2))
     for k in range(2):
-        parts.append(dot(ca_ref[...], s_ref[k, :, :half]))
+        carried_ref[:, k * half : (k + 1) * half] = dot(ca_ref[...], s_ref[k, :, :half])
         own = s_ref.shape[2] - half
         attn_ref[:, k * own : (k + 1) * own] = s_ref[k, :, half:]
-    carried = jnp.concatenate(parts, axis=1)
-    mixed = (y_ref[...] + scale * carried).astype(BF16).astype(F32)
-    gated = mixed * silu(z_ref[...].astype(F32))
-    mean = jnp.mean(gated * gated, axis=1, keepdims=True)
-    o_ref[...] = (gated * lax.rsqrt(mean + EPSILON) * gain_ref[...]).astype(BF16)
+    gain = gain_ref[...]
+    for lo in range(0, y_ref.shape[0], CHUNK):
+        at = slice(lo, lo + CHUNK)
+        mixed = (y_ref[at, :] + scale_ref[at, :] * carried_ref[at, :]).astype(BF16).astype(F32)
+        gated = mixed * silu(z_ref[at, :].astype(F32))
+        mean = jnp.mean(gated * gated, axis=1, keepdims=True)
+        o_ref[at, :] = (gated * lax.rsqrt(mean + EPSILON) * gain).astype(BF16)
 
 
 def pack_kernel(q_ref, k_ref, v_ref, out_ref):
@@ -222,8 +227,8 @@
         out_ref[d, :, width + QDIM :] = v_ref[:, at : at + QDIM]
 
 
-def attend_kernel(place_ref, lengths_ref, far_ref, o_ref, qkv_ref, sem, s_ref, m_ref, l_ref, acc_ref):
-    copy = pltpu.make_async_copy(far_ref, qkv_ref, sem)
+def attend_kernel(place_ref, lengths_ref, far_ref, out_ref, qkv_ref, o_ref, sems, s_ref, m_ref, l_ref, acc_ref):
+    copy = pltpu.make_async_copy(far_ref, qkv_ref, sems.at[0])
     copy.start()
     copy.wait()
     length = qkv_ref.shape[0]
@@ -297,6 +302,19 @@
         return outer
 
     lax.fori_loop(0, length // KEYS, one_tile, 0)
+    blocks, rows, out_width = out_ref.shape
+    sends = [
+        pltpu.make_async_copy(
+            o_ref.at[pl.ds(r * rows, rows), :],
+            out_ref.at[r, :, pl.ds(out_width - q_width, q_width)],
+            sems.at[1 + r],
+        )
+        for r in range(blocks)
+    ]
+    for send in sends:
+        send.start()
+    for send in sends:
+        send.wait()
 
 
 def work(microseconds):
@@ -401,10 +419,12 @@
     attended = call(
         attend_kernel,
         in_specs=[smem(), smem(), pl.BlockSpec(memory_space=pl.ANY)],
-        out_shape=jax.ShapeDtypeStruct((blocks * rows, o_width), BF16),
+        out_specs=pl.BlockSpec(memory_space=pl.ANY),
+        out_shape=jax.ShapeDtypeStruct((blocks, rows, half + o_width), BF16),
         scratch_shapes=[
             pltpu.VMEM((blocks * rows, o_width + 2 * QDIM), BF16),
-            pltpu.SemaphoreType.DMA,
+            pltpu.VMEM((blocks * rows, o_width), BF16),
+            pltpu.SemaphoreType.DMA((1 + blocks,)),
             pltpu.VMEM((blocks * rows // KEYS, tall, KEYS), F32),
             pltpu.VMEM((tall, 128), F32),
             pltpu.VMEM((tall, 128), F32),
@@ -415,22 +435,21 @@
     )(place, doc_lengths, qkv.reshape(blocks * rows, o_width + 2 * QDIM))
     own_states = call(
         scan_kernel,
-        grid=(STATE // PIECE,),
-        in_specs=[
-            pl.BlockSpec(memory_space=pl.ANY),
-            pl.BlockSpec((blocks, PIECE, o_width), lambda q: (0, q, 0)),
-        ],
-        out_specs=pl.BlockSpec((blocks, PIECE, half + o_width), lambda q: (0, q, 0)),
+        in_specs=[pl.BlockSpec(memory_space=pl.ANY)] * 2,
+        out_specs=pl.BlockSpec(memory_space=pl.ANY),
         out_shape=jax.ShapeDtypeStruct((blocks, STATE, half + o_width), BF16),
+        input_output_aliases={1: 0},
         scratch_shapes=[
             pltpu.VMEM((blocks, EXTRA, half), BF16),
             pltpu.VMEM((STATE // PIECE, blocks, PIECE, half), BF16),
+            pltpu.VMEM((STATE // PIECE, blocks, PIECE, half), BF16),
+            pltpu.SemaphoreType.DMA((STATE // PIECE,)),
             pltpu.SemaphoreType.DMA((STATE // PIECE,)),
             pltpu.SemaphoreType.DMA,
         ],
         name="scan",
         cost_estimate=work(4),
-    )(own_fresh, attended.reshape(blocks, rows, o_width))
+    )(own_fresh, attended)
     states = lax.all_to_all(own_states, "ctx", split_axis=0, concat_axis=0, tiled=True)
 
     mixer_out, attn_out = call(
@@ -445,6 +464,7 @@
             jax.ShapeDtypeStruct((rows, INNER), BF16),
             jax.ShapeDtypeStruct((rows, QHEADS * QDIM), BF16),
         ],
+        scratch_shapes=[pltpu.VMEM((rows, WIDTH), F32), pltpu.VMEM((rows, WIDTH), F32)],
         name="final",
         cost_estimate=work(7),
     )(local, states, c_act, keep, z_gate[0], norm_gain[None])

time: 135 us -> 133 us (0.985)
  Pallas kernels: 58.2 us -> 55.8 us
    pallas_call x1, Pallas kernels: 5.54 us -> 3.01 us  [on_device(): call(scan_kernel, in_specs=[pl.BlockSpec(memory_space=pl.ANY)] * 2, out_s...]
where the time goes in v4:
time: 133 us; the launch traced here: 131 us
  Pallas kernels  55.8 us (42%)
  blocking collectives  40.3 us (30%)
  starting transfers between devices  16.9 us (13%)
  waiting for transfers between devices  15.5 us (12%)
  local copies, waits for them, and re-layouts  1.72 us (1%)
    all_to_all x1, blocking collectives, on_device(): lax.all_to_all(own_states, 'ctx', split_axis=0, concat_axis=0, tiled=True)  40.3 us
    pallas_call x1, Pallas kernels, on_device(): call(attend_kernel, in_specs=[smem(), smem(), pl.BlockSpec(memory_space=p...  20.2 us
    pallas_call x1, Pallas kernels, on_device(): call(front_kernel, grid=(GROUPS,), in_specs=[smem(), smem(), wide(rows),...  10 us
    pallas_call x1, Pallas kernels, on_device(): call(final_kernel, grid=(GROUPS,), in_specs=[wide(rows), pl.BlockSpec((2,...  8.8 us
    all_to_all x1, starting transfers between devices, on_device(): qkv = lax.all_to_all(qkv, 'ctx', split_axis=0, concat_axis=0, tiled=True)  8.49 us
    pallas_call x1, Pallas kernels, on_device(): call(inner_kernel, grid=(GROUPS,), in_specs=[smem(), smem(), wide(rows),...  8.46 us
    all_to_all x1, waiting for transfers between devices, on_device(): lax.all_to_all(fresh, 'ctx', split_axis=0, concat_axis=0, tiled=True)  8.37 us
    all_to_all x1, waiting for transfers between devices, on_device(): qkv = lax.all_to_all(qkv, 'ctx', split_axis=0, concat_axis=0, tiled=True)  6.6 us
  transfers between devices with their start and end apart: 3, of which 3 were waited for; matrix products, arithmetic and copies ran while one was open for 1% of the time, Pallas kernels for 33%

profile of v4, /device:TPU:0, one launch (start us, length us, event | category | flops | bytes accessed | tf_op | source)
XLA Modules:
  0.0 131.5 jit_solution(10401580438151179294)
XLA Ops:
  0.6 0.9 slice_bitcast_fusion
  1.6 3.9 %collective-permute-start = (bf16[8,10240]{1,0:T(8,128)(2,1)S(1)}, bf16[8,10240]{1,0:T(8,128)(2,1)S(1)}, u32[]{:S(2)}, u32[]{:S(2)}) collective-permute-start(bf16[8,10240]{1,0:T(8,128)(2,1)S(1)} %slice_bitcast_fusion), channel_id=1, source_target_pairs={{0,8},{8,16},{16,24},{24,32},{32,40},{40,48},{48,56},{56,64},{64,7... | collective-permute-start | bytes 491528 | tf_op jit(solution)/shard_map/ppermute | solution.py:347
  5.5 2.9 %pack.1 = bf16[16,128,512]{2,1,0:T(8,128)(2,1)} custom-call(bf16[128,4096]{1,0:T(8,128)(2,1)} %bitcast.20, bf16[128,1024]{1,0:T(8,128)(2,1)} %bitcast.24, bf16[128,1024]{1,0:T(8,128)(2,1)} %bitcast.25), custom_call_target="tpu_custom_call" | custom-call | bytes 10500000 | tf_op jit(solution)/shard_map/pack/pallas_call | solution.py:341
  8.4 0.0 copy-start.1
  8.4 0.5 collective-permute-done.hx_ref.hb_ref.hc_ref
  8.9 0.0 copy-start
  8.9 8.5 %all-to-all-start = ((bf16[16,128,512]{2,1,0:T(8,128)(2,1)}), bf16[16,128,512]{2,1,0:T(8,128)(2,1)}, u32[]{:S(2)}, u32[]{:S(2)}) async-start(bf16[16,128,512]{2,1,0:T(8,128)(2,1)} %pack.1), calls=%async_computation | async-start | bytes 4194304 | tf_op jit(solution)/shard_map/all_to_all | solution.py:349
  17.4 0.0 copy-done.1
  17.4 0.1 broadcast_in_dim.20
  17.5 0.7 broadcast_in_dim_reshape.3.skip_ref
  18.2 0.6 pad_add_fusion.place_ref
  18.8 2.4 %prep.1 = (f32[8,128,16]{2,1,0:T(8,128)}, f32[128,128]{1,0:T(8,128)}, bf16[8,128,32]{2,1,0:T(8,128)(2,1)}, bf16[8,128,32]{2,1,0:T(8,128)(2,1)}, bf16[8,8,16]{2,1,0:T(8,128)(2,1)}) custom-call(s32[2]{0:T(128)} %pad_add_fusion.place_ref, s32[8,6]{1,0:T(8,128)} %lengths_ref.7, bf16[128,128]{1,0:T(8,128)(2,1)} %bitcast.27, f32[1,128]{1,0:T(1,128)} %bitcast.28), custom_call_target="tpu_custom_call" | custom-call | bytes 10500000 | tf_op jit(solution)/shard_map/prep/pallas_call | solution.py:351
  21.3 0.0 copy-done
  21.3 10.0 %front.1 = (bf16[128,8192]{1,0:T(8,128)(2,1)}, bf16[128,1024]{1,0:T(8,128)(2,1)}, bf16[128,1024]{1,0:T(8,128)(2,1)}, bf16[16,136,512]{2,1,0:T(8,128)(2,1)}) custom-call(s32[2]{0:T(128)} %pad_add_fusion.place_ref, s32[8,6]{1,0:T(8,128)} %lengths_ref.7, bf16[128,10240]{1,0:T(8,128)(2,1)} %bitcast.16, bf16[128,10240]{1,0:T(8,128)(2,1)} %bitcast.17, ...), custom_call_target="tpu_custom_call" | custom-call | bytes 140000000 | tf_op jit(solution)/shard_map/front/pallas_call | solution.py:373
  31.3 8.5 %inner.1.y_ref = f32[128,8192]{1,0:T(8,128)} custom-call(s32[2]{0:T(128)} %pad_add_fusion.place_ref, s32[8,6]{1,0:T(8,128)} %lengths_ref.7, bf16[128,8192]{1,0:T(8,128)(2,1)} %get-tuple-element.23.xa_ref, bf16[128,1024]{1,0:T(8,128)(2,1)} %get-tuple-element.24.ba_ref, bf16[128,1024]{1,0:T(8,128)(2,1)} %get-tuple-element.25.ca_ref, ...), custom_call_target="tpu_custom_call" | custom-call | bytes 31500000 | tf_op jit(solution)/shard_map/inner/pallas_call | solution.py:402
  39.8 6.6 %all-to-all-done = bf16[16,128,512]{2,1,0:T(8,128)(2,1)} async-done(((bf16[16,128,512]{2,1,0:T(8,128)(2,1)}), bf16[16,128,512]{2,1,0:T(8,128)(2,1)}, u32[]{:S(2)}, u32[]{:S(2)}) %all-to-all-start) | async-done | bytes 2097184 | tf_op jit(solution)/shard_map/all_to_all | solution.py:349
  46.3 4.5 %all-to-all-start.1 = ((bf16[16,136,512]{2,1,0:T(8,128)(2,1)}), bf16[16,136,512]{2,1,0:T(8,128)(2,1)}, u32[]{:S(2)}, u32[]{:S(2)}) async-start(bf16[16,136,512]{2,1,0:T(8,128)(2,1)} %get-tuple-element.29), calls=%async_computation.1 | async-start | bytes 4456448 | tf_op jit(solution)/shard_map/all_to_all | solution.py:416
  50.8 20.2 %attend.1.held_out_ref = bf16[16,128,768]{2,1,0:T(8,128)(2,1)} custom-call(s32[2]{0:T(128)} %pad_add_fusion.place_ref, s32[8,6]{1,0:T(8,128)} %lengths_ref.7, bf16[2048,512]{1,0:T(8,128)(2,1)} %bitcast.10.far_ref), custom_call_target="tpu_custom_call" | custom-call | bytes 105000000 | tf_op jit(solution)/shard_map/attend/pallas_call | solution.py:419
  71.0 8.4 %all-to-all-done.1.f_ref = bf16[16,136,512]{2,1,0:T(8,128)(2,1)} async-done(((bf16[16,136,512]{2,1,0:T(8,128)(2,1)}), bf16[16,136,512]{2,1,0:T(8,128)(2,1)}, u32[]{:S(2)}, u32[]{:S(2)}) %all-to-all-start.1) | async-done | bytes 2228256 | tf_op jit(solution)/shard_map/all_to_all | solution.py:416
  79.4 3.0 %scan.1 = bf16[16,128,768]{2,1,0:T(8,128)(2,1)} custom-call(bf16[16,136,512]{2,1,0:T(8,128)(2,1)} %all-to-all-done.1.f_ref, bf16[16,128,768]{2,1,0:T(8,128)(2,1)} %attend.1.held_out_ref), custom_call_target="tpu_custom_call", output_to_operand_aliasing={{}: (1, {})} | custom-call | bytes 14000000 | tf_op jit(solution)/shard_map/scan/pallas_call | solution.py:436
  82.4 40.3 %all_to_all.15.s_ref = bf16[16,128,768]{2,1,0:T(8,128)(2,1)} all-to-all(bf16[16,128,768]{2,1,0:T(8,128)(2,1)} %scan.1), channel_id=1, replica_groups=mesh['ctx'=16,'batch'=8] {'ctx'}, dimensions={0} | all-to-all | bytes 6291456 | tf_op jit(solution)/shard_map/all_to_all | solution.py:453
  122.7 8.8 %final.1 = (bf16[128,8192]{1,0:T(8,128)(2,1)}, bf16[128,4096]{1,0:T(8,128)(2,1)}) custom-call(f32[128,8192]{1,0:T(8,128)} %inner.1.y_ref, bf16[16,128,768]{2,1,0:T(8,128)(2,1)} %all_to_all.15.s_ref, bf16[128,1024]{1,0:T(8,128)(2,1)} %get-tuple-element.25.ca_ref, bf16[8,128,32]{2,1,0:T(8,128)(2,1)} %get-tuple-element.31.keep_ref, bf16[128,8192]{1,0:T(8,128)(2,1)} %bitcast.19, ...), custom_call_target="tpu_custom_call" | custom-call | bytes 24500000 | tf_op jit(solution)/shard_map/final/pallas_call | solution.py:455
Async XLA Ops:
  1.6 7.4 %collective-permute-start = (bf16[8,10240]{1,0:T(8,128)(2,1)S(1)}, bf16[8,10240]{1,0:T(8,128)(2,1)S(1)}, u32[]{:S(2)}, u32[]{:S(2)}) collective-permute-start(bf16[8,10240]{1,0:T(8,128)(2,1)S(1)} %slice_bitcast_fusion), channel_id=1, source_target_pairs={{0,8},{8,16},{16,24},{24,32},{32,40},{40,48},{48,56},{56,64},{64,7... | collective-permute-start | bytes 491528 | tf_op jit(solution)/shard_map/ppermute | solution.py:347
  8.4 9.0 %copy-start.1 = (f32[128]{0:T(128)S(1)}, f32[128]{0:T(128)}, u32[]{:S(2)}) copy-start(f32[128]{0:T(128)} %param.18) | copy-start | bytes 1540
  8.9 12.3 %copy-start = (bf16[8,10240]{1,0:T(8,128)(2,1)}, bf16[8,10240]{1,0:T(8,128)(2,1)S(1)}, u32[]{:S(2)}) copy-start(bf16[8,10240]{1,0:T(8,128)(2,1)S(1)} %collective-permute-done.hx_ref.hb_ref.hc_ref) | copy-start | bytes 491524
  8.9 37.4 %all-to-all-start = ((bf16[16,128,512]{2,1,0:T(8,128)(2,1)}), bf16[16,128,512]{2,1,0:T(8,128)(2,1)}, u32[]{:S(2)}, u32[]{:S(2)}) async-start(bf16[16,128,512]{2,1,0:T(8,128)(2,1)} %pack.1), calls=%async_computation | async-start | bytes 4194304 | tf_op jit(solution)/shard_map/all_to_all | solution.py:349
  46.3 33.0 %all-to-all-start.1 = ((bf16[16,136,512]{2,1,0:T(8,128)(2,1)}), bf16[16,136,512]{2,1,0:T(8,128)(2,1)}, u32[]{:S(2)}, u32[]{:S(2)}) async-start(bf16[16,136,512]{2,1,0:T(8,128)(2,1)} %get-tuple-element.29), calls=%async_computation.1 | async-start | bytes 4456448 | tf_op jit(solution)/shard_map/all_to_all | solution.py:416

commit v5 on v4

--- a/solution.py
+++ b/solution.py
@@ -201,30 +201,62 @@
         store.wait()
 
 
-def final_kernel(y_ref, s_ref, ca_ref, keep_ref, z_ref, gain_ref, o_ref, attn_ref, scale_ref, carried_ref):
+def final_kernel(
+    y_far, s_far, z_far, ca_ref, keep_ref, gain_ref, o_ref, attn_ref,
+    y_ref, s_ref, z_ref, scale_ref, carried_ref, sems,
+):
     half = WIDTH // 2
-    scale_ref[...] = dot(keep_ref[0], expand_heads(2))
+
+    def copies(g):
+        cols = pl.ds(pl.multiple_of(g * WIDTH, WIDTH), WIDTH)
+        return (
+            pltpu.make_async_copy(s_far.at[pl.ds(2 * g, 2)], s_ref.at[g], sems.at[0, g]),
+            pltpu.make_async_copy(y_far.at[:, cols], y_ref.at[g], sems.at[1, g]),
+            pltpu.make_async_copy(z_far.at[:, cols], z_ref.at[g], sems.at[2, g]),
+        )
+
+    @pl.when(pl.program_id(0) == 0)
+    def _():
+        for group in range(GROUPS):
+            for copy in copies(group):
+                copy.start()
+
+    g = pl.program_id(0)
+    scale_ref[...] = dot(keep_ref[g], expand_heads(2))
+    state_copy, y_copy, z_copy = copies(g)
+    state_copy.wait()
+    ca = ca_ref[:, pl.ds(pl.multiple_of(g * STATE, STATE), STATE)]
     for k in range(2):
-        carried_ref[:, k * half : (k + 1) * half] = dot(ca_ref[...], s_ref[k, :, :half])
-        own = s_ref.shape[2] - half
-        attn_ref[:, k * own : (k + 1) * own] = s_ref[k, :, half:]
-    gain = gain_ref[...]
-    for lo in range(0, y_ref.shape[0], CHUNK):
+        carried_ref[:, k * half : (k + 1) * half] = dot(ca, s_ref[g, k, :, :half])
+        own = s_ref.shape[3] - half
+        attn_ref[:, k * own : (k + 1) * own] = s_ref[g, k, :, half:]
+    y_copy.wait()
+    z_copy.wait()
+    gain = gain_ref[:, pl.ds(pl.multiple_of(g * WIDTH, WIDTH), WIDTH)]
+    for lo in range(0, y_far.shape[0], CHUNK):
         at = slice(lo, lo + CHUNK)
-        mixed = (y_ref[at, :] + scale_ref[at, :] * carried_ref[at, :]).astype(BF16).astype(F32)
-        gated = mixed * silu(z_ref[at, :].astype(F32))
+        mixed = (y_ref[g, at, :] + scale_ref[at, :] * carried_ref[at, :]).astype(BF16).astype(F32)
+        gated = mixed * silu(z_ref[g, at, :].astype(F32))
         mean = jnp.mean(gated * gated, axis=1, keepdims=True)
         o_ref[at, :] = (gated * lax.rsqrt(mean + EPSILON) * gain).astype(BF16)
 
 
-def pack_kernel(q_ref, k_ref, v_ref, out_ref):
+def pack_kernel(q_ref, k_ref, v_ref, out_ref, sems):
     parts = out_ref.shape[0]
     width = q_ref.shape[1] // parts
+    copies = []
     for d in range(parts):
-        at = d * KVHEADS // parts * QDIM
-        out_ref[d, :, :width] = q_ref[:, d * width : (d + 1) * width]
-        out_ref[d, :, width : width + QDIM] = k_ref[:, at : at + QDIM]
-        out_ref[d, :, width + QDIM :] = v_ref[:, at : at + QDIM]
+        at = pl.ds(d * KVHEADS // parts * QDIM, QDIM)
+        q_cols = pl.ds(d * width, width)
+        copies += [
+            pltpu.make_async_copy(q_ref.at[:, q_cols], out_ref.at[d, :, pl.ds(0, width)], sems.at[0, d]),
+            pltpu.make_async_copy(k_ref.at[:, at], out_ref.at[d, :, pl.ds(width, QDIM)], sems.at[1, d]),
+            pltpu.make_async_copy(v_ref.at[:, at], out_ref.at[d, :, pl.ds(width + QDIM, QDIM)], sems.at[2, d]),
+        ]
+    for copy in copies:
+        copy.start()
+    for copy in copies:
+        copy.wait()
 
 
 def attend_kernel(place_ref, lengths_ref, far_ref, out_ref, qkv_ref, o_ref, sems, s_ref, m_ref, l_ref, acc_ref):
@@ -340,6 +372,9 @@
     o_width = QHEADS * QDIM // blocks
     qkv = call(
         pack_kernel,
+        in_specs=[pl.BlockSpec(memory_space=pl.ANY)] * 3,
+        out_specs=pl.BlockSpec(memory_space=pl.ANY),
+        scratch_shapes=[pltpu.SemaphoreType.DMA((3, blocks))],
         out_shape=jax.ShapeDtypeStruct((blocks, rows, o_width + 2 * QDIM), BF16),
         name="pack",
         cost_estimate=work(3),
@@ -455,19 +490,28 @@
     mixer_out, attn_out = call(
         final_kernel,
         grid=(GROUPS,),
-        in_specs=[
-            wide(rows), pl.BlockSpec((2, STATE, half + o_width), lambda g: (g, 0, 0)), group_cols(rows),
-            per_group_two, wide(rows), wide(1),
+        in_specs=[pl.BlockSpec(memory_space=pl.ANY)] * 3
+        + [
+            pl.BlockSpec((rows, GROUPS * STATE), lambda g: (0, 0)),
+            pl.BlockSpec((GROUPS, rows, 2 * PER_GROUP), lambda g: (0, 0, 0)),
+            pl.BlockSpec((1, INNER), lambda g: (0, 0)),
         ],
         out_specs=[wide(rows), pl.BlockSpec((rows, 2 * o_width), lambda g: (0, g))],
         out_shape=[
             jax.ShapeDtypeStruct((rows, INNER), BF16),
             jax.ShapeDtypeStruct((rows, QHEADS * QDIM), BF16),
         ],
-        scratch_shapes=[pltpu.VMEM((rows, WIDTH), F32), pltpu.VMEM((rows, WIDTH), F32)],
+        scratch_shapes=[
+            pltpu.VMEM((GROUPS, rows, WIDTH), F32),
+            pltpu.VMEM((GROUPS, 2, STATE, half + o_width), BF16),
+            pltpu.VMEM((GROUPS, rows, WIDTH), BF16),
+            pltpu.VMEM((rows, WIDTH), F32),
+            pltpu.VMEM((rows, WIDTH), F32),
+            pltpu.SemaphoreType.DMA((3, GROUPS)),
+        ],
         name="final",
         cost_estimate=work(7),
-    )(local, states, c_act, keep, z_gate[0], norm_gain[None])
+    )(local, states, z_gate[0], c_act, keep, norm_gain[None])
     return (mixer_out[None], attn_out[None])
 
 

time: 133 us -> 196 us (1.47)
  Pallas kernels: 55.8 us -> 115 us
  waiting for transfers between devices: 15.5 us -> 19 us
    pallas_call x2, Pallas kernels: 11.7 us -> 73.9 us  [the longest x1 65.1 us: on_device(): call(pack_kernel, in_specs=[pl.BlockSpec(memory_space=pl.ANY)] * 3, out_s...]
    all_to_all x1, waiting for transfers between devices: 8.37 us -> 11.5 us  [on_device(): lax.all_to_all(fresh, 'ctx', split_axis=0, concat_axis=0, tiled=True)]
    pallas_call x1, Pallas kernels: 20.2 us -> 17.4 us  [on_device(): call(attend_kernel, in_specs=[smem(), smem(), pl.BlockSpec(memory_space=p...]
  transfers between devices with their start and end apart: 3 -> 3, of which waited for: 3 -> 2; matrix products, arithmetic and copies ran while one was open for 1% -> 1% of each run, Pallas kernels for 33% -> 53%
where the time goes in v5:
time: 196 us; the launch traced here: 195 us
  Pallas kernels  115 us (59%)
  blocking collectives  41.6 us (21%)
  waiting for transfers between devices  19 us (10%)
  starting transfers between devices  15.8 us (8%)
    pallas_call x1, Pallas kernels, on_device(): call(pack_kernel, in_specs=[pl.BlockSpec(memory_space=pl.ANY)] * 3, out_s...  65.1 us
    all_to_all x1, blocking collectives, on_device(): lax.all_to_all(own_states, 'ctx', split_axis=0, concat_axis=0, tiled=True)  41.6 us
    pallas_call x1, Pallas kernels, on_device(): call(attend_kernel, in_specs=[smem(), smem(), pl.BlockSpec(memory_space=p...  17.4 us
    all_to_all x1, waiting for transfers between devices, on_device(): lax.all_to_all(fresh, 'ctx', split_axis=0, concat_axis=0, tiled=True)  11.5 us
    pallas_call x1, Pallas kernels, on_device(): call(front_kernel, grid=(GROUPS,), in_specs=[smem(), smem(), wide(rows),...  10 us
    pallas_call x1, Pallas kernels, on_device(): call(final_kernel, grid=(GROUPS,), in_specs=[pl.BlockSpec(memory_space=pl...  8.83 us
    pallas_call x1, Pallas kernels, on_device(): call(inner_kernel, grid=(GROUPS,), in_specs=[smem(), smem(), wide(rows),...  8.46 us
    all_to_all x1, waiting for transfers between devices, on_device(): qkv = lax.all_to_all(qkv, 'ctx', split_axis=0, concat_axis=0, tiled=True)  7.53 us
  transfers between devices with their start and end apart: 3, of which 2 were waited for; matrix products, arithmetic and copies ran while one was open for 1% of the time, Pallas kernels for 53%

profile of v5, /device:TPU:0, one launch (start us, length us, event | category | flops | bytes accessed | tf_op | source)
XLA Modules:
  0.0 194.8 jit_solution(3300581969634225526)
XLA Ops:
  0.6 0.9 slice_bitcast_fusion
  1.6 3.9 %collective-permute-start = (bf16[8,10240]{1,0:T(8,128)(2,1)S(1)}, bf16[8,10240]{1,0:T(8,128)(2,1)S(1)}, u32[]{:S(2)}, u32[]{:S(2)}) collective-permute-start(bf16[8,10240]{1,0:T(8,128)(2,1)S(1)} %slice_bitcast_fusion), channel_id=1, source_target_pairs={{0,8},{8,16},{16,24},{24,32},{32,40},{40,48},{48,56},{56,64},{64,7... | collective-permute-start | bytes 491528 | tf_op jit(solution)/shard_map/ppermute | solution.py:382
  5.5 65.1 %pack.1 = bf16[16,128,512]{2,1,0:T(8,128)(2,1)} custom-call(bf16[128,4096]{1,0:T(8,128)(2,1)} %bitcast.20, bf16[128,1024]{1,0:T(8,128)(2,1)} %bitcast.24, bf16[128,1024]{1,0:T(8,128)(2,1)} %bitcast.25), custom_call_target="tpu_custom_call" | custom-call | bytes 10500000 | tf_op jit(solution)/shard_map/pack/pallas_call | solution.py:373
  70.6 0.0 copy-start.1
  70.6 0.0 collective-permute-done.hx_ref.hb_ref.hc_ref
  70.6 0.0 copy-start
  70.6 7.5 %all-to-all-start = ((bf16[16,128,512]{2,1,0:T(8,128)(2,1)}), bf16[16,128,512]{2,1,0:T(8,128)(2,1)}, u32[]{:S(2)}, u32[]{:S(2)}) async-start(bf16[16,128,512]{2,1,0:T(8,128)(2,1)} %pack.1), calls=%async_computation | async-start | bytes 4194304 | tf_op jit(solution)/shard_map/all_to_all | solution.py:384
  78.1 0.0 copy-done.1
  78.1 0.1 broadcast_in_dim.20
  78.2 0.7 broadcast_in_dim_reshape.3.skip_ref
  78.9 0.6 pad_add_fusion.place_ref
  79.5 2.4 %prep.1 = (f32[8,128,16]{2,1,0:T(8,128)}, f32[128,128]{1,0:T(8,128)}, bf16[8,128,32]{2,1,0:T(8,128)(2,1)}, bf16[8,128,32]{2,1,0:T(8,128)(2,1)}, bf16[8,8,16]{2,1,0:T(8,128)(2,1)}) custom-call(s32[2]{0:T(128)} %pad_add_fusion.place_ref, s32[8,6]{1,0:T(8,128)} %lengths_ref.7, bf16[128,128]{1,0:T(8,128)(2,1)} %bitcast.27, f32[1,128]{1,0:T(1,128)} %bitcast.28), custom_call_target="tpu_custom_call" | custom-call | bytes 10500000 | tf_op jit(solution)/shard_map/prep/pallas_call | solution.py:386
  81.9 0.0 copy-done
  81.9 10.0 %front.1 = (bf16[128,8192]{1,0:T(8,128)(2,1)}, bf16[128,1024]{1,0:T(8,128)(2,1)}, bf16[128,1024]{1,0:T(8,128)(2,1)}, bf16[16,136,512]{2,1,0:T(8,128)(2,1)}) custom-call(s32[2]{0:T(128)} %pad_add_fusion.place_ref, s32[8,6]{1,0:T(8,128)} %lengths_ref.7, bf16[128,10240]{1,0:T(8,128)(2,1)} %bitcast.16, bf16[128,10240]{1,0:T(8,128)(2,1)} %bitcast.17, ...), custom_call_target="tpu_custom_call" | custom-call | bytes 140000000 | tf_op jit(solution)/shard_map/front/pallas_call | solution.py:408
  91.9 8.5 %inner.1.y_far = f32[128,8192]{1,0:T(8,128)} custom-call(s32[2]{0:T(128)} %pad_add_fusion.place_ref, s32[8,6]{1,0:T(8,128)} %lengths_ref.7, bf16[128,8192]{1,0:T(8,128)(2,1)} %get-tuple-element.23.xa_ref, bf16[128,1024]{1,0:T(8,128)(2,1)} %get-tuple-element.24.ba_ref, bf16[128,1024]{1,0:T(8,128)(2,1)} %get-tuple-element.25.ca_ref, ...), custom_call_target="tpu_custom_call" | custom-call | bytes 31500000 | tf_op jit(solution)/shard_map/inner/pallas_call | solution.py:437
  100.4 7.5 %all-to-all-done = bf16[16,128,512]{2,1,0:T(8,128)(2,1)} async-done(((bf16[16,128,512]{2,1,0:T(8,128)(2,1)}), bf16[16,128,512]{2,1,0:T(8,128)(2,1)}, u32[]{:S(2)}, u32[]{:S(2)}) %all-to-all-start) | async-done | bytes 2097184 | tf_op jit(solution)/shard_map/all_to_all | solution.py:384
  107.9 4.5 %all-to-all-start.1 = ((bf16[16,136,512]{2,1,0:T(8,128)(2,1)}), bf16[16,136,512]{2,1,0:T(8,128)(2,1)}, u32[]{:S(2)}, u32[]{:S(2)}) async-start(bf16[16,136,512]{2,1,0:T(8,128)(2,1)} %get-tuple-element.29), calls=%async_computation.1 | async-start | bytes 4456448 | tf_op jit(solution)/shard_map/all_to_all | solution.py:451
  112.4 17.4 %attend.1.held_out_ref = bf16[16,128,768]{2,1,0:T(8,128)(2,1)} custom-call(s32[2]{0:T(128)} %pad_add_fusion.place_ref, s32[8,6]{1,0:T(8,128)} %lengths_ref.7, bf16[2048,512]{1,0:T(8,128)(2,1)} %bitcast.10.far_ref), custom_call_target="tpu_custom_call" | custom-call | bytes 105000000 | tf_op jit(solution)/shard_map/attend/pallas_call | solution.py:454
  129.8 11.5 %all-to-all-done.1.f_ref = bf16[16,136,512]{2,1,0:T(8,128)(2,1)} async-done(((bf16[16,136,512]{2,1,0:T(8,128)(2,1)}), bf16[16,136,512]{2,1,0:T(8,128)(2,1)}, u32[]{:S(2)}, u32[]{:S(2)}) %all-to-all-start.1) | async-done | bytes 2228256 | tf_op jit(solution)/shard_map/all_to_all | solution.py:451
  141.3 3.0 %scan.1 = bf16[16,128,768]{2,1,0:T(8,128)(2,1)} custom-call(bf16[16,136,512]{2,1,0:T(8,128)(2,1)} %all-to-all-done.1.f_ref, bf16[16,128,768]{2,1,0:T(8,128)(2,1)} %attend.1.held_out_ref), custom_call_target="tpu_custom_call", output_to_operand_aliasing={{}: (1, {})} | custom-call | bytes 14000000 | tf_op jit(solution)/shard_map/scan/pallas_call | solution.py:471
  144.3 41.6 %all_to_all.15.s_far = bf16[16,128,768]{2,1,0:T(8,128)(2,1)} all-to-all(bf16[16,128,768]{2,1,0:T(8,128)(2,1)} %scan.1), channel_id=1, replica_groups=mesh['ctx'=16,'batch'=8] {'ctx'}, dimensions={0} | all-to-all | bytes 6291456 | tf_op jit(solution)/shard_map/all_to_all | solution.py:488
  185.9 8.8 %final.1 = (bf16[128,8192]{1,0:T(8,128)(2,1)}, bf16[128,4096]{1,0:T(8,128)(2,1)}) custom-call(f32[128,8192]{1,0:T(8,128)} %inner.1.y_far, bf16[16,128,768]{2,1,0:T(8,128)(2,1)} %all_to_all.15.s_far, bf16[128,8192]{1,0:T(8,128)(2,1)} %bitcast.19, bf16[128,1024]{1,0:T(8,128)(2,1)} %get-tuple-element.25.ca_ref, bf16[8,128,32]{2,1,0:T(8,128)(2,1)} %get-tuple-element.31.keep_ref, ...), custom_call_target="tpu_custom_call" | custom-call | bytes 24500000 | tf_op jit(solution)/shard_map/final/pallas_call | solution.py:490
Async XLA Ops:
  1.6 69.0 %collective-permute-start = (bf16[8,10240]{1,0:T(8,128)(2,1)S(1)}, bf16[8,10240]{1,0:T(8,128)(2,1)S(1)}, u32[]{:S(2)}, u32[]{:S(2)}) collective-permute-start(bf16[8,10240]{1,0:T(8,128)(2,1)S(1)} %slice_bitcast_fusion), channel_id=1, source_target_pairs={{0,8},{8,16},{16,24},{24,32},{32,40},{40,48},{48,56},{56,64},{64,7... | collective-permute-start | bytes 491528 | tf_op jit(solution)/shard_map/ppermute | solution.py:382
  70.6 7.5 %copy-start.1 = (f32[128]{0:T(128)S(1)}, f32[128]{0:T(128)}, u32[]{:S(2)}) copy-start(f32[128]{0:T(128)} %param.18) | copy-start | bytes 1540
  70.6 11.3 %copy-start = (bf16[8,10240]{1,0:T(8,128)(2,1)}, bf16[8,10240]{1,0:T(8,128)(2,1)S(1)}, u32[]{:S(2)}) copy-start(bf16[8,10240]{1,0:T(8,128)(2,1)S(1)} %collective-permute-done.hx_ref.hb_ref.hc_ref) | copy-start | bytes 491524
  70.6 37.4 %all-to-all-start = ((bf16[16,128,512]{2,1,0:T(8,128)(2,1)}), bf16[16,128,512]{2,1,0:T(8,128)(2,1)}, u32[]{:S(2)}, u32[]{:S(2)}) async-start(bf16[16,128,512]{2,1,0:T(8,128)(2,1)} %pack.1), calls=%async_computation | async-start | bytes 4194304 | tf_op jit(solution)/shard_map/all_to_all | solution.py:384
  107.9 33.4 %all-to-all-start.1 = ((bf16[16,136,512]{2,1,0:T(8,128)(2,1)}), bf16[16,136,512]{2,1,0:T(8,128)(2,1)}, u32[]{:S(2)}, u32[]{:S(2)}) async-start(bf16[16,136,512]{2,1,0:T(8,128)(2,1)} %get-tuple-element.29), calls=%async_computation.1 | async-start | bytes 4456448 | tf_op jit(solution)/shard_map/all_to_all | solution.py:451

commit v6 on v5

--- a/solution.py
+++ b/solution.py
@@ -167,7 +167,7 @@
             [jnp.where(lane < HEAD_DIM, x, zero), jnp.where(lane < HEAD_DIM, zero, x)], axis=0
         )
         y = dot(jnp.concatenate(weights, axis=1), both)
-        y_ref[:, at] = y + x.astype(F32) * skip_ref[:, at]
+        y_ref[:, at] = (y + x.astype(F32) * skip_ref[:, at]).astype(BF16)
 
 
 def scan_kernel(f_ref, held_out_ref, out_ref, tail_ref, held_ref, state_ref, sems, out_sems, tail_sem):
@@ -202,12 +202,13 @@
 
 
 def final_kernel(
-    y_far, s_far, z_far, ca_ref, keep_ref, gain_ref, o_ref, attn_ref,
-    y_ref, s_ref, z_ref, scale_ref, carried_ref, sems,
+    y_far, s_far, z_far, ca_ref, keep_ref, gain_ref, o_far, attn_far,
+    y_ref, s_ref, z_ref, o_ref, spread_ref, scale_ref, carried_ref, sems,
 ):
     half = WIDTH // 2
-
-    def copies(g):
+    own = s_ref.shape[3] - half
+
+    def loads(g):
         cols = pl.ds(pl.multiple_of(g * WIDTH, WIDTH), WIDTH)
         return (
             pltpu.make_async_copy(s_far.at[pl.ds(2 * g, 2)], s_ref.at[g], sems.at[0, g]),
@@ -215,48 +216,72 @@
             pltpu.make_async_copy(z_far.at[:, cols], z_ref.at[g], sems.at[2, g]),
         )
 
-    @pl.when(pl.program_id(0) == 0)
+    def stores(g):
+        cols = pl.ds(pl.multiple_of(g * WIDTH, WIDTH), WIDTH)
+        found = [pltpu.make_async_copy(o_ref.at[g], o_far.at[:, cols], sems.at[3, g])]
+        for k in range(2):
+            at = pl.ds(pl.multiple_of((2 * g + k) * own, own), own)
+            source = s_ref.at[g, k, :, pl.ds(half, own)]
+            found.append(pltpu.make_async_copy(source, attn_far.at[:, at], sems.at[4 + k, g]))
+        return found
+
+    g = pl.program_id(0)
+
+    @pl.when(g == 0)
     def _():
         for group in range(GROUPS):
-            for copy in copies(group):
+            for copy in loads(group):
                 copy.start()
-
-    g = pl.program_id(0)
-    scale_ref[...] = dot(keep_ref[g], expand_heads(2))
-    state_copy, y_copy, z_copy = copies(g)
+        spread_ref[...] = expand_heads(2)
+
+    scale_ref[...] = dot(keep_ref[g], spread_ref[...])
+    state_copy, y_copy, z_copy = loads(g)
+    mixer_store, *attn_stores = stores(g)
     state_copy.wait()
+    for copy in attn_stores:
+        copy.start()
     ca = ca_ref[:, pl.ds(pl.multiple_of(g * STATE, STATE), STATE)]
     for k in range(2):
         carried_ref[:, k * half : (k + 1) * half] = dot(ca, s_ref[g, k, :, :half])
-        own = s_ref.shape[3] - half
-        attn_ref[:, k * own : (k + 1) * own] = s_ref[g, k, :, half:]
     y_copy.wait()
     z_copy.wait()
     gain = gain_ref[:, pl.ds(pl.multiple_of(g * WIDTH, WIDTH), WIDTH)]
     for lo in range(0, y_far.shape[0], CHUNK):
         at = slice(lo, lo + CHUNK)
-        mixed = (y_ref[g, at, :] + scale_ref[at, :] * carried_ref[at, :]).astype(BF16).astype(F32)
+        mixed = (y_ref[g, at, :].astype(F32) + scale_ref[at, :] * carried_ref[at, :]).astype(BF16).astype(F32)
         gated = mixed * silu(z_ref[g, at, :].astype(F32))
         mean = jnp.mean(gated * gated, axis=1, keepdims=True)
-        o_ref[at, :] = (gated * lax.rsqrt(mean + EPSILON) * gain).astype(BF16)
-
-
-def pack_kernel(q_ref, k_ref, v_ref, out_ref, sems):
+        o_ref[g, at, :] = (gated * lax.rsqrt(mean + EPSILON) * gain).astype(BF16)
+    mixer_store.start()
+
+    @pl.when(g == GROUPS - 1)
+    def _():
+        for group in range(GROUPS):
+            for copy in stores(group):
+                copy.wait()
+
+
+def pack_kernel(q_ref, k_ref, v_ref, out_ref, held_ref, sems):
     parts = out_ref.shape[0]
     width = q_ref.shape[1] // parts
-    copies = []
+    loads, stores = [], []
     for d in range(parts):
         at = pl.ds(d * KVHEADS // parts * QDIM, QDIM)
         q_cols = pl.ds(d * width, width)
-        copies += [
-            pltpu.make_async_copy(q_ref.at[:, q_cols], out_ref.at[d, :, pl.ds(0, width)], sems.at[0, d]),
-            pltpu.make_async_copy(k_ref.at[:, at], out_ref.at[d, :, pl.ds(width, QDIM)], sems.at[1, d]),
-            pltpu.make_async_copy(v_ref.at[:, at], out_ref.at[d, :, pl.ds(width + QDIM, QDIM)], sems.at[2, d]),
+        loads += [
+            pltpu.make_async_copy(q_ref.at[:, q_cols], held_ref.at[d, :, pl.ds(0, width)], sems.at[0, d]),
+            pltpu.make_async_copy(k_ref.at[:, at], held_ref.at[d, :, pl.ds(width, QDIM)], sems.at[1, d]),
+            pltpu.make_async_copy(v_ref.at[:, at], held_ref.at[d, :, pl.ds(width + QDIM, QDIM)], sems.at[2, d]),
         ]
-    for copy in copies:
-        copy.start()
-    for copy in copies:
-        copy.wait()
+        stores.append(pltpu.make_async_copy(held_ref.at[d], out_ref.at[d], sems.at[3, d]))
+    for load in loads:
+        load.start()
+    for d in range(parts):
+        for load in loads[3 * d : 3 * d + 3]:
+            load.wait()
+        stores[d].start()
+    for store in stores:
+        store.wait()
 
 
 def attend_kernel(place_ref, lengths_ref, far_ref, out_ref, qkv_ref, o_ref, sems, s_ref, m_ref, l_ref, acc_ref):
@@ -374,7 +399,10 @@
         pack_kernel,
         in_specs=[pl.BlockSpec(memory_space=pl.ANY)] * 3,
         out_specs=pl.BlockSpec(memory_space=pl.ANY),
-        scratch_shapes=[pltpu.SemaphoreType.DMA((3, blocks))],
+        scratch_shapes=[
+            pltpu.VMEM((blocks, rows, o_width + 2 * QDIM), BF16),
+            pltpu.SemaphoreType.DMA((4, blocks)),
+        ],
         out_shape=jax.ShapeDtypeStruct((blocks, rows, o_width + 2 * QDIM), BF16),
         name="pack",
         cost_estimate=work(3),
@@ -442,7 +470,7 @@
             pl.BlockSpec((PER_GROUP, rows), lambda g: (g, 0)), wide(1),
         ],
         out_specs=wide(rows),
-        out_shape=jax.ShapeDtypeStruct((rows, INNER), F32),
+        out_shape=jax.ShapeDtypeStruct((rows, INNER), BF16),
         name="inner",
         cost_estimate=work(9),
     )(place, doc_lengths, x_act, b_act, c_act, col, row, jnp.repeat(skip_gain, HEAD_DIM)[None])
@@ -496,18 +524,20 @@
             pl.BlockSpec((GROUPS, rows, 2 * PER_GROUP), lambda g: (0, 0, 0)),
             pl.BlockSpec((1, INNER), lambda g: (0, 0)),
         ],
-        out_specs=[wide(rows), pl.BlockSpec((rows, 2 * o_width), lambda g: (0, g))],
+        out_specs=[pl.BlockSpec(memory_space=pl.ANY)] * 2,
         out_shape=[
             jax.ShapeDtypeStruct((rows, INNER), BF16),
             jax.ShapeDtypeStruct((rows, QHEADS * QDIM), BF16),
         ],
         scratch_shapes=[
-            pltpu.VMEM((GROUPS, rows, WIDTH), F32),
+            pltpu.VMEM((GROUPS, rows, WIDTH), BF16),
             pltpu.VMEM((GROUPS, 2, STATE, half + o_width), BF16),
             pltpu.VMEM((GROUPS, rows, WIDTH), BF16),
+            pltpu.VMEM((GROUPS, rows, WIDTH), BF16),
+            pltpu.VMEM((2 * PER_GROUP, WIDTH), BF16),
             pltpu.VMEM((rows, WIDTH), F32),
             pltpu.VMEM((rows, WIDTH), F32),
-            pltpu.SemaphoreType.DMA((3, GROUPS)),
+            pltpu.SemaphoreType.DMA((6, GROUPS)),
         ],
         name="final",
         cost_estimate=work(7),

time: 196 us -> 133 us (0.68)
  Pallas kernels: 115 us -> 53 us
    pallas_call x1, Pallas kernels: 65.1 us -> 2.87 us  [on_device(): call(pack_kernel, in_specs=[pl.BlockSpec(memory_space=pl.ANY)] * 3, out_s...]
  transfers between devices with their start and end apart: 3 -> 3, of which waited for: 2 -> 3; matrix products, arithmetic and copies ran while one was open for 1% -> 1% of each run, Pallas kernels for 53% -> 31%
where the time goes in v6:
time: 133 us; the launch traced here: 132 us
  Pallas kernels  53 us (40%)
  blocking collectives  40.2 us (30%)
  waiting for transfers between devices  18.7 us (14%)
  starting transfers between devices  16.9 us (13%)
  local copies, waits for them, and re-layouts  1.72 us (1%)
    all_to_all x1, blocking collectives, on_device(): lax.all_to_all(own_states, 'ctx', split_axis=0, concat_axis=0, tiled=True)  40.2 us
    pallas_call x1, Pallas kernels, on_device(): call(attend_kernel, in_specs=[smem(), smem(), pl.BlockSpec(memory_space=p...  17.3 us
    all_to_all x1, waiting for transfers between devices, on_device(): lax.all_to_all(fresh, 'ctx', split_axis=0, concat_axis=0, tiled=True)  11.2 us
    pallas_call x1, Pallas kernels, on_device(): call(front_kernel, grid=(GROUPS,), in_specs=[smem(), smem(), wide(rows),...  10 us
    pallas_call x1, Pallas kernels, on_device(): call(final_kernel, grid=(GROUPS,), in_specs=[pl.BlockSpec(memory_space=pl...  9.15 us
    all_to_all x1, starting transfers between devices, on_device(): qkv = lax.all_to_all(qkv, 'ctx', split_axis=0, concat_axis=0, tiled=True)  8.49 us
    pallas_call x1, Pallas kernels, on_device(): call(inner_kernel, grid=(GROUPS,), in_specs=[smem(), smem(), wide(rows),...  8.19 us
    all_to_all x1, waiting for transfers between devices, on_device(): qkv = lax.all_to_all(qkv, 'ctx', split_axis=0, concat_axis=0, tiled=True)  6.87 us
  transfers between devices with their start and end apart: 3, of which 3 were waited for; matrix products, arithmetic and copies ran while one was open for 1% of the time, Pallas kernels for 31%

profile of v6, /device:TPU:0, one launch (start us, length us, event | category | flops | bytes accessed | tf_op | source)
XLA Modules:
  0.0 131.8 jit_solution(3090354763393249258)
XLA Ops:
  0.6 0.9 slice_bitcast_fusion
  1.6 3.9 %collective-permute-start = (bf16[8,10240]{1,0:T(8,128)(2,1)S(1)}, bf16[8,10240]{1,0:T(8,128)(2,1)S(1)}, u32[]{:S(2)}, u32[]{:S(2)}) collective-permute-start(bf16[8,10240]{1,0:T(8,128)(2,1)S(1)} %slice_bitcast_fusion), channel_id=1, source_target_pairs={{0,8},{8,16},{16,24},{24,32},{32,40},{40,48},{48,56},{56,64},{64,7... | collective-permute-start | bytes 491528 | tf_op jit(solution)/shard_map/ppermute | solution.py:410
  5.5 2.9 %pack.1 = bf16[16,128,512]{2,1,0:T(8,128)(2,1)} custom-call(bf16[128,4096]{1,0:T(8,128)(2,1)} %bitcast.20, bf16[128,1024]{1,0:T(8,128)(2,1)} %bitcast.24, bf16[128,1024]{1,0:T(8,128)(2,1)} %bitcast.25), custom_call_target="tpu_custom_call" | custom-call | bytes 10500000 | tf_op jit(solution)/shard_map/pack/pallas_call | solution.py:398
  8.4 0.0 copy-start.1
  8.4 0.5 collective-permute-done.hx_ref.hb_ref.hc_ref
  8.9 0.0 copy-start
  8.9 8.5 %all-to-all-start = ((bf16[16,128,512]{2,1,0:T(8,128)(2,1)}), bf16[16,128,512]{2,1,0:T(8,128)(2,1)}, u32[]{:S(2)}, u32[]{:S(2)}) async-start(bf16[16,128,512]{2,1,0:T(8,128)(2,1)} %pack.1), calls=%async_computation | async-start | bytes 4194304 | tf_op jit(solution)/shard_map/all_to_all | solution.py:412
  17.4 0.0 copy-done.1
  17.4 0.1 broadcast_in_dim.20
  17.5 0.7 broadcast_in_dim_reshape.3.skip_ref
  18.2 0.6 pad_add_fusion.place_ref
  18.8 2.4 %prep.1 = (f32[8,128,16]{2,1,0:T(8,128)}, f32[128,128]{1,0:T(8,128)}, bf16[8,128,32]{2,1,0:T(8,128)(2,1)}, bf16[8,128,32]{2,1,0:T(8,128)(2,1)}, bf16[8,8,16]{2,1,0:T(8,128)(2,1)}) custom-call(s32[2]{0:T(128)} %pad_add_fusion.place_ref, s32[8,6]{1,0:T(8,128)} %lengths_ref.7, bf16[128,128]{1,0:T(8,128)(2,1)} %bitcast.27, f32[1,128]{1,0:T(1,128)} %bitcast.28), custom_call_target="tpu_custom_call" | custom-call | bytes 10500000 | tf_op jit(solution)/shard_map/prep/pallas_call | solution.py:414
  21.2 0.0 copy-done
  21.2 10.0 %front.1 = (bf16[128,8192]{1,0:T(8,128)(2,1)}, bf16[128,1024]{1,0:T(8,128)(2,1)}, bf16[128,1024]{1,0:T(8,128)(2,1)}, bf16[16,136,512]{2,1,0:T(8,128)(2,1)}) custom-call(s32[2]{0:T(128)} %pad_add_fusion.place_ref, s32[8,6]{1,0:T(8,128)} %lengths_ref.7, bf16[128,10240]{1,0:T(8,128)(2,1)} %bitcast.16, bf16[128,10240]{1,0:T(8,128)(2,1)} %bitcast.17, ...), custom_call_target="tpu_custom_call" | custom-call | bytes 140000000 | tf_op jit(solution)/shard_map/front/pallas_call | solution.py:436
  31.3 8.2 %inner.1.y_far = bf16[128,8192]{1,0:T(8,128)(2,1)} custom-call(s32[2]{0:T(128)} %pad_add_fusion.place_ref, s32[8,6]{1,0:T(8,128)} %lengths_ref.7, bf16[128,8192]{1,0:T(8,128)(2,1)} %get-tuple-element.23.xa_ref, bf16[128,1024]{1,0:T(8,128)(2,1)} %get-tuple-element.24.ba_ref, bf16[128,1024]{1,0:T(8,128)(2,1)} %get-tuple-element.25.ca_ref, ...), custom_call_target="tpu_custom_call" | custom-call | bytes 31500000 | tf_op jit(solution)/shard_map/inner/pallas_call | solution.py:465
  39.5 6.9 %all-to-all-done = bf16[16,128,512]{2,1,0:T(8,128)(2,1)} async-done(((bf16[16,128,512]{2,1,0:T(8,128)(2,1)}), bf16[16,128,512]{2,1,0:T(8,128)(2,1)}, u32[]{:S(2)}, u32[]{:S(2)}) %all-to-all-start) | async-done | bytes 2097184 | tf_op jit(solution)/shard_map/all_to_all | solution.py:412
  46.3 4.5 %all-to-all-start.1 = ((bf16[16,136,512]{2,1,0:T(8,128)(2,1)}), bf16[16,136,512]{2,1,0:T(8,128)(2,1)}, u32[]{:S(2)}, u32[]{:S(2)}) async-start(bf16[16,136,512]{2,1,0:T(8,128)(2,1)} %get-tuple-element.29), calls=%async_computation.1 | async-start | bytes 4456448 | tf_op jit(solution)/shard_map/all_to_all | solution.py:479
  50.8 17.3 %attend.1.held_out_ref = bf16[16,128,768]{2,1,0:T(8,128)(2,1)} custom-call(s32[2]{0:T(128)} %pad_add_fusion.place_ref, s32[8,6]{1,0:T(8,128)} %lengths_ref.7, bf16[2048,512]{1,0:T(8,128)(2,1)} %bitcast.10.far_ref), custom_call_target="tpu_custom_call" | custom-call | bytes 105000000 | tf_op jit(solution)/shard_map/attend/pallas_call | solution.py:482
  68.2 11.2 %all-to-all-done.1.f_ref = bf16[16,136,512]{2,1,0:T(8,128)(2,1)} async-done(((bf16[16,136,512]{2,1,0:T(8,128)(2,1)}), bf16[16,136,512]{2,1,0:T(8,128)(2,1)}, u32[]{:S(2)}, u32[]{:S(2)}) %all-to-all-start.1) | async-done | bytes 2228256 | tf_op jit(solution)/shard_map/all_to_all | solution.py:479
  79.4 3.0 %scan.1 = bf16[16,128,768]{2,1,0:T(8,128)(2,1)} custom-call(bf16[16,136,512]{2,1,0:T(8,128)(2,1)} %all-to-all-done.1.f_ref, bf16[16,128,768]{2,1,0:T(8,128)(2,1)} %attend.1.held_out_ref), custom_call_target="tpu_custom_call", output_to_operand_aliasing={{}: (1, {})} | custom-call | bytes 14000000 | tf_op jit(solution)/shard_map/scan/pallas_call | solution.py:499
  82.5 40.2 %all_to_all.15.s_far = bf16[16,128,768]{2,1,0:T(8,128)(2,1)} all-to-all(bf16[16,128,768]{2,1,0:T(8,128)(2,1)} %scan.1), channel_id=1, replica_groups=mesh['ctx'=16,'batch'=8] {'ctx'}, dimensions={0} | all-to-all | bytes 6291456 | tf_op jit(solution)/shard_map/all_to_all | solution.py:516
  122.7 9.1 %final.1 = (bf16[128,8192]{1,0:T(8,128)(2,1)}, bf16[128,4096]{1,0:T(8,128)(2,1)}) custom-call(bf16[128,8192]{1,0:T(8,128)(2,1)} %inner.1.y_far, bf16[16,128,768]{2,1,0:T(8,128)(2,1)} %all_to_all.15.s_far, bf16[128,8192]{1,0:T(8,128)(2,1)} %bitcast.19, bf16[128,1024]{1,0:T(8,128)(2,1)} %get-tuple-element.25.ca_ref, ...), custom_call_target="tpu_custom_call" | custom-call | bytes 24500000 | tf_op jit(solution)/shard_map/final/pallas_call | solution.py:518
Async XLA Ops:
  1.6 7.4 %collective-permute-start = (bf16[8,10240]{1,0:T(8,128)(2,1)S(1)}, bf16[8,10240]{1,0:T(8,128)(2,1)S(1)}, u32[]{:S(2)}, u32[]{:S(2)}) collective-permute-start(bf16[8,10240]{1,0:T(8,128)(2,1)S(1)} %slice_bitcast_fusion), channel_id=1, source_target_pairs={{0,8},{8,16},{16,24},{24,32},{32,40},{40,48},{48,56},{56,64},{64,7... | collective-permute-start | bytes 491528 | tf_op jit(solution)/shard_map/ppermute | solution.py:410
  8.4 9.1 %copy-start.1 = (f32[128]{0:T(128)S(1)}, f32[128]{0:T(128)}, u32[]{:S(2)}) copy-start(f32[128]{0:T(128)} %param.18) | copy-start | bytes 1540
  8.9 12.3 %copy-start = (bf16[8,10240]{1,0:T(8,128)(2,1)}, bf16[8,10240]{1,0:T(8,128)(2,1)S(1)}, u32[]{:S(2)}) copy-start(bf16[8,10240]{1,0:T(8,128)(2,1)S(1)} %collective-permute-done.hx_ref.hb_ref.hc_ref) | copy-start | bytes 491524
  8.9 37.4 %all-to-all-start = ((bf16[16,128,512]{2,1,0:T(8,128)(2,1)}), bf16[16,128,512]{2,1,0:T(8,128)(2,1)}, u32[]{:S(2)}, u32[]{:S(2)}) async-start(bf16[16,128,512]{2,1,0:T(8,128)(2,1)} %pack.1), calls=%async_computation | async-start | bytes 4194304 | tf_op jit(solution)/shard_map/all_to_all | solution.py:412
  46.3 33.1 %all-to-all-start.1 = ((bf16[16,136,512]{2,1,0:T(8,128)(2,1)}), bf16[16,136,512]{2,1,0:T(8,128)(2,1)}, u32[]{:S(2)}, u32[]{:S(2)}) async-start(bf16[16,136,512]{2,1,0:T(8,128)(2,1)} %get-tuple-element.29), calls=%async_computation.1 | async-start | bytes 4456448 | tf_op jit(solution)/shard_map/all_to_all | solution.py:479

commit v7 on v6

--- a/solution.py
+++ b/solution.py
@@ -202,63 +202,77 @@
 
 
 def final_kernel(
-    y_far, s_far, z_far, ca_ref, keep_ref, gain_ref, o_far, attn_far,
-    y_ref, s_ref, z_ref, o_ref, spread_ref, scale_ref, carried_ref, sems,
+    y_far, s_far, z_far, ca_far, keep_far, gain_far, o_far, attn_far,
+    y_ref, s_ref, z_ref, o_ref, ca_ref, keep_ref, gain_ref, scale_ref, even_ref, odd_ref, square_ref, sems,
 ):
+    rows = y_far.shape[0]
     half = WIDTH // 2
     own = s_ref.shape[3] - half
-
-    def loads(g):
-        cols = pl.ds(pl.multiple_of(g * WIDTH, WIDTH), WIDTH)
-        return (
+    small = (
+        pltpu.make_async_copy(keep_far, keep_ref, sems.at[6, 0]),
+        pltpu.make_async_copy(ca_far, ca_ref, sems.at[6, 1]),
+        pltpu.make_async_copy(gain_far, gain_ref, sems.at[6, 2]),
+    )
+    loads, stores = [], []
+    for g in range(GROUPS):
+        cols = pl.ds(g * WIDTH, WIDTH)
+        loads.append((
             pltpu.make_async_copy(s_far.at[pl.ds(2 * g, 2)], s_ref.at[g], sems.at[0, g]),
             pltpu.make_async_copy(y_far.at[:, cols], y_ref.at[g], sems.at[1, g]),
             pltpu.make_async_copy(z_far.at[:, cols], z_ref.at[g], sems.at[2, g]),
-        )
-
-    def stores(g):
-        cols = pl.ds(pl.multiple_of(g * WIDTH, WIDTH), WIDTH)
-        found = [pltpu.make_async_copy(o_ref.at[g], o_far.at[:, cols], sems.at[3, g])]
+        ))
+        stores.append([pltpu.make_async_copy(o_ref.at[g], o_far.at[:, cols], sems.at[3, g])])
         for k in range(2):
-            at = pl.ds(pl.multiple_of((2 * g + k) * own, own), own)
             source = s_ref.at[g, k, :, pl.ds(half, own)]
-            found.append(pltpu.make_async_copy(source, attn_far.at[:, at], sems.at[4 + k, g]))
-        return found
-
-    g = pl.program_id(0)
-
-    @pl.when(g == 0)
-    def _():
-        for group in range(GROUPS):
-            for copy in loads(group):
-                copy.start()
-        spread_ref[...] = expand_heads(2)
-
-    scale_ref[...] = dot(keep_ref[g], spread_ref[...])
-    state_copy, y_copy, z_copy = loads(g)
-    mixer_store, *attn_stores = stores(g)
-    state_copy.wait()
-    for copy in attn_stores:
+            target = attn_far.at[:, pl.ds((2 * g + k) * own, own)]
+            stores[g].append(pltpu.make_async_copy(source, target, sems.at[4 + k, g]))
+    for copy in small:
         copy.start()
-    ca = ca_ref[:, pl.ds(pl.multiple_of(g * STATE, STATE), STATE)]
-    for k in range(2):
-        carried_ref[:, k * half : (k + 1) * half] = dot(ca, s_ref[g, k, :, :half])
-    y_copy.wait()
-    z_copy.wait()
-    gain = gain_ref[:, pl.ds(pl.multiple_of(g * WIDTH, WIDTH), WIDTH)]
-    for lo in range(0, y_far.shape[0], CHUNK):
-        at = slice(lo, lo + CHUNK)
-        mixed = (y_ref[g, at, :].astype(F32) + scale_ref[at, :] * carried_ref[at, :]).astype(BF16).astype(F32)
-        gated = mixed * silu(z_ref[g, at, :].astype(F32))
-        mean = jnp.mean(gated * gated, axis=1, keepdims=True)
-        o_ref[g, at, :] = (gated * lax.rsqrt(mean + EPSILON) * gain).astype(BF16)
-    mixer_store.start()
-
-    @pl.when(g == GROUPS - 1)
-    def _():
-        for group in range(GROUPS):
-            for copy in stores(group):
-                copy.wait()
+    for group in loads:
+        for copy in group:
+            copy.start()
+    spread = expand_heads(2)
+    for copy in small:
+        copy.wait()
+    for g in range(GROUPS):
+        scale_ref[g] = dot(keep_ref[g], spread)
+
+    def carry(g, into_ref):
+        loads[g][0].wait()
+        for copy in stores[g][1:]:
+            copy.start()
+        ca = ca_ref[:, g * STATE : (g + 1) * STATE]
+        for k in range(2):
+            into_ref[:, k * half : (k + 1) * half] = dot(ca, s_ref[g, k, :, :half])
+
+    carry(0, even_ref)
+    for g in range(GROUPS):
+        here_ref, next_ref = (even_ref, odd_ref) if g % 2 == 0 else (odd_ref, even_ref)
+        if g + 1 < GROUPS:
+            carry(g + 1, next_ref)
+        for copy in loads[g][1:]:
+            copy.wait()
+        for lo in range(0, rows, CHUNK):
+            at = slice(lo, lo + CHUNK)
+            mixed = (y_ref[g, at, :].astype(F32) + scale_ref[g, at, :] * here_ref[at, :]).astype(BF16).astype(F32)
+            gated = mixed * silu(z_ref[g, at, :].astype(F32))
+            here_ref[at, :] = gated
+            total = gated[:, :128] * gated[:, :128]
+            for c in range(128, WIDTH, 128):
+                total = total + gated[:, c : c + 128] * gated[:, c : c + 128]
+            square_ref[at, :] = total
+        mean = jnp.sum(square_ref[...], axis=1, keepdims=True) * (1.0 / WIDTH)
+        square_ref[...] = jnp.broadcast_to(lax.rsqrt(mean + EPSILON), square_ref.shape)
+        for lo in range(0, rows, CHUNK):
+            at = slice(lo, lo + CHUNK)
+            factor = square_ref[at, :]
+            for c in range(0, WIDTH, 128):
+                gain = gain_ref[:, g * WIDTH + c : g * WIDTH + c + 128]
+                o_ref[g, at, c : c + 128] = (here_ref[at, c : c + 128] * factor * gain).astype(BF16)
+        stores[g][0].start()
+    for group in stores:
+        for copy in group:
+            copy.wait()
 
 
 def pack_kernel(q_ref, k_ref, v_ref, out_ref, held_ref, sems):
@@ -517,13 +531,7 @@
 
     mixer_out, attn_out = call(
         final_kernel,
-        grid=(GROUPS,),
-        in_specs=[pl.BlockSpec(memory_space=pl.ANY)] * 3
-        + [
-            pl.BlockSpec((rows, GROUPS * STATE), lambda g: (0, 0)),
-            pl.BlockSpec((GROUPS, rows, 2 * PER_GROUP), lambda g: (0, 0, 0)),
-            pl.BlockSpec((1, INNER), lambda g: (0, 0)),
-        ],
+        in_specs=[pl.BlockSpec(memory_space=pl.ANY)] * 6,
         out_specs=[pl.BlockSpec(memory_space=pl.ANY)] * 2,
         out_shape=[
             jax.ShapeDtypeStruct((rows, INNER), BF16),
@@ -534,10 +542,14 @@
             pltpu.VMEM((GROUPS, 2, STATE, half + o_width), BF16),
             pltpu.VMEM((GROUPS, rows, WIDTH), BF16),
             pltpu.VMEM((GROUPS, rows, WIDTH), BF16),
-            pltpu.VMEM((2 * PER_GROUP, WIDTH), BF16),
+            pltpu.VMEM((rows, GROUPS * STATE), BF16),
+            pltpu.VMEM((GROUPS, rows, 2 * PER_GROUP), BF16),
+            pltpu.VMEM((1, INNER), F32),
+            pltpu.VMEM((GROUPS, rows, WIDTH), F32),
             pltpu.VMEM((rows, WIDTH), F32),
             pltpu.VMEM((rows, WIDTH), F32),
-            pltpu.SemaphoreType.DMA((6, GROUPS)),
+            pltpu.VMEM((rows, 128), F32),
+            pltpu.SemaphoreType.DMA((7, GROUPS)),
         ],
         name="final",
         cost_estimate=work(7),

time: 133 us -> 131 us (0.985)
  Pallas kernels: 53 us -> 51.1 us
    pallas_call x1, Pallas kernels: 9.15 us -> 7.23 us  [on_device(): call(final_kernel, in_specs=[pl.BlockSpec(memory_space=pl.ANY)] * 6, out_...]
where the time goes in v7:
time: 131 us; the launch traced here: 130 us
  Pallas kernels  51.1 us (39%)
  blocking collectives  40.2 us (31%)
  waiting for transfers between devices  18.7 us (14%)
  starting transfers between devices  16.9 us (13%)
  local copies, waits for them, and re-layouts  1.72 us (1%)
    all_to_all x1, blocking collectives, on_device(): lax.all_to_all(own_states, 'ctx', split_axis=0, concat_axis=0, tiled=True)  40.2 us
    pallas_call x1, Pallas kernels, on_device(): call(attend_kernel, in_specs=[smem(), smem(), pl.BlockSpec(memory_space=p...  17.3 us
    all_to_all x1, waiting for transfers between devices, on_device(): lax.all_to_all(fresh, 'ctx', split_axis=0, concat_axis=0, tiled=True)  11.2 us
    pallas_call x1, Pallas kernels, on_device(): call(front_kernel, grid=(GROUPS,), in_specs=[smem(), smem(), wide(rows),...  10 us
    all_to_all x1, starting transfers between devices, on_device(): qkv = lax.all_to_all(qkv, 'ctx', split_axis=0, concat_axis=0, tiled=True)  8.49 us
    pallas_call x1, Pallas kernels, on_device(): call(inner_kernel, grid=(GROUPS,), in_specs=[smem(), smem(), wide(rows),...  8.19 us
    pallas_call x1, Pallas kernels, on_device(): call(final_kernel, in_specs=[pl.BlockSpec(memory_space=pl.ANY)] * 6, out_...  7.23 us
    all_to_all x1, waiting for transfers between devices, on_device(): qkv = lax.all_to_all(qkv, 'ctx', split_axis=0, concat_axis=0, tiled=True)  6.87 us
  transfers between devices with their start and end apart: 3, of which 3 were waited for; matrix products, arithmetic and copies ran while one was open for 1% of the time, Pallas kernels for 31%

profile of v7, /device:TPU:0, one launch (start us, length us, event | category | flops | bytes accessed | tf_op | source)
XLA Modules:
  0.0 129.9 jit_solution(2135042420225260989)
XLA Ops:
  0.6 0.9 slice_bitcast_fusion
  1.6 3.9 %collective-permute-start = (bf16[8,10240]{1,0:T(8,128)(2,1)S(1)}, bf16[8,10240]{1,0:T(8,128)(2,1)S(1)}, u32[]{:S(2)}, u32[]{:S(2)}) collective-permute-start(bf16[8,10240]{1,0:T(8,128)(2,1)S(1)} %slice_bitcast_fusion), channel_id=1, source_target_pairs={{0,8},{8,16},{16,24},{24,32},{32,40},{40,48},{48,56},{56,64},{64,7... | collective-permute-start | bytes 491528 | tf_op jit(solution)/shard_map/ppermute | solution.py:424
  5.5 2.9 %pack.1 = bf16[16,128,512]{2,1,0:T(8,128)(2,1)} custom-call(bf16[128,4096]{1,0:T(8,128)(2,1)} %bitcast.20, bf16[128,1024]{1,0:T(8,128)(2,1)} %bitcast.24, bf16[128,1024]{1,0:T(8,128)(2,1)} %bitcast.25), custom_call_target="tpu_custom_call" | custom-call | bytes 10500000 | tf_op jit(solution)/shard_map/pack/pallas_call | solution.py:412
  8.4 0.0 copy-start.1
  8.4 0.5 collective-permute-done.hx_ref.hb_ref.hc_ref
  8.9 0.0 copy-start
  8.9 8.5 %all-to-all-start = ((bf16[16,128,512]{2,1,0:T(8,128)(2,1)}), bf16[16,128,512]{2,1,0:T(8,128)(2,1)}, u32[]{:S(2)}, u32[]{:S(2)}) async-start(bf16[16,128,512]{2,1,0:T(8,128)(2,1)} %pack.1), calls=%async_computation | async-start | bytes 4194304 | tf_op jit(solution)/shard_map/all_to_all | solution.py:426
  17.4 0.0 copy-done.1
  17.4 0.1 broadcast_in_dim.20
  17.5 0.7 broadcast_in_dim_reshape.3.skip_ref
  18.2 0.6 pad_add_fusion.place_ref
  18.8 2.4 %prep.1 = (f32[8,128,16]{2,1,0:T(8,128)}, f32[128,128]{1,0:T(8,128)}, bf16[8,128,32]{2,1,0:T(8,128)(2,1)}, bf16[8,128,32]{2,1,0:T(8,128)(2,1)}, bf16[8,8,16]{2,1,0:T(8,128)(2,1)}) custom-call(s32[2]{0:T(128)} %pad_add_fusion.place_ref, s32[8,6]{1,0:T(8,128)} %lengths_ref.7, bf16[128,128]{1,0:T(8,128)(2,1)} %bitcast.27, f32[1,128]{1,0:T(1,128)} %bitcast.28), custom_call_target="tpu_custom_call" | custom-call | bytes 10500000 | tf_op jit(solution)/shard_map/prep/pallas_call | solution.py:428
  21.2 0.0 copy-done
  21.2 10.0 %front.1 = (bf16[128,8192]{1,0:T(8,128)(2,1)}, bf16[128,1024]{1,0:T(8,128)(2,1)}, bf16[128,1024]{1,0:T(8,128)(2,1)}, bf16[16,136,512]{2,1,0:T(8,128)(2,1)}) custom-call(s32[2]{0:T(128)} %pad_add_fusion.place_ref, s32[8,6]{1,0:T(8,128)} %lengths_ref.7, bf16[128,10240]{1,0:T(8,128)(2,1)} %bitcast.16, bf16[128,10240]{1,0:T(8,128)(2,1)} %bitcast.17, ...), custom_call_target="tpu_custom_call" | custom-call | bytes 140000000 | tf_op jit(solution)/shard_map/front/pallas_call | solution.py:450
  31.3 8.2 %inner.1.y_far = bf16[128,8192]{1,0:T(8,128)(2,1)} custom-call(s32[2]{0:T(128)} %pad_add_fusion.place_ref, s32[8,6]{1,0:T(8,128)} %lengths_ref.7, bf16[128,8192]{1,0:T(8,128)(2,1)} %get-tuple-element.23.xa_ref, bf16[128,1024]{1,0:T(8,128)(2,1)} %get-tuple-element.24.ba_ref, bf16[128,1024]{1,0:T(8,128)(2,1)} %get-tuple-element.25.ca_ref.ca_far, ...), custom_call_target="tpu_custom_call" | custom-call | bytes 31500000 | tf_op jit(solution)/shard_map/inner/pallas_call | solution.py:479
  39.5 6.9 %all-to-all-done = bf16[16,128,512]{2,1,0:T(8,128)(2,1)} async-done(((bf16[16,128,512]{2,1,0:T(8,128)(2,1)}), bf16[16,128,512]{2,1,0:T(8,128)(2,1)}, u32[]{:S(2)}, u32[]{:S(2)}) %all-to-all-start) | async-done | bytes 2097184 | tf_op jit(solution)/shard_map/all_to_all | solution.py:426
  46.3 4.5 %all-to-all-start.1 = ((bf16[16,136,512]{2,1,0:T(8,128)(2,1)}), bf16[16,136,512]{2,1,0:T(8,128)(2,1)}, u32[]{:S(2)}, u32[]{:S(2)}) async-start(bf16[16,136,512]{2,1,0:T(8,128)(2,1)} %get-tuple-element.29), calls=%async_computation.1 | async-start | bytes 4456448 | tf_op jit(solution)/shard_map/all_to_all | solution.py:493
  50.8 17.3 %attend.1.held_out_ref = bf16[16,128,768]{2,1,0:T(8,128)(2,1)} custom-call(s32[2]{0:T(128)} %pad_add_fusion.place_ref, s32[8,6]{1,0:T(8,128)} %lengths_ref.7, bf16[2048,512]{1,0:T(8,128)(2,1)} %bitcast.10.far_ref), custom_call_target="tpu_custom_call" | custom-call | bytes 105000000 | tf_op jit(solution)/shard_map/attend/pallas_call | solution.py:496
  68.2 11.2 %all-to-all-done.1.f_ref = bf16[16,136,512]{2,1,0:T(8,128)(2,1)} async-done(((bf16[16,136,512]{2,1,0:T(8,128)(2,1)}), bf16[16,136,512]{2,1,0:T(8,128)(2,1)}, u32[]{:S(2)}, u32[]{:S(2)}) %all-to-all-start.1) | async-done | bytes 2228256 | tf_op jit(solution)/shard_map/all_to_all | solution.py:493
  79.4 3.0 %scan.1 = bf16[16,128,768]{2,1,0:T(8,128)(2,1)} custom-call(bf16[16,136,512]{2,1,0:T(8,128)(2,1)} %all-to-all-done.1.f_ref, bf16[16,128,768]{2,1,0:T(8,128)(2,1)} %attend.1.held_out_ref), custom_call_target="tpu_custom_call", output_to_operand_aliasing={{}: (1, {})} | custom-call | bytes 14000000 | tf_op jit(solution)/shard_map/scan/pallas_call | solution.py:513
  82.5 40.2 %all_to_all.15.s_far = bf16[16,128,768]{2,1,0:T(8,128)(2,1)} all-to-all(bf16[16,128,768]{2,1,0:T(8,128)(2,1)} %scan.1), channel_id=1, replica_groups=mesh['ctx'=16,'batch'=8] {'ctx'}, dimensions={0} | all-to-all | bytes 6291456 | tf_op jit(solution)/shard_map/all_to_all | solution.py:530
  122.7 7.2 %final.1 = (bf16[128,8192]{1,0:T(8,128)(2,1)}, bf16[128,4096]{1,0:T(8,128)(2,1)}) custom-call(bf16[128,8192]{1,0:T(8,128)(2,1)} %inner.1.y_far, bf16[16,128,768]{2,1,0:T(8,128)(2,1)} %all_to_all.15.s_far, bf16[128,8192]{1,0:T(8,128)(2,1)} %bitcast.19, bf16[128,1024]{1,0:T(8,128)(2,1)} %get-tuple-element.25.ca_ref.ca_far, ...), custom_call_target="tpu_custom_call" | custom-call | bytes 24500000 | tf_op jit(solution)/shard_map/final/pallas_call | solution.py:532
Async XLA Ops:
  1.6 7.4 %collective-permute-start = (bf16[8,10240]{1,0:T(8,128)(2,1)S(1)}, bf16[8,10240]{1,0:T(8,128)(2,1)S(1)}, u32[]{:S(2)}, u32[]{:S(2)}) collective-permute-start(bf16[8,10240]{1,0:T(8,128)(2,1)S(1)} %slice_bitcast_fusion), channel_id=1, source_target_pairs={{0,8},{8,16},{16,24},{24,32},{32,40},{40,48},{48,56},{56,64},{64,7... | collective-permute-start | bytes 491528 | tf_op jit(solution)/shard_map/ppermute | solution.py:424
  8.4 9.1 %copy-start.1 = (f32[128]{0:T(128)S(1)}, f32[128]{0:T(128)}, u32[]{:S(2)}) copy-start(f32[128]{0:T(128)} %param.18) | copy-start | bytes 1540
  8.9 12.3 %copy-start = (bf16[8,10240]{1,0:T(8,128)(2,1)}, bf16[8,10240]{1,0:T(8,128)(2,1)S(1)}, u32[]{:S(2)}) copy-start(bf16[8,10240]{1,0:T(8,128)(2,1)S(1)} %collective-permute-done.hx_ref.hb_ref.hc_ref) | copy-start | bytes 491524
  8.9 37.4 %all-to-all-start = ((bf16[16,128,512]{2,1,0:T(8,128)(2,1)}), bf16[16,128,512]{2,1,0:T(8,128)(2,1)}, u32[]{:S(2)}, u32[]{:S(2)}) async-start(bf16[16,128,512]{2,1,0:T(8,128)(2,1)} %pack.1), calls=%async_computation | async-start | bytes 4194304 | tf_op jit(solution)/shard_map/all_to_all | solution.py:426
  46.3 33.1 %all-to-all-start.1 = ((bf16[16,136,512]{2,1,0:T(8,128)(2,1)}), bf16[16,136,512]{2,1,0:T(8,128)(2,1)}, u32[]{:S(2)}, u32[]{:S(2)}) async-start(bf16[16,136,512]{2,1,0:T(8,128)(2,1)} %get-tuple-element.29), calls=%async_computation.1 | async-start | bytes 4456448 | tf_op jit(solution)/shard_map/all_to_all | solution.py:493

commit v8 on v7

--- a/solution.py
+++ b/solution.py
@@ -28,6 +28,7 @@
 KEYS = 256
 PIECE = 32
 CHUNK = 16
+RIM = 4
 
 F32 = jnp.float32
 BF16 = jnp.bfloat16
@@ -121,7 +122,7 @@
 
     def conv(src, rim, weight, bias, dst, lo):
         at = slice(lo, lo + 128)
-        pad_ref[0:8, :] = rim[:, at].astype(F32)
+        pad_ref[8 - RIM : 8, :] = rim[:, at].astype(F32)
         pad_ref[8 : 8 + rows, :] = src[:, at].astype(F32)
         acc = pad_ref[8 : 8 + rows, :] * weight[3:4, at] + bias[:, at]
         for d in range(1, CONV):
@@ -421,7 +422,7 @@
         name="pack",
         cost_estimate=work(3),
     )(queries[0], attn_keys[0], attn_values[0])
-    rim = lax.ppermute(raw[rows - 8 :], "ctx", [(r, r + 1) for r in range(blocks - 1)])
+    rim = lax.ppermute(raw[rows - RIM :], "ctx", [(r, r + 1) for r in range(blocks - 1)])
     rim, qkv = lax.optimization_barrier((rim, qkv))
     qkv = lax.all_to_all(qkv, "ctx", split_axis=0, concat_axis=0, tiled=True)
 
@@ -453,7 +454,7 @@
         in_specs=[
             smem(), smem(),
             wide(rows), b_cols(rows), c_cols(rows),
-            wide(8), b_cols(8), c_cols(8),
+            wide(RIM), b_cols(RIM), c_cols(RIM),
             wide(CONV), b_cols(CONV), c_cols(CONV),
             wide(1), b_cols(1), c_cols(1),
             per_group_two, pl.BlockSpec((1, 8, PER_GROUP), lambda g: (g, 0, 0)),

time: 131 us -> 132 us (level)
  blocking collectives: 40.2 us -> 41.6 us
    all_to_all x1, blocking collectives: 40.2 us -> 41.6 us  [on_device(): lax.all_to_all(own_states, 'ctx', split_axis=0, concat_axis=0, tiled=True)]
  transfers between devices with their start and end apart: 3 -> 3, of which waited for: 3 -> 2; matrix products, arithmetic and copies ran while one was open for 1% -> 1% of each run, Pallas kernels for 31% -> 31%
where the time goes in v8:
time: 132 us; the launch traced here: 131 us
  Pallas kernels  51 us (39%)
  blocking collectives  41.6 us (32%)
  waiting for transfers between devices  19.4 us (15%)
  starting transfers between devices  15.9 us (12%)
  local copies, waits for them, and re-layouts  1.77 us (1%)
    all_to_all x1, blocking collectives, on_device(): lax.all_to_all(own_states, 'ctx', split_axis=0, concat_axis=0, tiled=True)  41.6 us
    pallas_call x1, Pallas kernels, on_device(): call(attend_kernel, in_specs=[smem(), smem(), pl.BlockSpec(memory_space=p...  17.3 us
    all_to_all x1, waiting for transfers between devices, on_device(): lax.all_to_all(fresh, 'ctx', split_axis=0, concat_axis=0, tiled=True)  11.6 us
    pallas_call x1, Pallas kernels, on_device(): call(front_kernel, grid=(GROUPS,), in_specs=[smem(), smem(), wide(rows),...  9.94 us
    pallas_call x1, Pallas kernels, on_device(): call(inner_kernel, grid=(GROUPS,), in_specs=[smem(), smem(), wide(rows),...  8.19 us
    all_to_all x1, waiting for transfers between devices, on_device(): qkv = lax.all_to_all(qkv, 'ctx', split_axis=0, concat_axis=0, tiled=True)  7.82 us
    all_to_all x1, starting transfers between devices, on_device(): qkv = lax.all_to_all(qkv, 'ctx', split_axis=0, concat_axis=0, tiled=True)  7.53 us
    pallas_call x1, Pallas kernels, on_device(): call(final_kernel, in_specs=[pl.BlockSpec(memory_space=pl.ANY)] * 6, out_...  7.23 us
  transfers between devices with their start and end apart: 3, of which 2 were waited for; matrix products, arithmetic and copies ran while one was open for 1% of the time, Pallas kernels for 31%

profile of v8, /device:TPU:0, one launch (start us, length us, event | category | flops | bytes accessed | tf_op | source)
XLA Modules:
  0.0 131.0 jit_solution(15014005555226819426)
XLA Ops:
  0.6 1.0 slice_bitcast_fusion
  1.6 3.9 %collective-permute-start = (bf16[4,10240]{1,0:T(4,128)(2,1)S(1)}, bf16[4,10240]{1,0:T(4,128)(2,1)S(1)}, u32[]{:S(2)}, u32[]{:S(2)}) collective-permute-start(bf16[4,10240]{1,0:T(4,128)(2,1)S(1)} %slice_bitcast_fusion), channel_id=1, source_target_pairs={{0,8},{8,16},{16,24},{24,32},{32,40},{40,48},{48,56},{56,64},{64,7... | collective-permute-start | bytes 245768 | tf_op jit(solution)/shard_map/ppermute | solution.py:425
  5.5 2.9 %pack.1 = bf16[16,128,512]{2,1,0:T(8,128)(2,1)} custom-call(bf16[128,4096]{1,0:T(8,128)(2,1)} %bitcast.20, bf16[128,1024]{1,0:T(8,128)(2,1)} %bitcast.24, bf16[128,1024]{1,0:T(8,128)(2,1)} %bitcast.25), custom_call_target="tpu_custom_call" | custom-call | bytes 10500000 | tf_op jit(solution)/shard_map/pack/pallas_call | solution.py:413
  8.4 0.0 copy-start.1
  8.4 0.0 collective-permute-done.hx_ref.hb_ref.hc_ref
  8.4 0.0 copy-start
  8.4 7.5 %all-to-all-start = ((bf16[16,128,512]{2,1,0:T(8,128)(2,1)}), bf16[16,128,512]{2,1,0:T(8,128)(2,1)}, u32[]{:S(2)}, u32[]{:S(2)}) async-start(bf16[16,128,512]{2,1,0:T(8,128)(2,1)} %pack.1), calls=%async_computation | async-start | bytes 4194304 | tf_op jit(solution)/shard_map/all_to_all | solution.py:427
  16.0 0.0 copy-done.1
  16.0 0.1 broadcast_in_dim.20
  16.0 0.7 broadcast_in_dim_reshape.3.skip_ref
  16.8 0.6 pad_add_fusion.place_ref
  17.4 2.4 %prep.1 = (f32[8,128,16]{2,1,0:T(8,128)}, f32[128,128]{1,0:T(8,128)}, bf16[8,128,32]{2,1,0:T(8,128)(2,1)}, bf16[8,128,32]{2,1,0:T(8,128)(2,1)}, bf16[8,8,16]{2,1,0:T(8,128)(2,1)}) custom-call(s32[2]{0:T(128)} %pad_add_fusion.place_ref, s32[8,6]{1,0:T(8,128)} %lengths_ref.7, bf16[128,128]{1,0:T(8,128)(2,1)} %bitcast.27, f32[1,128]{1,0:T(1,128)} %bitcast.28), custom_call_target="tpu_custom_call" | custom-call | bytes 10500000 | tf_op jit(solution)/shard_map/prep/pallas_call | solution.py:429
  19.8 0.0 copy-done
  19.8 9.9 %front.1 = (bf16[128,8192]{1,0:T(8,128)(2,1)}, bf16[128,1024]{1,0:T(8,128)(2,1)}, bf16[128,1024]{1,0:T(8,128)(2,1)}, bf16[16,136,512]{2,1,0:T(8,128)(2,1)}) custom-call(s32[2]{0:T(128)} %pad_add_fusion.place_ref, s32[8,6]{1,0:T(8,128)} %lengths_ref.7, bf16[128,10240]{1,0:T(8,128)(2,1)} %bitcast.16, bf16[128,10240]{1,0:T(8,128)(2,1)} %bitcast.17, ...), custom_call_target="tpu_custom_call" | custom-call | bytes 140000000 | tf_op jit(solution)/shard_map/front/pallas_call | solution.py:451
  29.7 8.2 %inner.1.y_far = bf16[128,8192]{1,0:T(8,128)(2,1)} custom-call(s32[2]{0:T(128)} %pad_add_fusion.place_ref, s32[8,6]{1,0:T(8,128)} %lengths_ref.7, bf16[128,8192]{1,0:T(8,128)(2,1)} %get-tuple-element.23.xa_ref, bf16[128,1024]{1,0:T(8,128)(2,1)} %get-tuple-element.24.ba_ref, bf16[128,1024]{1,0:T(8,128)(2,1)} %get-tuple-element.25.ca_ref.ca_far, ...), custom_call_target="tpu_custom_call" | custom-call | bytes 31500000 | tf_op jit(solution)/shard_map/inner/pallas_call | solution.py:480
  37.9 7.8 %all-to-all-done = bf16[16,128,512]{2,1,0:T(8,128)(2,1)} async-done(((bf16[16,128,512]{2,1,0:T(8,128)(2,1)}), bf16[16,128,512]{2,1,0:T(8,128)(2,1)}, u32[]{:S(2)}, u32[]{:S(2)}) %all-to-all-start) | async-done | bytes 2097184 | tf_op jit(solution)/shard_map/all_to_all | solution.py:427
  45.7 4.5 %all-to-all-start.1 = ((bf16[16,136,512]{2,1,0:T(8,128)(2,1)}), bf16[16,136,512]{2,1,0:T(8,128)(2,1)}, u32[]{:S(2)}, u32[]{:S(2)}) async-start(bf16[16,136,512]{2,1,0:T(8,128)(2,1)} %get-tuple-element.29), calls=%async_computation.1 | async-start | bytes 4456448 | tf_op jit(solution)/shard_map/all_to_all | solution.py:494
  50.2 17.3 %attend.1.held_out_ref = bf16[16,128,768]{2,1,0:T(8,128)(2,1)} custom-call(s32[2]{0:T(128)} %pad_add_fusion.place_ref, s32[8,6]{1,0:T(8,128)} %lengths_ref.7, bf16[2048,512]{1,0:T(8,128)(2,1)} %bitcast.10.far_ref), custom_call_target="tpu_custom_call" | custom-call | bytes 105000000 | tf_op jit(solution)/shard_map/attend/pallas_call | solution.py:497
  67.6 11.6 %all-to-all-done.1.f_ref = bf16[16,136,512]{2,1,0:T(8,128)(2,1)} async-done(((bf16[16,136,512]{2,1,0:T(8,128)(2,1)}), bf16[16,136,512]{2,1,0:T(8,128)(2,1)}, u32[]{:S(2)}, u32[]{:S(2)}) %all-to-all-start.1) | async-done | bytes 2228256 | tf_op jit(solution)/shard_map/all_to_all | solution.py:494
  79.1 3.0 %scan.1 = bf16[16,128,768]{2,1,0:T(8,128)(2,1)} custom-call(bf16[16,136,512]{2,1,0:T(8,128)(2,1)} %all-to-all-done.1.f_ref, bf16[16,128,768]{2,1,0:T(8,128)(2,1)} %attend.1.held_out_ref), custom_call_target="tpu_custom_call", output_to_operand_aliasing={{}: (1, {})} | custom-call | bytes 14000000 | tf_op jit(solution)/shard_map/scan/pallas_call | solution.py:514
  82.2 41.6 %all_to_all.15.s_far = bf16[16,128,768]{2,1,0:T(8,128)(2,1)} all-to-all(bf16[16,128,768]{2,1,0:T(8,128)(2,1)} %scan.1), channel_id=1, replica_groups=mesh['ctx'=16,'batch'=8] {'ctx'}, dimensions={0} | all-to-all | bytes 6291456 | tf_op jit(solution)/shard_map/all_to_all | solution.py:531
  123.8 7.2 %final.1 = (bf16[128,8192]{1,0:T(8,128)(2,1)}, bf16[128,4096]{1,0:T(8,128)(2,1)}) custom-call(bf16[128,8192]{1,0:T(8,128)(2,1)} %inner.1.y_far, bf16[16,128,768]{2,1,0:T(8,128)(2,1)} %all_to_all.15.s_far, bf16[128,8192]{1,0:T(8,128)(2,1)} %bitcast.19, bf16[128,1024]{1,0:T(8,128)(2,1)} %get-tuple-element.25.ca_ref.ca_far, ...), custom_call_target="tpu_custom_call" | custom-call | bytes 24500000 | tf_op jit(solution)/shard_map/final/pallas_call | solution.py:533
Async XLA Ops:
  1.6 6.8 %collective-permute-start = (bf16[4,10240]{1,0:T(4,128)(2,1)S(1)}, bf16[4,10240]{1,0:T(4,128)(2,1)S(1)}, u32[]{:S(2)}, u32[]{:S(2)}) collective-permute-start(bf16[4,10240]{1,0:T(4,128)(2,1)S(1)} %slice_bitcast_fusion), channel_id=1, source_target_pairs={{0,8},{8,16},{16,24},{24,32},{32,40},{40,48},{48,56},{56,64},{64,7... | collective-permute-start | bytes 245768 | tf_op jit(solution)/shard_map/ppermute | solution.py:425
  8.4 7.6 %copy-start.1 = (f32[128]{0:T(128)S(1)}, f32[128]{0:T(128)}, u32[]{:S(2)}) copy-start(f32[128]{0:T(128)} %param.18) | copy-start | bytes 1540
  8.4 11.4 %copy-start = (bf16[4,10240]{1,0:T(4,128)(2,1)}, bf16[4,10240]{1,0:T(4,128)(2,1)S(1)}, u32[]{:S(2)}) copy-start(bf16[4,10240]{1,0:T(4,128)(2,1)S(1)} %collective-permute-done.hx_ref.hb_ref.hc_ref) | copy-start | bytes 245764
  8.4 37.3 %all-to-all-start = ((bf16[16,128,512]{2,1,0:T(8,128)(2,1)}), bf16[16,128,512]{2,1,0:T(8,128)(2,1)}, u32[]{:S(2)}, u32[]{:S(2)}) async-start(bf16[16,128,512]{2,1,0:T(8,128)(2,1)} %pack.1), calls=%async_computation | async-start | bytes 4194304 | tf_op jit(solution)/shard_map/all_to_all | solution.py:427
  45.7 33.4 %all-to-all-start.1 = ((bf16[16,136,512]{2,1,0:T(8,128)(2,1)}), bf16[16,136,512]{2,1,0:T(8,128)(2,1)}, u32[]{:S(2)}, u32[]{:S(2)}) async-start(bf16[16,136,512]{2,1,0:T(8,128)(2,1)} %get-tuple-element.29), calls=%async_computation.1 | async-start | bytes 4456448 | tf_op jit(solution)/shard_map/all_to_all | solution.py:494

commit v9 on v8

--- a/solution.py
+++ b/solution.py
@@ -26,7 +26,7 @@
 LOG2E = 1.4426950408889634
 EXTRA = 8
 KEYS = 256
-PIECE = 32
+PIECE = 16
 CHUNK = 16
 RIM = 4
 

time: 132 us -> 132 us (level)
  Pallas kernels: 51 us -> 54 us
  waiting for transfers between devices: 19.4 us -> 16.5 us
    all_to_all x1, waiting for transfers between devices: 11.6 us -> 8.71 us  [on_device(): lax.all_to_all(fresh, 'ctx', split_axis=0, concat_axis=0, tiled=True)]
    pallas_call x1, Pallas kernels: 17.3 us -> 20.2 us  [on_device(): call(attend_kernel, in_specs=[smem(), smem(), pl.BlockSpec(memory_space=p...]
  transfers between devices with their start and end apart: 3 -> 3, of which waited for: 2 -> 2; matrix products, arithmetic and copies ran while one was open for 1% -> 1% of each run, Pallas kernels for 31% -> 33%
where the time goes in v9:
time: 132 us; the launch traced here: 131 us
  Pallas kernels  54 us (41%)
  blocking collectives  41.6 us (32%)
  waiting for transfers between devices  16.5 us (12%)
  starting transfers between devices  15.9 us (12%)
  local copies, waits for them, and re-layouts  1.77 us (1%)
    all_to_all x1, blocking collectives, on_device(): lax.all_to_all(own_states, 'ctx', split_axis=0, concat_axis=0, tiled=True)  41.6 us
    pallas_call x1, Pallas kernels, on_device(): call(attend_kernel, in_specs=[smem(), smem(), pl.BlockSpec(memory_space=p...  20.2 us
    pallas_call x1, Pallas kernels, on_device(): call(front_kernel, grid=(GROUPS,), in_specs=[smem(), smem(), wide(rows),...  9.94 us
    all_to_all x1, waiting for transfers between devices, on_device(): lax.all_to_all(fresh, 'ctx', split_axis=0, concat_axis=0, tiled=True)  8.71 us
    pallas_call x1, Pallas kernels, on_device(): call(inner_kernel, grid=(GROUPS,), in_specs=[smem(), smem(), wide(rows),...  8.19 us
    all_to_all x1, waiting for transfers between devices, on_device(): qkv = lax.all_to_all(qkv, 'ctx', split_axis=0, concat_axis=0, tiled=True)  7.82 us
    all_to_all x1, starting transfers between devices, on_device(): qkv = lax.all_to_all(qkv, 'ctx', split_axis=0, concat_axis=0, tiled=True)  7.53 us
    pallas_call x1, Pallas kernels, on_device(): call(final_kernel, in_specs=[pl.BlockSpec(memory_space=pl.ANY)] * 6, out_...  7.23 us
  transfers between devices with their start and end apart: 3, of which 2 were waited for; matrix products, arithmetic and copies ran while one was open for 1% of the time, Pallas kernels for 33%

profile of v9, /device:TPU:0, one launch (start us, length us, event | category | flops | bytes accessed | tf_op | source)
XLA Modules:
  0.0 131.1 jit_solution(4176826086087930827)
XLA Ops:
  0.6 1.0 slice_bitcast_fusion
  1.6 3.9 %collective-permute-start = (bf16[4,10240]{1,0:T(4,128)(2,1)S(1)}, bf16[4,10240]{1,0:T(4,128)(2,1)S(1)}, u32[]{:S(2)}, u32[]{:S(2)}) collective-permute-start(bf16[4,10240]{1,0:T(4,128)(2,1)S(1)} %slice_bitcast_fusion), channel_id=1, source_target_pairs={{0,8},{8,16},{16,24},{24,32},{32,40},{40,48},{48,56},{56,64},{64,7... | collective-permute-start | bytes 245768 | tf_op jit(solution)/shard_map/ppermute | solution.py:425
  5.5 2.9 %pack.1 = bf16[16,128,512]{2,1,0:T(8,128)(2,1)} custom-call(bf16[128,4096]{1,0:T(8,128)(2,1)} %bitcast.20, bf16[128,1024]{1,0:T(8,128)(2,1)} %bitcast.24, bf16[128,1024]{1,0:T(8,128)(2,1)} %bitcast.25), custom_call_target="tpu_custom_call" | custom-call | bytes 10500000 | tf_op jit(solution)/shard_map/pack/pallas_call | solution.py:413
  8.4 0.0 copy-start.1
  8.4 0.0 collective-permute-done.hx_ref.hb_ref.hc_ref
  8.4 0.0 copy-start
  8.4 7.5 %all-to-all-start = ((bf16[16,128,512]{2,1,0:T(8,128)(2,1)}), bf16[16,128,512]{2,1,0:T(8,128)(2,1)}, u32[]{:S(2)}, u32[]{:S(2)}) async-start(bf16[16,128,512]{2,1,0:T(8,128)(2,1)} %pack.1), calls=%async_computation | async-start | bytes 4194304 | tf_op jit(solution)/shard_map/all_to_all | solution.py:427
  16.0 0.0 copy-done.1
  16.0 0.1 broadcast_in_dim.20
  16.0 0.7 broadcast_in_dim_reshape.3.skip_ref
  16.8 0.6 pad_add_fusion.place_ref
  17.4 2.4 %prep.1 = (f32[8,128,16]{2,1,0:T(8,128)}, f32[128,128]{1,0:T(8,128)}, bf16[8,128,32]{2,1,0:T(8,128)(2,1)}, bf16[8,128,32]{2,1,0:T(8,128)(2,1)}, bf16[8,8,16]{2,1,0:T(8,128)(2,1)}) custom-call(s32[2]{0:T(128)} %pad_add_fusion.place_ref, s32[8,6]{1,0:T(8,128)} %lengths_ref.7, bf16[128,128]{1,0:T(8,128)(2,1)} %bitcast.27, f32[1,128]{1,0:T(1,128)} %bitcast.28), custom_call_target="tpu_custom_call" | custom-call | bytes 10500000 | tf_op jit(solution)/shard_map/prep/pallas_call | solution.py:429
  19.8 0.0 copy-done
  19.8 9.9 %front.1 = (bf16[128,8192]{1,0:T(8,128)(2,1)}, bf16[128,1024]{1,0:T(8,128)(2,1)}, bf16[128,1024]{1,0:T(8,128)(2,1)}, bf16[16,136,512]{2,1,0:T(8,128)(2,1)}) custom-call(s32[2]{0:T(128)} %pad_add_fusion.place_ref, s32[8,6]{1,0:T(8,128)} %lengths_ref.7, bf16[128,10240]{1,0:T(8,128)(2,1)} %bitcast.16, bf16[128,10240]{1,0:T(8,128)(2,1)} %bitcast.17, ...), custom_call_target="tpu_custom_call" | custom-call | bytes 140000000 | tf_op jit(solution)/shard_map/front/pallas_call | solution.py:451
  29.7 8.2 %inner.1.y_far = bf16[128,8192]{1,0:T(8,128)(2,1)} custom-call(s32[2]{0:T(128)} %pad_add_fusion.place_ref, s32[8,6]{1,0:T(8,128)} %lengths_ref.7, bf16[128,8192]{1,0:T(8,128)(2,1)} %get-tuple-element.23.xa_ref, bf16[128,1024]{1,0:T(8,128)(2,1)} %get-tuple-element.24.ba_ref, bf16[128,1024]{1,0:T(8,128)(2,1)} %get-tuple-element.25.ca_ref.ca_far, ...), custom_call_target="tpu_custom_call" | custom-call | bytes 31500000 | tf_op jit(solution)/shard_map/inner/pallas_call | solution.py:480
  37.9 7.8 %all-to-all-done = bf16[16,128,512]{2,1,0:T(8,128)(2,1)} async-done(((bf16[16,128,512]{2,1,0:T(8,128)(2,1)}), bf16[16,128,512]{2,1,0:T(8,128)(2,1)}, u32[]{:S(2)}, u32[]{:S(2)}) %all-to-all-start) | async-done | bytes 2097184 | tf_op jit(solution)/shard_map/all_to_all | solution.py:427
  45.7 4.5 %all-to-all-start.1 = ((bf16[16,136,512]{2,1,0:T(8,128)(2,1)}), bf16[16,136,512]{2,1,0:T(8,128)(2,1)}, u32[]{:S(2)}, u32[]{:S(2)}) async-start(bf16[16,136,512]{2,1,0:T(8,128)(2,1)} %get-tuple-element.29), calls=%async_computation.1 | async-start | bytes 4456448 | tf_op jit(solution)/shard_map/all_to_all | solution.py:494
  50.2 20.2 %attend.1.held_out_ref = bf16[16,128,768]{2,1,0:T(8,128)(2,1)} custom-call(s32[2]{0:T(128)} %pad_add_fusion.place_ref, s32[8,6]{1,0:T(8,128)} %lengths_ref.7, bf16[2048,512]{1,0:T(8,128)(2,1)} %bitcast.10.far_ref), custom_call_target="tpu_custom_call" | custom-call | bytes 105000000 | tf_op jit(solution)/shard_map/attend/pallas_call | solution.py:497
  70.4 8.7 %all-to-all-done.1.f_ref = bf16[16,136,512]{2,1,0:T(8,128)(2,1)} async-done(((bf16[16,136,512]{2,1,0:T(8,128)(2,1)}), bf16[16,136,512]{2,1,0:T(8,128)(2,1)}, u32[]{:S(2)}, u32[]{:S(2)}) %all-to-all-start.1) | async-done | bytes 2228256 | tf_op jit(solution)/shard_map/all_to_all | solution.py:494
  79.1 3.1 %scan.1 = bf16[16,128,768]{2,1,0:T(8,128)(2,1)} custom-call(bf16[16,136,512]{2,1,0:T(8,128)(2,1)} %all-to-all-done.1.f_ref, bf16[16,128,768]{2,1,0:T(8,128)(2,1)} %attend.1.held_out_ref), custom_call_target="tpu_custom_call", output_to_operand_aliasing={{}: (1, {})} | custom-call | bytes 14000000 | tf_op jit(solution)/shard_map/scan/pallas_call | solution.py:514
  82.3 41.6 %all_to_all.15.s_far = bf16[16,128,768]{2,1,0:T(8,128)(2,1)} all-to-all(bf16[16,128,768]{2,1,0:T(8,128)(2,1)} %scan.1), channel_id=1, replica_groups=mesh['ctx'=16,'batch'=8] {'ctx'}, dimensions={0} | all-to-all | bytes 6291456 | tf_op jit(solution)/shard_map/all_to_all | solution.py:531
  123.9 7.2 %final.1 = (bf16[128,8192]{1,0:T(8,128)(2,1)}, bf16[128,4096]{1,0:T(8,128)(2,1)}) custom-call(bf16[128,8192]{1,0:T(8,128)(2,1)} %inner.1.y_far, bf16[16,128,768]{2,1,0:T(8,128)(2,1)} %all_to_all.15.s_far, bf16[128,8192]{1,0:T(8,128)(2,1)} %bitcast.19, bf16[128,1024]{1,0:T(8,128)(2,1)} %get-tuple-element.25.ca_ref.ca_far, ...), custom_call_target="tpu_custom_call" | custom-call | bytes 24500000 | tf_op jit(solution)/shard_map/final/pallas_call | solution.py:533
Async XLA Ops:
  1.6 6.8 %collective-permute-start = (bf16[4,10240]{1,0:T(4,128)(2,1)S(1)}, bf16[4,10240]{1,0:T(4,128)(2,1)S(1)}, u32[]{:S(2)}, u32[]{:S(2)}) collective-permute-start(bf16[4,10240]{1,0:T(4,128)(2,1)S(1)} %slice_bitcast_fusion), channel_id=1, source_target_pairs={{0,8},{8,16},{16,24},{24,32},{32,40},{40,48},{48,56},{56,64},{64,7... | collective-permute-start | bytes 245768 | tf_op jit(solution)/shard_map/ppermute | solution.py:425
  8.4 7.6 %copy-start.1 = (f32[128]{0:T(128)S(1)}, f32[128]{0:T(128)}, u32[]{:S(2)}) copy-start(f32[128]{0:T(128)} %param.18) | copy-start | bytes 1540
  8.4 11.4 %copy-start = (bf16[4,10240]{1,0:T(4,128)(2,1)}, bf16[4,10240]{1,0:T(4,128)(2,1)S(1)}, u32[]{:S(2)}) copy-start(bf16[4,10240]{1,0:T(4,128)(2,1)S(1)} %collective-permute-done.hx_ref.hb_ref.hc_ref) | copy-start | bytes 245764
  8.4 37.3 %all-to-all-start = ((bf16[16,128,512]{2,1,0:T(8,128)(2,1)}), bf16[16,128,512]{2,1,0:T(8,128)(2,1)}, u32[]{:S(2)}, u32[]{:S(2)}) async-start(bf16[16,128,512]{2,1,0:T(8,128)(2,1)} %pack.1), calls=%async_computation | async-start | bytes 4194304 | tf_op jit(solution)/shard_map/all_to_all | solution.py:427
  45.7 33.4 %all-to-all-start.1 = ((bf16[16,136,512]{2,1,0:T(8,128)(2,1)}), bf16[16,136,512]{2,1,0:T(8,128)(2,1)}, u32[]{:S(2)}, u32[]{:S(2)}) async-start(bf16[16,136,512]{2,1,0:T(8,128)(2,1)} %get-tuple-element.29), calls=%async_computation.1 | async-start | bytes 4456448 | tf_op jit(solution)/shard_map/all_to_all | solution.py:494
